TPU v7x, 256 devices: a whole 4x4x8 slice. The times are simulated.
256 devices in a mesh: row: 32 (over z_hi, y, x), col: 8 (over z_lo, core).
Axes of the slice: x: 4, y: 4, z: 8 (z_hi: 2, z_lo: 4; z = z_hi * 4 + z_lo), core: 2. Of those that a mesh axis runs over, the one named last changes fastest.
Arguments:
- tile_values: float32 [32, 8, 64, 128, 128], P('row', 'col'), may hold values from -0.09375 to 0.09375
- tile_row: int32 [32, 8, 64], P('row', 'col'), may hold values from 0 to 31
- tile_col: int32 [32, 8, 64], P('row', 'col'), may hold values from 0 to 127
- counts: int32 [32, 8], P('row', 'col'), may hold values from 21 to 64, as said below
- diagonal: float32 [131072], P(('row', 'col')), may hold values from 1 to 3
- current: float32 [8, 131072], P(None, ('row', 'col')), may hold values from -6 to 6
- previous: float32 [8, 131072], P(None, ('row', 'col')), may hold values from -6 to 6
- previous_image: float32 [8, 131072], P(None, ('row', 'col')), may hold values from -6 to 6
Outputs:
- image: float32 [8, 131072], P(None, ('row', 'col'))
- residual: float32 [8, 131072], P(None, ('row', 'col'))
- residual_image: float32 [8, 131072], P(None, ('row', 'col'))
- reduced: float32 [24, 24], replicated
Inputs may be any that keep to these rules, and one draw needn't show every extreme that they name: `counts`: every device has between 21 and 64 live slots; in every draw one device has exactly 64 and one exactly 21.
All inputs are finite; a program needn't handle non-finite values.
Results may differ from a plain program's by a relative error of at most 0.0003.
Values sent between devices are 32-bit elements; how exact they have to be, the bound alone decides.
A program may use at most 64 MiB of HBM per device.

v0:
```python
import jax
import jax.numpy as jnp
from jax import lax
from jax.sharding import PartitionSpec as P

highest = lax.Precision.HIGHEST
group_width = 8


def apply_operator(vectors, diagonal, tile_values, tile_row, tile_col, counts):
    vector_count = vectors.shape[0]
    tile_size = tile_values.shape[-1]
    slot_count = tile_values.shape[2]
    blocks = tile_values.reshape(slot_count, tile_size, tile_size)
    rows_here = tile_row.reshape(slot_count)
    cols_here = tile_col.reshape(slot_count)
    live_count = counts.reshape(())
    row_vectors = lax.all_gather(vectors, "col", axis=1, tiled=True)
    column_vectors = lax.all_gather(vectors, "row", axis=1, tiled=True)
    row_tiles = row_vectors.reshape(vector_count, -1, tile_size)
    column_tiles = column_vectors.reshape(vector_count, -1, tile_size)
    slot_ids = jnp.arange(group_width, dtype=jnp.int32)

    def visit(group_index, carry):
        row_sum, column_sum = carry
        first_slot = group_index * group_width
        chosen = lax.dynamic_slice_in_dim(blocks, first_slot, group_width, 0)
        rows_now = lax.dynamic_slice_in_dim(rows_here, first_slot, group_width, 0)
        cols_now = lax.dynamic_slice_in_dim(cols_here, first_slot, group_width, 0)
        weight = (first_slot + slot_ids < live_count).astype(jnp.float32)[None, :, None]
        direct = (
            jnp.einsum("sij,ksj->ksi", chosen, column_tiles[:, cols_now, :], precision=highest)
            * weight
        )
        mirror = (
            jnp.einsum("sij,ksi->ksj", chosen, row_tiles[:, rows_now, :], precision=highest)
            * weight
        )
        return (row_sum.at[:, rows_now, :].add(direct), column_sum.at[:, cols_now, :].add(mirror))

    groups = (live_count + group_width - 1) // group_width
    row_sum, column_sum = lax.fori_loop(
        0, groups, visit, (jnp.zeros_like(row_tiles), jnp.zeros_like(column_tiles))
    )
    owned = lax.psum_scatter(
        row_sum.reshape(vector_count, -1), "col", scatter_dimension=1, tiled=True
    )
    owned = owned + lax.psum_scatter(
        column_sum.reshape(vector_count, -1), "row", scatter_dimension=1, tiled=True
    )
    return diagonal[None, :] * vectors + owned


def dot_rows(left, right):
    return jnp.dot(left, right.T, precision=highest)


def local(tile_values, tile_row, tile_col, counts, diagonal, current, previous, previous_image):
    image = apply_operator(current, diagonal, tile_values, tile_row, tile_col, counts)
    small_gram, small_proj = lax.psum(
        (dot_rows(current, current), dot_rows(current, image)), ("row", "col")
    )
    factor = jnp.linalg.cholesky(small_gram)
    ritz_matrix = jax.scipy.linalg.cho_solve((factor, True), small_proj)
    residual = image - jnp.dot(ritz_matrix.T, current, precision=highest)
    residual_image = apply_operator(residual, diagonal, tile_values, tile_row, tile_col, counts)
    search_basis = jnp.concatenate([current, residual, previous], 0)
    basis_image = jnp.concatenate([image, residual_image, previous_image], 0)
    correlation, mixed_terms = lax.psum(
        (dot_rows(search_basis, search_basis), dot_rows(search_basis, basis_image)), ("row", "col")
    )
    pencil = 0.5 * (mixed_terms + mixed_terms.T)
    lower_factor = jnp.linalg.cholesky(correlation)
    half_solve = jax.scipy.linalg.solve_triangular(lower_factor, pencil, lower=True)
    reduced = jax.scipy.linalg.solve_triangular(lower_factor, half_solve.T, lower=True)
    return (image, residual, residual_image, reduced)


def solution(mesh):
    return jax.shard_map(
        local,
        mesh=mesh,
        in_specs=(
            P("row", "col", None, None, None),
            P("row", "col", None),
            P("row", "col", None),
            P("row", "col"),
            P(("row", "col")),
            P(None, ("row", "col")),
            P(None, ("row", "col")),
            P(None, ("row", "col")),
        ),
        out_specs=(P(None, ("row", "col")), P(None, ("row", "col")), P(None, ("row", "col")), P()),
        check_vma=False,
    )
```

profile of v0, /device:TPU:24, one launch (start us, length us, event | category | flops | bytes accessed | tf_op | source)
XLA Modules:
  0.0 1057.6 jit_solution(8274827680721586273)
XLA Ops:
  7.9 99.9 %all_gather.12 = f32[8,16384]{1,0:T(8,128)S(1)} all-gather(f32[8,512]{1,0:T(8,128)} %param.19), channel_id=1, replica_groups=mesh['row'=32,'col'=8] {'row'}, dimensions={1}, use_global_device_ids=true | all-gather | bytes 540672 | tf_op jit(solution)/shard_map/all_gather | solution.py:19
  107.7 14.2 %all_gather.13 = f32[8,4096]{1,0:T(8,128)S(1)} all-gather(f32[8,512]{1,0:T(8,128)} %param.19), channel_id=1, replica_groups=mesh['row'=32,'col'=8] {'col'}, dimensions={1}, use_global_device_ids=true | all-gather | bytes 147456 | tf_op jit(solution)/shard_map/all_gather | solution.py:18
  122.0 30.9 %while.26 = (s32[]{:T(128)}, f32[8,32,128]{2,0,1:T(8,128)S(1)}, f32[8,128,128]{2,0,1:T(8,128)S(1)}, s32[]{:T(128)}, s32[64]{0:T(128)}, /*index=5*/s32[64]{0:T(12...) while((s32[]{:T(128)}, f32[8,32,128]{2,0,1:T(8,128)S(1)}, ...), condition=%wide.region_3.4_spmd.clone, body=%wide.region_0.3_spmd.clone.sunk | while | flops 25200716 | bytes 1516135 | solution.py:42
  124.0 1.6 convolution_multiply_fusion.9
  126.9 2.0 convolution_multiply_fusion.8
  131.7 1.6 convolution_multiply_fusion.9
  134.6 2.0 convolution_multiply_fusion.8
  136.6 0.8 scatter_fusion
  139.4 1.6 convolution_multiply_fusion.9
  142.4 2.0 convolution_multiply_fusion.8
  147.1 1.6 convolution_multiply_fusion.9
  150.1 2.0 convolution_multiply_fusion.8
  154.5 73.1 %reduce-scatter.5.cloned.1.call-done = f32[8,512]{1,0:T(8,128)} async-done(((f32[8,4096]{1,0:T(8,128)}), f32[8,512]{1,0:T(8,128)}) %reduce-scatter.5.cloned.1.call-update) | async-done | bytes 16400 | tf_op jit(solution)/shard_map/reduce_scatter | solution.py:45
  227.5 210.4 %reduce-scatter.7.cloned.1.call-done = f32[8,512]{1,0:T(8,128)} async-done(((f32[8,16384]{1,0:T(8,128)}), f32[8,512]{1,0:T(8,128)}) %reduce-scatter.7.cloned.1.call-update) | async-done | bytes 16400 | tf_op jit(solution)/shard_map/reduce_scatter | solution.py:48
  438.8 87.7 %all-reduce.1 = (f32[8,8]{0,1:T(8,128)S(1)}, f32[8,8]{0,1:T(8,128)S(1)}) all-reduce(f32[8,8]{0,1:T(8,128)S(1)} %convolution_bitcast_fusion.1, f32[8,8]{0,1:T(8,128)S(1)} %fusion.40), channel_id=1, replica_groups=mesh['row'=32,'col'=8] {'row','col'}, use_global_device_ids=true, to_apply=%region_9.10 | all-reduce | flops 128 | bytes 1024 | tf_op jit(solution)/shard_map/psum | solution.py:60
  529.8 95.1 %all_gather.14 = f32[8,16384]{1,0:T(8,128)S(1)} all-gather(f32[8,512]{1,0:T(8,128)S(1)} %convolution_subtract_fusion), channel_id=1, replica_groups=mesh['row'=32,'col'=8] {'row'}, dimensions={1}, use_global_device_ids=true | all-gather | bytes 540672 | tf_op jit(solution)/shard_map/all_gather | solution.py:19
  624.9 14.0 %all_gather.15 = f32[8,4096]{1,0:T(8,128)S(1)} all-gather(f32[8,512]{1,0:T(8,128)S(1)} %convolution_subtract_fusion), channel_id=1, replica_groups=mesh['row'=32,'col'=8] {'col'}, dimensions={1}, use_global_device_ids=true | all-gather | bytes 147456 | tf_op jit(solution)/shard_map/all_gather | solution.py:18
  638.9 30.9 %while.27 = (s32[]{:T(128)}, f32[8,32,128]{2,0,1:T(8,128)S(1)}, f32[8,128,128]{2,0,1:T(8,128)S(1)}, s32[]{:T(128)}, s32[64]{0:T(128)}, /*index=5*/s32[64]{0:T(12...) while((s32[]{:T(128)}, f32[8,32,128]{2,0,1:T(8,128)S(1)}, ...), condition=%wide.region_13.14_spmd.clone, body=%wide.region_10.13_spmd.clone.sunk | while | flops 25200716 | bytes 1516135 | solution.py:42
  641.0 1.6 convolution_multiply_fusion.11
  643.9 2.0 convolution_multiply_fusion.10
  648.7 1.6 convolution_multiply_fusion.11
  651.6 2.0 convolution_multiply_fusion.10
  656.4 1.6 convolution_multiply_fusion.11
  659.3 2.0 convolution_multiply_fusion.10
  664.1 1.6 convolution_multiply_fusion.11
  667.0 2.0 convolution_multiply_fusion.10
  671.3 74.0 %reduce-scatter.9.cloned.1.call-done = f32[8,512]{1,0:T(8,128)} async-done(((f32[8,4096]{1,0:T(8,128)}), f32[8,512]{1,0:T(8,128)}) %reduce-scatter.9.cloned.1.call-update) | async-done | bytes 16400 | tf_op jit(solution)/shard_map/reduce_scatter | solution.py:45
  745.2 210.3 %reduce-scatter.11.cloned.1.call-done = f32[8,512]{1,0:T(8,128)} async-done(((f32[8,16384]{1,0:T(8,128)}), f32[8,512]{1,0:T(8,128)}) %reduce-scatter.11.cloned.1.call-update) | async-done | bytes 16400 | tf_op jit(solution)/shard_map/reduce_scatter | solution.py:48
  956.5 88.1 %all-reduce = (f32[24,24]{0,1:T(8,128)S(1)}, f32[24,24]{0,1:T(8,128)S(1)}) all-reduce(f32[24,24]{0,1:T(8,128)S(1)} %fusion.16, f32[24,24]{0,1:T(8,128)S(1)} %fusion.22), channel_id=1, replica_groups=mesh['row'=32,'col'=8] {'row','col'}, use_global_device_ids=true, to_apply=%region_19.20 | all-reduce | flops 1152 | bytes 9216 | tf_op jit(solution)/shard_map/psum | solution.py:69
  1044.6 2.2 cholesky.64
  1048.1 1.8 custom-call.19
  1050.3 0.8 fusion.27
  (120 shorter events, 41.9 us)
Async XLA Ops:
  7.2 220.4 %reduce-scatter.5.cloned.1.call-start = ((), (), s32[]{:S(2)}) async-start(), calls=%async_computation.4 | async-start | bytes 147456 | tf_op jit(solution)/shard_map/reduce_scatter | solution.py:45
  122.0 32.4 %copy-start.4 = (f32[8,512]{1,0:T(8,128)S(1)}, f32[8,512]{1,0:T(8,128)}, u32[]{:S(2)}) copy-start(f32[8,512]{1,0:T(8,128)} %param.19) | copy-start | bytes 49156
  122.0 316.0 %copy-start.8 = (f32[512]{0:T(512)S(1)}, f32[512]{0:T(512)}, u32[]{:S(2)}) copy-start(f32[512]{0:T(512)} %param.18) | copy-start | bytes 6148
  152.9 0.7 copy-start.3
  152.9 0.8 copy-start.1
  153.5 284.4 %reduce-scatter.7.cloned.1.call-start = ((), (), s32[]{:S(2)}) async-start(), calls=%async_computation.5 | async-start | bytes 540672 | tf_op jit(solution)/shard_map/reduce_scatter | solution.py:48
  154.3 590.9 %reduce-scatter.9.cloned.1.call-start = ((), (), s32[]{:S(2)}) async-start(), calls=%async_computation.6 | async-start | bytes 147456 | tf_op jit(solution)/shard_map/reduce_scatter | solution.py:45
  438.7 517.5 %copy-start.6 = (f32[8,512]{1,0:T(8,128)}, f32[8,512]{1,0:T(8,128)S(1)}, u32[]{:S(2)}) copy-start(f32[8,512]{1,0:T(8,128)S(1)} %add_add_fusion.1) | copy-start | bytes 49156
  529.8 426.4 %copy-start.5 = (f32[8,512]{1,0:T(8,128)}, f32[8,512]{1,0:T(8,128)S(1)}, u32[]{:S(2)}) copy-start(f32[8,512]{1,0:T(8,128)S(1)} %convolution_subtract_fusion) | copy-start | bytes 49156
  638.9 32.1 %copy-start.10 = (f32[8,512]{1,0:T(8,128)S(1)}, f32[8,512]{1,0:T(8,128)}, u32[]{:S(2)}) copy-start(f32[8,512]{1,0:T(8,128)} %param.20) | copy-start | bytes 49156
  638.9 317.3 %copy-start.9 = (f32[8,512]{1,0:T(8,128)S(1)}, f32[8,512]{1,0:T(8,128)}, u32[]{:S(2)}) copy-start(f32[8,512]{1,0:T(8,128)} %param.21) | copy-start | bytes 49156
  669.8 0.7 copy-start.2
  669.8 0.8 copy-start
  670.5 285.0 %reduce-scatter.11.cloned.1.call-start = ((), (), s32[]{:S(2)}) async-start(), calls=%async_computation.7 | async-start | bytes 540672 | tf_op jit(solution)/shard_map/reduce_scatter | solution.py:48
  956.3 94.8 %copy-start.7 = (f32[8,512]{1,0:T(8,128)}, f32[8,512]{1,0:T(8,128)S(1)}, u32[]{:S(2)}) copy-start(f32[8,512]{1,0:T(8,128)S(1)} %add_add_fusion) | copy-start | bytes 49156
Sparse Core Ops, SparseCore 0:
  153.7 73.8 reduce-scatter.4
  230.2 207.7 reduce-scatter.6
  670.6 74.5 reduce-scatter.8
  747.7 207.7 reduce-scatter.10
where the time goes:
time: 1060 us
  waiting for transfers between devices  569 us (54%)
  blocking collectives  399 us (38%)
  other arithmetic  33.5 us (3%)
  matrix products  30.5 us (3%)
  between operations  14.6 us (1%)
  local copies, waits for them, and re-layouts  10.7 us (1%)
    reduce_scatter x2, waiting for transfers between devices, apply_operator(): lax.psum_scatter(column_sum.reshape(vector_count, -1), 'row', scatter_dim...  421 us
    all_gather x2, blocking collectives, apply_operator(): column_vectors = lax.all_gather(vectors, 'row', axis=1, tiled=True)  195 us
    reduce_scatter x2, waiting for transfers between devices, apply_operator(): lax.psum_scatter(row_sum.reshape(vector_count, -1), 'col', scatter_dimens...  147 us
    psum x1, blocking collectives, local(): lax.psum((dot_rows(search_basis, search_basis), dot_rows(search_basis, ba...  88.1 us
    psum x1, blocking collectives, local(): lax.psum((dot_rows(current, current), dot_rows(current, image)), ('row',...  87.7 us
    all_gather x2, blocking collectives, apply_operator(): row_vectors = lax.all_gather(vectors, 'col', axis=1, tiled=True)  28.1 us
  transfers between devices with their start and end apart: 4, of which 4 were waited for; matrix products, arithmetic and copies ran while one was open for 0% of the time, Pallas kernels for 0%

commit v1 on v0

v1 whole, which is shorter than its diff:
```python
import functools

import jax
import jax.numpy as jnp
from jax import lax
from jax.experimental import pallas as pl
from jax.experimental.pallas import tpu as pltpu
from jax.sharding import PartitionSpec as P

highest = lax.Precision.HIGHEST
group_width = 8
MESH = pl.DeviceIdType.MESH


def _barrier(n_row, n_col, r, c):
    barrier = pltpu.get_barrier_semaphore()

    def greet_col(k, carry):
        pl.semaphore_signal(barrier, 1, device_id=(r, lax.rem(c + k, n_col)), device_id_type=MESH)
        return carry

    def greet_row(k, carry):
        pl.semaphore_signal(barrier, 1, device_id=(lax.rem(r + k, n_row), c), device_id_type=MESH)
        return carry

    lax.fori_loop(1, n_col, greet_col, 0)
    lax.fori_loop(1, n_row, greet_row, 0)
    pl.semaphore_wait(barrier, n_row + n_col - 2)


def _gather_kernel(n_row, n_col, x_ref, rowv_ref, colv_ref, send_row, recv_row, send_col, recv_col, local_sem):
    vt = x_ref.shape[0]
    r = lax.axis_index("row")
    c = lax.axis_index("col")
    _barrier(n_row, n_col, r, c)

    def row_copy(j, src):
        return pltpu.make_async_remote_copy(
            src_ref=x_ref,
            dst_ref=rowv_ref.at[pl.ds(src * vt, vt)],
            send_sem=send_row.at[j],
            recv_sem=recv_row.at[src],
            device_id=(r, j),
            device_id_type=MESH,
        )

    def col_copy(i, src):
        return pltpu.make_async_remote_copy(
            src_ref=x_ref,
            dst_ref=colv_ref.at[pl.ds(src * vt, vt)],
            send_sem=send_col.at[i],
            recv_sem=recv_col.at[src],
            device_id=(i, c),
            device_id_type=MESH,
        )

    own_row = pltpu.make_async_copy(x_ref, rowv_ref.at[pl.ds(c * vt, vt)], local_sem.at[0])
    own_col = pltpu.make_async_copy(x_ref, colv_ref.at[pl.ds(r * vt, vt)], local_sem.at[1])
    own_row.start()
    own_col.start()

    def start_col(k, carry):
        row_copy(lax.rem(c + k, n_col), c).start()
        return carry

    def start_row(k, carry):
        col_copy(lax.rem(r + k, n_row), r).start()
        return carry

    lax.fori_loop(1, n_col, start_col, 0)
    lax.fori_loop(1, n_row, start_row, 0)

    def wait_col(k, carry):
        row_copy(lax.rem(c + k, n_col), c).wait_send()
        row_copy(c, lax.rem(c + n_col - k, n_col)).wait_recv()
        return carry

    def wait_row(k, carry):
        col_copy(lax.rem(r + k, n_row), r).wait_send()
        col_copy(r, lax.rem(r + n_row - k, n_row)).wait_recv()
        return carry

    lax.fori_loop(1, n_col, wait_col, 0)
    lax.fori_loop(1, n_row, wait_row, 0)
    own_row.wait()
    own_col.wait()


def gather_tiles(x_tiles, n_row, n_col):
    vt, k, t = x_tiles.shape
    vmem = pl.BlockSpec(memory_space=pltpu.VMEM)
    return pl.pallas_call(
        functools.partial(_gather_kernel, n_row, n_col),
        out_shape=(
            jax.ShapeDtypeStruct((n_col * vt, k, t), x_tiles.dtype),
            jax.ShapeDtypeStruct((n_row * vt, k, t), x_tiles.dtype),
        ),
        in_specs=[vmem],
        out_specs=(vmem, vmem),
        scratch_shapes=[
            pltpu.SemaphoreType.DMA((n_col,)),
            pltpu.SemaphoreType.DMA((n_col,)),
            pltpu.SemaphoreType.DMA((n_row,)),
            pltpu.SemaphoreType.DMA((n_row,)),
            pltpu.SemaphoreType.DMA((2,)),
        ],
        compiler_params=pltpu.CompilerParams(collective_id=0, has_side_effects=True),
    )(x_tiles)


def _reduce_kernel(n_row, n_col, base_ref, rsum_ref, csum_ref, out_ref, got_row, got_col,
                   send_row, recv_row, send_col, recv_col, local_sem):
    vt = base_ref.shape[0]
    r = lax.axis_index("row")
    c = lax.axis_index("col")
    _barrier(n_row, n_col, r, c)

    def row_copy(j, src):
        return pltpu.make_async_remote_copy(
            src_ref=rsum_ref.at[pl.ds(j * vt, vt)],
            dst_ref=got_row.at[src],
            send_sem=send_row.at[j],
            recv_sem=recv_row.at[src],
            device_id=(r, j),
            device_id_type=MESH,
        )

    def col_copy(i, src):
        return pltpu.make_async_remote_copy(
            src_ref=csum_ref.at[pl.ds(i * vt, vt)],
            dst_ref=got_col.at[src],
            send_sem=send_col.at[i],
            recv_sem=recv_col.at[src],
            device_id=(i, c),
            device_id_type=MESH,
        )

    own_row = pltpu.make_async_copy(rsum_ref.at[pl.ds(c * vt, vt)], got_row.at[c], local_sem.at[0])
    own_col = pltpu.make_async_copy(csum_ref.at[pl.ds(r * vt, vt)], got_col.at[r], local_sem.at[1])
    own_row.start()
    own_col.start()

    def start_col(k, carry):
        row_copy(lax.rem(c + k, n_col), c).start()
        return carry

    def start_row(k, carry):
        col_copy(lax.rem(r + k, n_row), r).start()
        return carry

    lax.fori_loop(1, n_col, start_col, 0)
    lax.fori_loop(1, n_row, start_row, 0)

    def wait_col(k, carry):
        row_copy(lax.rem(c + k, n_col), c).wait_send()
        row_copy(c, lax.rem(c + n_col - k, n_col)).wait_recv()
        return carry

    def wait_row(k, carry):
        col_copy(lax.rem(r + k, n_row), r).wait_send()
        col_copy(r, lax.rem(r + n_row - k, n_row)).wait_recv()
        return carry

    lax.fori_loop(1, n_col, wait_col, 0)
    lax.fori_loop(1, n_row, wait_row, 0)
    own_row.wait()
    own_col.wait()
    out_ref[...] = base_ref[...] + jnp.sum(got_row[...], axis=0) + jnp.sum(got_col[...], axis=0)


def reduce_tiles(base_tiles, row_sum, col_sum, n_row, n_col):
    vt, k, t = base_tiles.shape
    vmem = pl.BlockSpec(memory_space=pltpu.VMEM)
    return pl.pallas_call(
        functools.partial(_reduce_kernel, n_row, n_col),
        out_shape=jax.ShapeDtypeStruct((vt, k, t), base_tiles.dtype),
        in_specs=[vmem, vmem, vmem],
        out_specs=vmem,
        scratch_shapes=[
            pltpu.VMEM((n_col, vt, k, t), jnp.float32),
            pltpu.VMEM((n_row, vt, k, t), jnp.float32),
            pltpu.SemaphoreType.DMA((n_col,)),
            pltpu.SemaphoreType.DMA((n_col,)),
            pltpu.SemaphoreType.DMA((n_row,)),
            pltpu.SemaphoreType.DMA((n_row,)),
            pltpu.SemaphoreType.DMA((2,)),
        ],
        compiler_params=pltpu.CompilerParams(collective_id=1, has_side_effects=True),
    )(base_tiles, row_sum, col_sum)


def apply_operator(vectors, diagonal, tile_values, tile_row, tile_col, counts, n_row, n_col):
    vector_count = vectors.shape[0]
    tile_size = tile_values.shape[-1]
    slot_count = tile_values.shape[2]
    blocks = tile_values.reshape(slot_count, tile_size, tile_size)
    rows_here = tile_row.reshape(slot_count)
    cols_here = tile_col.reshape(slot_count)
    live_count = counts.reshape(())
    x_tiles = vectors.reshape(vector_count, -1, tile_size).transpose(1, 0, 2)
    row_tiles, column_tiles = gather_tiles(x_tiles, n_row, n_col)
    slot_ids = jnp.arange(group_width, dtype=jnp.int32)

    def visit(group_index, carry):
        row_sum, column_sum = carry
        first_slot = group_index * group_width
        chosen = lax.dynamic_slice_in_dim(blocks, first_slot, group_width, 0)
        rows_now = lax.dynamic_slice_in_dim(rows_here, first_slot, group_width, 0)
        cols_now = lax.dynamic_slice_in_dim(cols_here, first_slot, group_width, 0)
        weight = (first_slot + slot_ids < live_count).astype(jnp.float32)[:, None, None]
        direct = (
            jnp.einsum("sij,skj->ski", chosen, column_tiles[cols_now], precision=highest)
            * weight
        )
        mirror = (
            jnp.einsum("sij,ski->skj", chosen, row_tiles[rows_now], precision=highest)
            * weight
        )
        return (row_sum.at[rows_now].add(direct), column_sum.at[cols_now].add(mirror))

    groups = (live_count + group_width - 1) // group_width
    row_sum, column_sum = lax.fori_loop(
        0, groups, visit, (jnp.zeros_like(row_tiles), jnp.zeros_like(column_tiles))
    )
    base = (diagonal[None, :] * vectors).reshape(vector_count, -1, tile_size).transpose(1, 0, 2)
    owned = reduce_tiles(base, row_sum, column_sum, n_row, n_col)
    return owned.transpose(1, 0, 2).reshape(vector_count, -1)


def dot_rows(left, right):
    return jnp.dot(left, right.T, precision=highest)


def local(n_row, n_col, tile_values, tile_row, tile_col, counts, diagonal, current, previous, previous_image):
    op = functools.partial(apply_operator, n_row=n_row, n_col=n_col)
    image = op(current, diagonal, tile_values, tile_row, tile_col, counts)
    small_gram, small_proj = lax.psum(
        (dot_rows(current, current), dot_rows(current, image)), ("row", "col")
    )
    factor = jnp.linalg.cholesky(small_gram)
    ritz_matrix = jax.scipy.linalg.cho_solve((factor, True), small_proj)
    residual = image - jnp.dot(ritz_matrix.T, current, precision=highest)
    residual_image = op(residual, diagonal, tile_values, tile_row, tile_col, counts)
    search_basis = jnp.concatenate([current, residual, previous], 0)
    basis_image = jnp.concatenate([image, residual_image, previous_image], 0)
    correlation, mixed_terms = lax.psum(
        (dot_rows(search_basis, search_basis), dot_rows(search_basis, basis_image)), ("row", "col")
    )
    pencil = 0.5 * (mixed_terms + mixed_terms.T)
    lower_factor = jnp.linalg.cholesky(correlation)
    half_solve = jax.scipy.linalg.solve_triangular(lower_factor, pencil, lower=True)
    reduced = jax.scipy.linalg.solve_triangular(lower_factor, half_solve.T, lower=True)
    return (image, residual, residual_image, reduced)


def solution(mesh):
    n_row = mesh.shape["row"]
    n_col = mesh.shape["col"]
    return jax.shard_map(
        functools.partial(local, n_row, n_col),
        mesh=mesh,
        in_specs=(
            P("row", "col", None, None, None),
            P("row", "col", None),
            P("row", "col", None),
            P("row", "col"),
            P(("row", "col")),
            P(None, ("row", "col")),
            P(None, ("row", "col")),
            P(None, ("row", "col")),
        ),
        out_specs=(P(None, ("row", "col")), P(None, ("row", "col")), P(None, ("row", "col")), P()),
        check_vma=False,
    )
```

time: 1060 us -> 391 us (0.37)
  waiting for transfers between devices: 569 us -> 0 us
  blocking collectives: 399 us -> 160 us
  Pallas kernels: 0 us -> 162 us
  between operations: 14.6 us -> 1.52 us
    reduce_scatter x4 -> x0, waiting for transfers between devices: 568 us -> none  [the longest x2 421 us: apply_operator(): lax.psum_scatter(column_sum.reshape(vector_count, -1), 'row', scatter_dim...]
    all_gather x4 -> x0, blocking collectives: 223 us -> none  [the longest x2 195 us: apply_operator(): column_vectors = lax.all_gather(vectors, 'row', axis=1, tiled=True)]
    pallas_call x0 -> x4, Pallas kernels: none -> 162 us  [the longest x2 109 us: reduce_tiles(): pl.pallas_call(functools.partial(_reduce_kernel, n_row, n_col), out_shape...]
    psum x1, blocking collectives: 88.1 us -> 77.4 us  [local(): lax.psum((dot_rows(search_basis, search_basis), dot_rows(search_basis, ba...]
    dot_general x16 -> x12, matrix products: 28.3 us -> 21.2 us  [the longest x6 11.8 us: visit(): jnp.einsum('sij,skj->ski', chosen, column_tiles[cols_now], precision=high...]
  transfers between devices with their start and end apart: 4 -> 0, of which waited for: 4 -> 0; matrix products, arithmetic and copies ran while one was open for 0% -> 0% of each run, Pallas kernels for 0% -> 0%
where the time goes in v1:
time: 391 us; the launch traced here: 386 us
  Pallas kernels  162 us (41%)
  blocking collectives  160 us (41%)
  other arithmetic  27.2 us (7%)
  matrix products  26.2 us (7%)
  local copies, waits for them, and re-layouts  8.92 us (2%)
    pallas_call x2, Pallas kernels, reduce_tiles(): pl.pallas_call(functools.partial(_reduce_kernel, n_row, n_col), out_shape...  109 us
    psum x1, blocking collectives, local(): lax.psum((dot_rows(current, current), dot_rows(current, image)), ('row',...  82.2 us
    psum x1, blocking collectives, local(): lax.psum((dot_rows(search_basis, search_basis), dot_rows(search_basis, ba...  77.4 us
    pallas_call x2, Pallas kernels, gather_tiles(): pl.pallas_call(functools.partial(_gather_kernel, n_row, n_col), out_shape...  53.1 us
    dot_general x6, matrix products, visit(): jnp.einsum('sij,skj->ski', chosen, column_tiles[cols_now], precision=high...  11.8 us
    dot_general x6, matrix products, visit(): jnp.einsum('sij,ski->skj', chosen, row_tiles[rows_now], precision=highest)  9.45 us

profile of v1, /device:TPU:24, one launch (start us, length us, event | category | flops | bytes accessed | tf_op | source)
XLA Modules:
  0.0 386.2 jit_solution(6563396595548488280)
XLA Ops:
  1.3 26.7 %shard_map.111 = (f32[32,8,128]{2,1,0:T(8,128)S(1)}, f32[128,8,128]{2,1,0:T(8,128)S(1)}) custom-call(f32[4,8,128]{2,1,0:T(8,128)} %bitcast.82), custom_call_target="tpu_custom_call" | custom-call | tf_op jit(solution)/shard_map/pallas_call | solution.py:92
  28.1 23.1 %while.26 = (s32[]{:T(128)}, f32[32,8,128]{2,1,0:T(8,128)S(1)}, f32[128,8,128]{2,1,0:T(8,128)S(1)}, s32[]{:T(128)}, s32[64]{0:T(128)}, /*index=5*/s32[64]{0:T(12...) while((s32[]{:T(128)}, f32[32,8,128]{2,1,0:T(8,128)S(1)}, ...), condition=%wide.region_3.4_spmd.clone, body=%wide.region_0.3_spmd.clone.sunk | while | flops 25200716 | bytes 1516135 | solution.py:222
  30.1 1.6 convolution_multiply_fusion.9
  33.1 2.0 convolution_multiply_fusion.8
  35.0 0.8 scatter_fusion
  37.8 1.6 convolution_multiply_fusion.9
  40.8 2.0 convolution_multiply_fusion.8
  42.7 0.8 scatter_fusion
  45.5 1.6 convolution_multiply_fusion.9
  48.5 2.0 convolution_multiply_fusion.8
  50.4 0.8 scatter_fusion
  51.9 55.9 %shard_map.112 = f32[4,8,128]{2,1,0:T(8,128)} custom-call(f32[4,8,128]{2,1,0:T(8,128)} %multiply_bitcast_fusion.1.base_ref, f32[32,8,128]{2,1,0:T(8,128)S(1)} %get-tuple-element.129.rsum_ref, f32[128,8,128]{2,1,0:T(8,128)S(1)} %get-tuple-element.130.csum_ref), custom_call_target="tpu_custom_call" | custom-call | tf_op jit(solution)/shard_map/pallas_call | solution.py:174
  107.8 0.8 convolution_bitcast_fusion.1
  108.8 82.2 %all-reduce.1 = (f32[8,8]{0,1:T(8,128)S(1)}, f32[8,8]{0,1:T(8,128)S(1)}) all-reduce(f32[8,8]{0,1:T(8,128)S(1)} %convolution_bitcast_fusion.1, f32[8,8]{0,1:T(8,128)S(1)} %fusion.36), channel_id=1, replica_groups=mesh['row'=32,'col'=8] {'row','col'}, use_global_device_ids=true, to_apply=%region_7.8 | all-reduce | flops 128 | bytes 1024 | tf_op jit(solution)/shard_map/psum | solution.py:237
  194.1 1.5 convolution_subtract_fusion
  195.6 26.4 %shard_map.113 = (f32[32,8,128]{2,1,0:T(8,128)S(1)}, f32[128,8,128]{2,1,0:T(8,128)S(1)}) custom-call(f32[4,8,128]{2,1,0:T(8,128)} %bitcast.87), custom_call_target="tpu_custom_call" | custom-call | tf_op jit(solution)/shard_map/pallas_call | solution.py:92
  222.1 23.1 %while.27 = (s32[]{:T(128)}, f32[32,8,128]{2,1,0:T(8,128)S(1)}, f32[128,8,128]{2,1,0:T(8,128)S(1)}, s32[]{:T(128)}, s32[64]{0:T(128)}, /*index=5*/s32[64]{0:T(12...) while((s32[]{:T(128)}, f32[32,8,128]{2,1,0:T(8,128)S(1)}, ...), condition=%wide.region_11.12_spmd.clone, body=%wide.region_8.11_spmd.clone.sunk | while | flops 25200716 | bytes 1516135 | solution.py:222
  224.1 1.6 convolution_multiply_fusion.11
  227.1 2.0 convolution_multiply_fusion.10
  229.0 0.8 scatter_fusion.2
  231.8 1.6 convolution_multiply_fusion.11
  234.8 2.0 convolution_multiply_fusion.10
  236.7 0.8 scatter_fusion.2
  239.5 1.6 convolution_multiply_fusion.11
  242.5 2.0 convolution_multiply_fusion.10
  245.9 53.3 %shard_map.114 = f32[4,8,128]{2,1,0:T(8,128)} custom-call(f32[4,8,128]{2,1,0:T(8,128)} %multiply_bitcast_fusion.base_ref, f32[32,8,128]{2,1,0:T(8,128)S(1)} %get-tuple-element.133.rsum_ref, f32[128,8,128]{2,1,0:T(8,128)S(1)} %get-tuple-element.134.csum_ref), custom_call_target="tpu_custom_call" | custom-call | tf_op jit(solution)/shard_map/pallas_call | solution.py:174
  299.2 0.9 fusion.12
  300.3 77.4 %all-reduce = (f32[24,24]{0,1:T(8,128)S(1)}, f32[24,24]{0,1:T(8,128)S(1)}) all-reduce(f32[24,24]{0,1:T(8,128)S(1)} %fusion.12, f32[24,24]{0,1:T(8,128)S(1)} %fusion.18), channel_id=1, replica_groups=mesh['row'=32,'col'=8] {'row','col'}, use_global_device_ids=true, to_apply=%region_15.16 | all-reduce | flops 1152 | bytes 9216 | tf_op jit(solution)/shard_map/psum | solution.py:246
  377.8 2.2 cholesky.64
  381.3 1.8 custom-call.19
  383.4 0.8 fusion.23
  384.9 1.3 copy.48
  (80 shorter events, 27.7 us)
Async XLA Ops:
  28.0 23.2 %copy-start = (f32[8,512]{1,0:T(8,128)S(1)}, f32[8,512]{1,0:T(8,128)}, u32[]{:S(2)}) copy-start(f32[8,512]{1,0:T(8,128)} %param.19) | copy-start | bytes 49156
  28.0 23.2 %copy-start.3 = (f32[512]{0:T(512)S(1)}, f32[512]{0:T(512)}, u32[]{:S(2)}) copy-start(f32[512]{0:T(512)} %param.18) | copy-start | bytes 6148
  222.0 23.3 %copy-start.2 = (f32[8,512]{1,0:T(8,128)S(1)}, f32[8,512]{1,0:T(8,128)}, u32[]{:S(2)}) copy-start(f32[8,512]{1,0:T(8,128)} %convolution_subtract_fusion) | copy-start | bytes 49156
  222.1 77.1 %copy-start.1 = (f32[4,8,128]{2,1,0:T(8,128)S(1)}, f32[4,8,128]{2,1,0:T(8,128)}, u32[]{:S(2)}) copy-start(f32[4,8,128]{2,1,0:T(8,128)} %shard_map.112) | copy-start | bytes 49156
  222.1 77.1 %copy-start.4 = (f32[8,512]{1,0:T(8,128)S(1)}, f32[8,512]{1,0:T(8,128)}, u32[]{:S(2)}) copy-start(f32[8,512]{1,0:T(8,128)} %param.21) | copy-start | bytes 49156
  222.1 77.1 %copy-start.5 = (f32[8,512]{1,0:T(8,128)S(1)}, f32[8,512]{1,0:T(8,128)}, u32[]{:S(2)}) copy-start(f32[8,512]{1,0:T(8,128)} %param.20) | copy-start | bytes 49156

commit v2 on v1

--- a/solution.py
+++ b/solution.py
@@ -189,6 +189,98 @@
     )(base_tiles, row_sum, col_sum)
 
 
+def _psum_kernel(n_row, n_col, x_ref, out_ref, got_col, mid, got_row,
+                 send_col, recv_col, send_row, recv_row, local_sem):
+    r = lax.axis_index("row")
+    c = lax.axis_index("col")
+    _barrier(n_row, n_col, r, c)
+
+    def col_copy(j, src):
+        return pltpu.make_async_remote_copy(
+            src_ref=x_ref,
+            dst_ref=got_col.at[src],
+            send_sem=send_col.at[j],
+            recv_sem=recv_col.at[src],
+            device_id=(r, j),
+            device_id_type=MESH,
+        )
+
+    def row_copy(i, src):
+        return pltpu.make_async_remote_copy(
+            src_ref=mid,
+            dst_ref=got_row.at[src],
+            send_sem=send_row.at[i],
+            recv_sem=recv_row.at[src],
+            device_id=(i, c),
+            device_id_type=MESH,
+        )
+
+    own_col = pltpu.make_async_copy(x_ref, got_col.at[c], local_sem.at[0])
+    own_col.start()
+
+    def start_col(k, carry):
+        col_copy(lax.rem(c + k, n_col), c).start()
+        return carry
+
+    def wait_col(k, carry):
+        col_copy(lax.rem(c + k, n_col), c).wait_send()
+        col_copy(c, lax.rem(c + n_col - k, n_col)).wait_recv()
+        return carry
+
+    lax.fori_loop(1, n_col, start_col, 0)
+    lax.fori_loop(1, n_col, wait_col, 0)
+    own_col.wait()
+    mid[...] = jnp.sum(got_col[...], axis=0)
+
+    own_row = pltpu.make_async_copy(mid, got_row.at[r], local_sem.at[1])
+    own_row.start()
+
+    def start_row(k, carry):
+        row_copy(lax.rem(r + k, n_row), r).start()
+        return carry
+
+    def wait_row(k, carry):
+        row_copy(lax.rem(r + k, n_row), r).wait_send()
+        row_copy(r, lax.rem(r + n_row - k, n_row)).wait_recv()
+        return carry
+
+    lax.fori_loop(1, n_row, start_row, 0)
+    lax.fori_loop(1, n_row, wait_row, 0)
+    own_row.wait()
+    out_ref[...] = jnp.sum(got_row[...], axis=0)
+
+
+def psum_small(values, n_row, n_col, collective_id):
+    flat = jnp.concatenate([v.reshape(-1) for v in values])
+    tile = 8 * 128
+    padded = -(-flat.shape[0] // tile) * tile
+    packed = jnp.pad(flat, (0, padded - flat.shape[0])).reshape(-1, 128)
+    s, t = packed.shape
+    vmem = pl.BlockSpec(memory_space=pltpu.VMEM)
+    total = pl.pallas_call(
+        functools.partial(_psum_kernel, n_row, n_col),
+        out_shape=jax.ShapeDtypeStruct((s, t), jnp.float32),
+        in_specs=[vmem],
+        out_specs=vmem,
+        scratch_shapes=[
+            pltpu.VMEM((n_col, s, t), jnp.float32),
+            pltpu.VMEM((s, t), jnp.float32),
+            pltpu.VMEM((n_row, s, t), jnp.float32),
+            pltpu.SemaphoreType.DMA((n_col,)),
+            pltpu.SemaphoreType.DMA((n_col,)),
+            pltpu.SemaphoreType.DMA((n_row,)),
+            pltpu.SemaphoreType.DMA((n_row,)),
+            pltpu.SemaphoreType.DMA((2,)),
+        ],
+        compiler_params=pltpu.CompilerParams(collective_id=collective_id, has_side_effects=True),
+    )(packed).reshape(-1)
+    out, start = [], 0
+    for v in values:
+        out.append(total[start:start + v.size].reshape(v.shape))
+        start += v.size
+    return out
+
+
 def apply_operator(vectors, diagonal, tile_values, tile_row, tile_col, counts, n_row, n_col):
     vector_count = vectors.shape[0]
     tile_size = tile_values.shape[-1]
@@ -234,8 +326,8 @@
 def local(n_row, n_col, tile_values, tile_row, tile_col, counts, diagonal, current, previous, previous_image):
     op = functools.partial(apply_operator, n_row=n_row, n_col=n_col)
     image = op(current, diagonal, tile_values, tile_row, tile_col, counts)
-    small_gram, small_proj = lax.psum(
-        (dot_rows(current, current), dot_rows(current, image)), ("row", "col")
+    small_gram, small_proj = psum_small(
+        (dot_rows(current, current), dot_rows(current, image)), n_row, n_col, 2
     )
     factor = jnp.linalg.cholesky(small_gram)
     ritz_matrix = jax.scipy.linalg.cho_solve((factor, True), small_proj)
@@ -243,8 +335,8 @@
     residual_image = op(residual, diagonal, tile_values, tile_row, tile_col, counts)
     search_basis = jnp.concatenate([current, residual, previous], 0)
     basis_image = jnp.concatenate([image, residual_image, previous_image], 0)
-    correlation, mixed_terms = lax.psum(
-        (dot_rows(search_basis, search_basis), dot_rows(search_basis, basis_image)), ("row", "col")
+    correlation, mixed_terms = psum_small(
+        (dot_rows(search_basis, search_basis), dot_rows(search_basis, basis_image)), n_row, n_col, 3
     )
     pencil = 0.5 * (mixed_terms + mixed_terms.T)
     lower_factor = jnp.linalg.cholesky(correlation)

time: 391 us -> 288 us (0.74)
  blocking collectives: 160 us -> 0 us
  matrix products: 26.2 us -> 61.5 us
  other arithmetic: 27.2 us -> 58.4 us
  Pallas kernels: 162 us -> 140 us
  local copies, waits for them, and re-layouts: 8.92 us -> 22.2 us
    psum x2 -> x0, blocking collectives: 160 us -> none  [the longest x1 82.2 us: local(): lax.psum((dot_rows(current, current), dot_rows(current, image)), ('row',...]
    pallas_call x2, Pallas kernels: 109 us -> 45 us  [reduce_tiles(): pl.pallas_call(functools.partial(_reduce_kernel, n_row, n_col), out_shape...]
    pallas_call x0 -> x2, Pallas kernels: none -> 43.2 us  [psum_small(): pl.pallas_call(functools.partial(_psum_kernel, n_row, n_col), out_shape=j...]
    dot_general x6 -> x16, matrix products: 11.8 us -> 31.4 us  [visit(): jnp.einsum('sij,skj->ski', chosen, column_tiles[cols_now], precision=high...]
    dot_general x6 -> x16, matrix products: 9.45 us -> 25.2 us  [visit(): jnp.einsum('sij,ski->skj', chosen, row_tiles[rows_now], precision=highest)]
    scatter-add x6 -> x16, other arithmetic: 4.77 us -> 12.7 us  [visit(): row_sum.at[rows_now].add(direct)]
    scatter-add x6 -> x16, other arithmetic: 4.67 us -> 12.5 us  [visit(): column_sum.at[cols_now].add(mirror)]
    select_n x6 -> x16, other arithmetic: 4.51 us -> 12 us  [visit(): column_tiles[cols_now]]
where the time goes in v2:
time: 288 us; the launch traced here: 285 us
  Pallas kernels  140 us (49%)
  matrix products  61.5 us (21%)
  other arithmetic  58.4 us (20%)
  local copies, waits for them, and re-layouts  22.2 us (8%)
    pallas_call x2, Pallas kernels, gather_tiles(): pl.pallas_call(functools.partial(_gather_kernel, n_row, n_col), out_shape...  51.9 us
    pallas_call x2, Pallas kernels, reduce_tiles(): pl.pallas_call(functools.partial(_reduce_kernel, n_row, n_col), out_shape...  45 us
    pallas_call x2, Pallas kernels, psum_small(): pl.pallas_call(functools.partial(_psum_kernel, n_row, n_col), out_shape=j...  43.2 us
    dot_general x16, matrix products, visit(): jnp.einsum('sij,skj->ski', chosen, column_tiles[cols_now], precision=high...  31.4 us
    dot_general x16, matrix products, visit(): jnp.einsum('sij,ski->skj', chosen, row_tiles[rows_now], precision=highest)  25.2 us
    scatter-add x16, other arithmetic, visit(): row_sum.at[rows_now].add(direct)  12.7 us
    scatter-add x16, other arithmetic, visit(): column_sum.at[cols_now].add(mirror)  12.5 us
    select_n x16, other arithmetic, visit(): column_tiles[cols_now]  12 us

profile of v2, /device:TPU:24, one launch (start us, length us, event | category | flops | bytes accessed | tf_op | source)
XLA Modules:
  0.0 285.1 jit_solution(10935020316923724386)
XLA Ops:
  1.3 26.7 %shard_map.111 = (f32[32,8,128]{2,1,0:T(8,128)S(1)}, f32[128,8,128]{2,1,0:T(8,128)S(1)}) custom-call(f32[4,8,128]{2,1,0:T(8,128)} %bitcast.86), custom_call_target="tpu_custom_call" | custom-call | tf_op jit(solution)/shard_map/pallas_call | solution.py:92
  28.1 61.7 %while.26 = (s32[]{:T(128)}, f32[32,8,128]{2,1,0:T(8,128)S(1)}, f32[128,8,128]{2,1,0:T(8,128)S(1)}, s32[]{:T(128)}, s32[64]{0:T(128)}, /*index=5*/s32[64]{0:T(12...) while((s32[]{:T(128)}, f32[32,8,128]{2,1,0:T(8,128)S(1)}, ...), condition=%wide.region_3.4_spmd.clone, body=%wide.region_0.3_spmd.clone.sunk | while | flops 25200716 | bytes 1516135 | solution.py:314
  30.1 1.6 convolution_multiply_fusion.9
  33.1 2.0 convolution_multiply_fusion.8
  37.8 1.6 convolution_multiply_fusion.9
  40.8 2.0 convolution_multiply_fusion.8
  48.5 2.0 convolution_multiply_fusion.8
  56.2 2.0 convolution_multiply_fusion.8
  63.9 2.0 convolution_multiply_fusion.8
  68.7 1.6 convolution_multiply_fusion.9
  71.6 2.0 convolution_multiply_fusion.8
  79.3 2.0 convolution_multiply_fusion.8
  84.1 1.6 convolution_multiply_fusion.9
  87.0 2.0 convolution_multiply_fusion.8
  90.4 24.8 %shard_map.112 = f32[4,8,128]{2,1,0:T(8,128)} custom-call(f32[4,8,128]{2,1,0:T(8,128)} %multiply_bitcast_fusion.1.base_ref, f32[32,8,128]{2,1,0:T(8,128)S(1)} %get-tuple-element.129.rsum_ref, f32[128,8,128]{2,1,0:T(8,128)S(1)} %get-tuple-element.130.csum_ref), custom_call_target="tpu_custom_call" | custom-call | tf_op jit(solution)/shard_map/pallas_call | solution.py:174
  117.2 19.9 %shard_map.113 = f32[8,128]{1,0:T(8,128)} custom-call(f32[8,128]{1,0:T(8,128)} %fusion.31.x_ref), custom_call_target="tpu_custom_call" | custom-call | tf_op jit(solution)/shard_map/pallas_call | solution.py:260
  142.5 25.1 %shard_map.114 = (f32[32,8,128]{2,1,0:T(8,128)S(1)}, f32[128,8,128]{2,1,0:T(8,128)S(1)}) custom-call(f32[4,8,128]{2,1,0:T(8,128)} %bitcast.91), custom_call_target="tpu_custom_call" | custom-call | tf_op jit(solution)/shard_map/pallas_call | solution.py:92
  167.8 61.7 %while.27 = (s32[]{:T(128)}, f32[32,8,128]{2,1,0:T(8,128)S(1)}, f32[128,8,128]{2,1,0:T(8,128)S(1)}, s32[]{:T(128)}, s32[64]{0:T(128)}, /*index=5*/s32[64]{0:T(12...) while((s32[]{:T(128)}, f32[32,8,128]{2,1,0:T(8,128)S(1)}, ...), condition=%wide.region_9.10_spmd.clone, body=%wide.region_6.9_spmd.clone.sunk | while | flops 25200716 | bytes 1516135 | solution.py:314
  172.7 2.0 convolution_multiply_fusion.10
  180.4 2.0 convolution_multiply_fusion.10
  188.1 2.0 convolution_multiply_fusion.10
  192.9 1.6 convolution_multiply_fusion.11
  195.9 2.0 convolution_multiply_fusion.10
  203.6 2.0 convolution_multiply_fusion.10
  211.3 2.0 convolution_multiply_fusion.10
  216.0 1.6 convolution_multiply_fusion.11
  219.0 2.0 convolution_multiply_fusion.10
  226.7 2.0 convolution_multiply_fusion.10
  230.1 20.2 %shard_map.115 = f32[4,8,128]{2,1,0:T(8,128)} custom-call(f32[4,8,128]{2,1,0:T(8,128)} %multiply_bitcast_fusion.base_ref, f32[32,8,128]{2,1,0:T(8,128)S(1)} %get-tuple-element.133.rsum_ref, f32[128,8,128]{2,1,0:T(8,128)S(1)} %get-tuple-element.134.csum_ref), custom_call_target="tpu_custom_call" | custom-call | tf_op jit(solution)/shard_map/pallas_call | solution.py:174
  252.2 23.3 %shard_map.116 = f32[16,128]{1,0:T(8,128)} custom-call(f32[16,128]{1,0:T(8,128)} %fusion.26.x_ref), custom_call_target="tpu_custom_call" | custom-call | tf_op jit(solution)/shard_map/pallas_call | solution.py:260
  276.6 2.2 cholesky.64
  280.1 1.8 custom-call.19
  (192 shorter events, 97.4 us)
Async XLA Ops:
  28.0 61.8 %copy-start = (f32[8,512]{1,0:T(8,128)S(1)}, f32[8,512]{1,0:T(8,128)}, u32[]{:S(2)}) copy-start(f32[8,512]{1,0:T(8,128)} %param.19) | copy-start | bytes 49156
  28.0 61.8 %copy-start.3 = (f32[512]{0:T(512)S(1)}, f32[512]{0:T(512)}, u32[]{:S(2)}) copy-start(f32[512]{0:T(512)} %param.18) | copy-start | bytes 6148
  167.7 61.8 %copy-start.2 = (f32[8,512]{1,0:T(8,128)S(1)}, f32[8,512]{1,0:T(8,128)}, u32[]{:S(2)}) copy-start(f32[8,512]{1,0:T(8,128)} %convolution_subtract_fusion) | copy-start | bytes 49156
  167.7 82.5 %copy-start.1 = (f32[4,8,128]{2,1,0:T(8,128)S(1)}, f32[4,8,128]{2,1,0:T(8,128)}, u32[]{:S(2)}) copy-start(f32[4,8,128]{2,1,0:T(8,128)} %shard_map.112) | copy-start | bytes 49156
  167.7 82.5 %copy-start.4 = (f32[8,512]{1,0:T(8,128)S(1)}, f32[8,512]{1,0:T(8,128)}, u32[]{:S(2)}) copy-start(f32[8,512]{1,0:T(8,128)} %param.21) | copy-start | bytes 49156
  167.8 82.5 %copy-start.5 = (f32[8,512]{1,0:T(8,128)S(1)}, f32[8,512]{1,0:T(8,128)}, u32[]{:S(2)}) copy-start(f32[8,512]{1,0:T(8,128)} %param.20) | copy-start | bytes 49156

commit v3 on v2

--- a/solution.py
+++ b/solution.py
@@ -281,6 +281,69 @@
     return out
 
 
+def _slots_kernel(group, rows_ref, cols_ref, count_ref, tiles_ref, rowv_ref, colv_ref,
+                  rsum_ref, csum_ref):
+    g = pl.program_id(0)
+
+    @pl.when(g == 0)
+    def _():
+        rsum_ref[...] = jnp.zeros_like(rsum_ref)
+        csum_ref[...] = jnp.zeros_like(csum_ref)
+
+    for s in range(group):
+        slot = g * group + s
+
+        @pl.when(slot < count_ref[0])
+        def _():
+            a = rows_ref[slot]
+            b = cols_ref[slot]
+            block = tiles_ref[s]
+            direct = lax.dot_general(
+                colv_ref[b], block, (((1,), (1,)), ((), ())),
+                precision=highest, preferred_element_type=jnp.float32,
+            )
+            rsum_ref[a] += direct
+            mirror = jnp.dot(rowv_ref[a], block, precision=highest,
+                             preferred_element_type=jnp.float32)
+            csum_ref[b] += mirror
+
+
+def slot_products(blocks, rows_here, cols_here, live_count, row_tiles, column_tiles):
+    slot_count, tile, _ = blocks.shape
+    group = group_width
+    groups = slot_count // group
+
+    def tile_map(g, rows, cols, count):
+        last = jnp.maximum(count[0] - 1, 0) // group
+        return (jnp.minimum(g, last), 0, 0)
+
+    def whole(g, rows, cols, count):
+        return (0, 0, 0)
+
+    grid_spec = pltpu.PrefetchScalarGridSpec(
+        num_scalar_prefetch=3,
+        grid=(groups,),
+        in_specs=[
+            pl.BlockSpec((group, tile, tile), tile_map),
+            pl.BlockSpec(row_tiles.shape, whole),
+            pl.BlockSpec(column_tiles.shape, whole),
+        ],
+        out_specs=[
+            pl.BlockSpec(row_tiles.shape, whole),
+            pl.BlockSpec(column_tiles.shape, whole),
+        ],
+    )
+    return pl.pallas_call(
+        functools.partial(_slots_kernel, group),
+        grid_spec=grid_spec,
+        out_shape=(
+            jax.ShapeDtypeStruct(row_tiles.shape, jnp.float32),
+            jax.ShapeDtypeStruct(column_tiles.shape, jnp.float32),
+        ),
+        compiler_params=pltpu.CompilerParams(dimension_semantics=("arbitrary",)),
+    )(rows_here, cols_here, live_count.reshape(1), blocks, row_tiles, column_tiles)
+
+
 def apply_operator(vectors, diagonal, tile_values, tile_row, tile_col, counts, n_row, n_col):
     vector_count = vectors.shape[0]
     tile_size = tile_values.shape[-1]
@@ -291,29 +354,7 @@
     live_count = counts.reshape(())
     x_tiles = vectors.reshape(vector_count, -1, tile_size).transpose(1, 0, 2)
     row_tiles, column_tiles = gather_tiles(x_tiles, n_row, n_col)
-    slot_ids = jnp.arange(group_width, dtype=jnp.int32)
-
-    def visit(group_index, carry):
-        row_sum, column_sum = carry
-        first_slot = group_index * group_width
-        chosen = lax.dynamic_slice_in_dim(blocks, first_slot, group_width, 0)
-        rows_now = lax.dynamic_slice_in_dim(rows_here, first_slot, group_width, 0)
-        cols_now = lax.dynamic_slice_in_dim(cols_here, first_slot, group_width, 0)
-        weight = (first_slot + slot_ids < live_count).astype(jnp.float32)[:, None, None]
-        direct = (
-            jnp.einsum("sij,skj->ski", chosen, column_tiles[cols_now], precision=highest)
-            * weight
-        )
-        mirror = (
-            jnp.einsum("sij,ski->skj", chosen, row_tiles[rows_now], precision=highest)
-            * weight
-        )
-        return (row_sum.at[rows_now].add(direct), column_sum.at[cols_now].add(mirror))
-
-    groups = (live_count + group_width - 1) // group_width
-    row_sum, column_sum = lax.fori_loop(
-        0, groups, visit, (jnp.zeros_like(row_tiles), jnp.zeros_like(column_tiles))
-    )
+    row_sum, column_sum = slot_products(blocks, rows_here, cols_here, live_count, row_tiles, column_tiles)
     base = (diagonal[None, :] * vectors).reshape(vector_count, -1, tile_size).transpose(1, 0, 2)
     owned = reduce_tiles(base, row_sum, column_sum, n_row, n_col)
     return owned.transpose(1, 0, 2).reshape(vector_count, -1)

time: 288 us -> 201 us (0.70)
  matrix products: 61.5 us -> 5.02 us
  other arithmetic: 58.4 us -> 10.6 us
  Pallas kernels: 140 us -> 179 us
  local copies, waits for them, and re-layouts: 22.2 us -> 4.37 us
    dot_general x32 -> x0, matrix products: 56.6 us -> none  [the longest x16 31.4 us: visit(): jnp.einsum('sij,skj->ski', chosen, column_tiles[cols_now], precision=high...]
    scatter-add x32 -> x0, other arithmetic: 25.2 us -> none  [the longest x16 12.7 us: visit(): row_sum.at[rows_now].add(direct)]
    pallas_call x0 -> x2, Pallas kernels: none -> 23.8 us  [slot_products(): pl.pallas_call(functools.partial(_slots_kernel, group), grid_spec=grid_sp...]
    gather x32 -> x0, local copies, waits for them, and re-layouts: 17.8 us -> none  [the longest x16 8.88 us: visit(): row_tiles[rows_now]]
    select_n x16 -> x0, other arithmetic: 12 us -> none  [visit(): column_tiles[cols_now]]
    pallas_call x2, Pallas kernels: 45 us -> 55.6 us  [reduce_tiles(): pl.pallas_call(functools.partial(_reduce_kernel, n_row, n_col), out_shape...]
    convert_element_type x16 -> x0, other arithmetic: 10.4 us -> none  [visit(): (first_slot + slot_ids < live_count).astype(jnp.float32)[:, None, None]]
    pallas_call x2, Pallas kernels: 43.2 us -> 46.3 us  [psum_small(): pl.pallas_call(functools.partial(_psum_kernel, n_row, n_col), out_shape=j...]
where the time goes in v3:
time: 201 us; the launch traced here: 200 us
  Pallas kernels  179 us (89%)
  other arithmetic  10.6 us (5%)
  matrix products  5.02 us (2%)
  local copies, waits for them, and re-layouts  4.37 us (2%)
    pallas_call x2, Pallas kernels, reduce_tiles(): pl.pallas_call(functools.partial(_reduce_kernel, n_row, n_col), out_shape...  55.6 us
    pallas_call x2, Pallas kernels, gather_tiles(): pl.pallas_call(functools.partial(_gather_kernel, n_row, n_col), out_shape...  53 us
    pallas_call x2, Pallas kernels, psum_small(): pl.pallas_call(functools.partial(_psum_kernel, n_row, n_col), out_shape=j...  46.3 us
    pallas_call x2, Pallas kernels, slot_products(): pl.pallas_call(functools.partial(_slots_kernel, group), grid_spec=grid_sp...  23.8 us

profile of v3, /device:TPU:24, one launch (start us, length us, event | category | flops | bytes accessed | tf_op | source)
XLA Modules:
  0.0 200.1 jit_solution(9417446273620698783)
XLA Ops:
  0.7 27.6 %shard_map.111 = (f32[32,8,128]{2,1,0:T(8,128)}, f32[128,8,128]{2,1,0:T(8,128)}) custom-call(f32[4,8,128]{2,1,0:T(8,128)} %bitcast.76), custom_call_target="tpu_custom_call" | custom-call | tf_op jit(solution)/shard_map/pallas_call | solution.py:92
  28.9 11.9 %shard_map.112 = (f32[32,8,128]{2,1,0:T(8,128)}, f32[128,8,128]{2,1,0:T(8,128)}) custom-call(s32[64]{0:T(128)} %bitcast.85, s32[64]{0:T(128)} %bitcast.87, s32[1]{0:T(128)} %bitcast.72.count_ref, f32[64,128,128]{2,1,0:T(8,128)} %bitcast.74, f32[32,8,128]{2,1,0:T(8,128)} %get-tuple-element.13.rowv_ref, f32[128,8,128]{2,1,0:T(8,128)} %get-tuple-element.14.colv_ref), custom_call_target="tpu_custom_call" | custom-call | tf_op jit(solution)/shard_map/pallas_call | solution.py:336
  40.8 0.6 multiply_bitcast_fusion.1.base_ref
  41.4 30.1 %shard_map.113 = f32[4,8,128]{2,1,0:T(8,128)} custom-call(f32[4,8,128]{2,1,0:T(8,128)} %multiply_bitcast_fusion.1.base_ref, f32[32,8,128]{2,1,0:T(8,128)} %get-tuple-element.15.rsum_ref, f32[128,8,128]{2,1,0:T(8,128)} %get-tuple-element.16.csum_ref), custom_call_target="tpu_custom_call" | custom-call | tf_op jit(solution)/shard_map/pallas_call | solution.py:174
  71.5 0.9 convolution_bitcast_fusion.1
  72.6 0.1 fusion.28
  72.8 0.7 fusion.19.x_ref
  73.5 20.7 %shard_map.114 = f32[8,128]{1,0:T(8,128)} custom-call(f32[8,128]{1,0:T(8,128)} %fusion.19.x_ref), custom_call_target="tpu_custom_call" | custom-call | tf_op jit(solution)/shard_map/pallas_call | solution.py:260
  94.2 0.8 slice.44
  95.1 0.7 cholesky.30
  95.8 0.6 compare_reduce_fusion.1
  96.5 0.6 fusion.16
  97.1 0.6 custom-call.16
  97.7 0.2 fusion.17
  98.1 1.5 convolution_subtract_fusion
  99.6 25.4 %shard_map.115 = (f32[32,8,128]{2,1,0:T(8,128)}, f32[128,8,128]{2,1,0:T(8,128)}) custom-call(f32[4,8,128]{2,1,0:T(8,128)} %bitcast.81), custom_call_target="tpu_custom_call" | custom-call | tf_op jit(solution)/shard_map/pallas_call | solution.py:92
  125.0 11.9 %shard_map.116 = (f32[32,8,128]{2,1,0:T(8,128)}, f32[128,8,128]{2,1,0:T(8,128)}) custom-call(s32[64]{0:T(128)} %bitcast.86, s32[64]{0:T(128)} %bitcast.88, s32[1]{0:T(128)} %bitcast.73.count_ref, f32[64,128,128]{2,1,0:T(8,128)} %bitcast.75, f32[32,8,128]{2,1,0:T(8,128)} %get-tuple-element.17.rowv_ref, f32[128,8,128]{2,1,0:T(8,128)} %get-tuple-element.18.colv_ref), custom_call_target="tpu_custom_call" | custom-call | tf_op jit(solution)/shard_map/pallas_call | solution.py:336
  136.9 0.6 multiply_bitcast_fusion.base_ref
  137.5 25.5 %shard_map.117 = f32[4,8,128]{2,1,0:T(8,128)} custom-call(f32[4,8,128]{2,1,0:T(8,128)} %multiply_bitcast_fusion.base_ref, f32[32,8,128]{2,1,0:T(8,128)} %get-tuple-element.19.rsum_ref, f32[128,8,128]{2,1,0:T(8,128)} %get-tuple-element.20.csum_ref), custom_call_target="tpu_custom_call" | custom-call | tf_op jit(solution)/shard_map/pallas_call | solution.py:174
  163.1 0.9 fusion
  164.1 0.2 fusion.6
  164.3 0.7 fusion.14.x_ref
  165.0 25.6 %shard_map.118 = f32[16,128]{1,0:T(8,128)} custom-call(f32[16,128]{1,0:T(8,128)} %fusion.14.x_ref), custom_call_target="tpu_custom_call" | custom-call | tf_op jit(solution)/shard_map/pallas_call | solution.py:260
  190.6 0.8 fusion.27
  191.6 2.2 %cholesky.64 = f32[24,24]{1,0:T(8,128)S(1)} custom-call(f32[24,24]{1,0:T(8,128)S(1)} %fusion.13), custom_call_target="Cholesky" | custom-call | tf_op jit(solution)/shard_map/jit(cholesky)/cholesky | solution.py:383
  193.8 0.6 compare_reduce_fusion
  194.5 0.6 fusion.7
  195.1 1.8 custom-call.19
  197.1 0.2 convolution_bitcast_fusion
  197.3 0.8 fusion.11
  198.2 0.6 copy.27
  198.8 1.3 copy.28
  (28 shorter events, 1.1 us)
Async XLA Ops:
  0.6 40.2 %copy-start = (f32[8,512]{1,0:T(8,128)S(1)}, f32[8,512]{1,0:T(8,128)}, u32[]{:S(2)}) copy-start(f32[8,512]{1,0:T(8,128)} %param.15) | copy-start | bytes 49156
  0.6 40.2 %copy-start.3 = (f32[512]{0:T(512)S(1)}, f32[512]{0:T(512)}, u32[]{:S(2)}) copy-start(f32[512]{0:T(512)} %param.14) | copy-start | bytes 6148
  40.8 122.3 %copy-start.4 = (f32[8,512]{1,0:T(8,128)S(1)}, f32[8,512]{1,0:T(8,128)}, u32[]{:S(2)}) copy-start(f32[8,512]{1,0:T(8,128)} %param.17) | copy-start | bytes 49156
  40.8 122.3 %copy-start.5 = (f32[8,512]{1,0:T(8,128)S(1)}, f32[8,512]{1,0:T(8,128)}, u32[]{:S(2)}) copy-start(f32[8,512]{1,0:T(8,128)} %param.16) | copy-start | bytes 49156
  71.5 91.6 %copy-start.1 = (f32[4,8,128]{2,1,0:T(8,128)S(1)}, f32[4,8,128]{2,1,0:T(8,128)}, u32[]{:S(2)}) copy-start(f32[4,8,128]{2,1,0:T(8,128)} %shard_map.113) | copy-start | bytes 49156
  99.6 37.3 %copy-start.2 = (f32[8,512]{1,0:T(8,128)S(1)}, f32[8,512]{1,0:T(8,128)}, u32[]{:S(2)}) copy-start(f32[8,512]{1,0:T(8,128)} %convolution_subtract_fusion) | copy-start | bytes 49156

commit v4 on v1

--- a/solution.py
+++ b/solution.py
@@ -86,7 +86,7 @@
     own_col.wait()
 
 
-def gather_tiles(x_tiles, n_row, n_col):
+def gather_tiles(x_tiles, n_row, n_col, collective_id):
     vt, k, t = x_tiles.shape
     vmem = pl.BlockSpec(memory_space=pltpu.VMEM)
     return pl.pallas_call(
@@ -104,16 +104,38 @@
             pltpu.SemaphoreType.DMA((n_row,)),
             pltpu.SemaphoreType.DMA((2,)),
         ],
-        compiler_params=pltpu.CompilerParams(collective_id=0, has_side_effects=True),
+        compiler_params=pltpu.CompilerParams(collective_id=collective_id, has_side_effects=True),
     )(x_tiles)
 
 
-def _reduce_kernel(n_row, n_col, base_ref, rsum_ref, csum_ref, out_ref, got_row, got_col,
-                   send_row, recv_row, send_col, recv_col, local_sem):
+def _reduce_kernel(n_row, n_col, base_ref, rsum_ref, csum_ref, small_ref, out_ref, small_out,
+                   got_row, got_col, got_small_col, mid, got_small_row,
+                   send_row, recv_row, send_col, recv_col,
+                   send_small_col, recv_small_col, send_small_row, recv_small_row, local_sem):
     vt = base_ref.shape[0]
     r = lax.axis_index("row")
     c = lax.axis_index("col")
     _barrier(n_row, n_col, r, c)
+
+    def small_col_copy(j, src):
+        return pltpu.make_async_remote_copy(
+            src_ref=small_ref,
+            dst_ref=got_small_col.at[src],
+            send_sem=send_small_col.at[j],
+            recv_sem=recv_small_col.at[src],
+            device_id=(r, j),
+            device_id_type=MESH,
+        )
+
+    def small_row_copy(i, src):
+        return pltpu.make_async_remote_copy(
+            src_ref=mid,
+            dst_ref=got_small_row.at[src],
+            send_sem=send_small_row.at[i],
+            recv_sem=recv_small_row.at[src],
+            device_id=(i, c),
+            device_id_type=MESH,
+        )
 
     def row_copy(j, src):
         return pltpu.make_async_remote_copy(
@@ -135,6 +157,15 @@
             device_id_type=MESH,
         )
 
+    own_small = pltpu.make_async_copy(small_ref, got_small_col.at[c], local_sem.at[2])
+    own_small.start()
+
+    def start_small_col(k, carry):
+        small_col_copy(lax.rem(c + k, n_col), c).start()
+        return carry
+
+    lax.fori_loop(1, n_col, start_small_col, 0)
+
     own_row = pltpu.make_async_copy(rsum_ref.at[pl.ds(c * vt, vt)], got_row.at[c], local_sem.at[0])
     own_col = pltpu.make_async_copy(csum_ref.at[pl.ds(r * vt, vt)], got_col.at[r], local_sem.at[1])
     own_row.start()
@@ -148,8 +179,26 @@
         col_copy(lax.rem(r + k, n_row), r).start()
         return carry
 
+    lax.fori_loop(1, n_row, start_row, 0)
     lax.fori_loop(1, n_col, start_col, 0)
-    lax.fori_loop(1, n_row, start_row, 0)
+
+    def wait_small_col(k, carry):
+        small_col_copy(lax.rem(c + k, n_col), c).wait_send()
+        small_col_copy(c, lax.rem(c + n_col - k, n_col)).wait_recv()
+        return carry
+
+    lax.fori_loop(1, n_col, wait_small_col, 0)
+    own_small.wait()
+    mid[...] = jnp.sum(got_small_col[...], axis=0)
+
+    own_mid = pltpu.make_async_copy(mid, got_small_row.at[r], local_sem.at[3])
+    own_mid.start()
+
+    def start_small_row(k, carry):
+        small_row_copy(lax.rem(r + k, n_row), r).start()
+        return carry
+
+    lax.fori_loop(1, n_row, start_small_row, 0)
 
     def wait_col(k, carry):
         row_copy(lax.rem(c + k, n_col), c).wait_send()
@@ -167,85 +216,187 @@
     own_col.wait()
     out_ref[...] = base_ref[...] + jnp.sum(got_row[...], axis=0) + jnp.sum(got_col[...], axis=0)
 
-
-def reduce_tiles(base_tiles, row_sum, col_sum, n_row, n_col):
+    def wait_small_row(k, carry):
+        small_row_copy(lax.rem(r + k, n_row), r).wait_send()
+        small_row_copy(r, lax.rem(r + n_row - k, n_row)).wait_recv()
+        return carry
+
+    lax.fori_loop(1, n_row, wait_small_row, 0)
+    own_mid.wait()
+    small_out[...] = jnp.sum(got_small_row[...], axis=0)
+
+
+def pack_small(values):
+    flat = jnp.concatenate([v.reshape(-1) for v in values])
+    tile = 8 * 128
+    padded = -(-flat.shape[0] // tile) * tile
+    return jnp.pad(flat, (0, padded - flat.shape[0])).reshape(-1, 128)
+
+
+def unpack_small(total, values):
+    total = total.reshape(-1)
+    out, start = [], 0
+    for v in values:
+        out.append(total[start:start + v.size].reshape(v.shape))
+        start += v.size
+    return out
+
+
+def reduce_tiles(base_tiles, row_sum, col_sum, small, n_row, n_col, collective_id):
     vt, k, t = base_tiles.shape
+    s = small.shape[0]
     vmem = pl.BlockSpec(memory_space=pltpu.VMEM)
     return pl.pallas_call(
         functools.partial(_reduce_kernel, n_row, n_col),
-        out_shape=jax.ShapeDtypeStruct((vt, k, t), base_tiles.dtype),
-        in_specs=[vmem, vmem, vmem],
-        out_specs=vmem,
+        out_shape=(
+            jax.ShapeDtypeStruct((vt, k, t), base_tiles.dtype),
+            jax.ShapeDtypeStruct((s, 128), jnp.float32),
+        ),
+        in_specs=[vmem, vmem, vmem, vmem],
+        out_specs=(vmem, vmem),
         scratch_shapes=[
             pltpu.VMEM((n_col, vt, k, t), jnp.float32),
             pltpu.VMEM((n_row, vt, k, t), jnp.float32),
-            pltpu.SemaphoreType.DMA((n_col,)),
-            pltpu.SemaphoreType.DMA((n_col,)),
-            pltpu.SemaphoreType.DMA((n_row,)),
-            pltpu.SemaphoreType.DMA((n_row,)),
-            pltpu.SemaphoreType.DMA((2,)),
+            pltpu.VMEM((n_col, s, 128), jnp.float32),
+            pltpu.VMEM((s, 128), jnp.float32),
+            pltpu.VMEM((n_row, s, 128), jnp.float32),
+            pltpu.SemaphoreType.DMA((n_col,)),
+            pltpu.SemaphoreType.DMA((n_col,)),
+            pltpu.SemaphoreType.DMA((n_row,)),
+            pltpu.SemaphoreType.DMA((n_row,)),
+            pltpu.SemaphoreType.DMA((n_col,)),
+            pltpu.SemaphoreType.DMA((n_col,)),
+            pltpu.SemaphoreType.DMA((n_row,)),
+            pltpu.SemaphoreType.DMA((n_row,)),
+            pltpu.SemaphoreType.DMA((4,)),
         ],
-        compiler_params=pltpu.CompilerParams(collective_id=1, has_side_effects=True),
-    )(base_tiles, row_sum, col_sum)
-
-
-def apply_operator(vectors, diagonal, tile_values, tile_row, tile_col, counts, n_row, n_col):
-    vector_count = vectors.shape[0]
-    tile_size = tile_values.shape[-1]
+        compiler_params=pltpu.CompilerParams(collective_id=collective_id, has_side_effects=True),
+    )(base_tiles, row_sum, col_sum, small)
+
+
+def _slots_kernel(group, rows_k, rows_ref, cols_ref, count_ref, tiles_ref, rowv_ref, colv_ref,
+                  rsum_ref, csum_ref):
+    g = pl.program_id(0)
+
+    @pl.when(g == 0)
+    def _():
+        rsum_ref[...] = jnp.zeros_like(rsum_ref)
+        csum_ref[...] = jnp.zeros_like(csum_ref)
+
+    for s in range(group):
+        slot = g * group + s
+
+        @pl.when(slot < count_ref[0])
+        def _():
+            a = rows_ref[slot]
+            b = cols_ref[slot]
+            block = tiles_ref[s]
+            direct = lax.dot_general(
+                colv_ref[b, pl.ds(0, rows_k), :], block, (((1,), (1,)), ((), ())),
+                precision=highest, preferred_element_type=jnp.float32,
+            )
+            rsum_ref[a] += direct
+            mirror = jnp.dot(rowv_ref[a, pl.ds(0, rows_k), :], block, precision=highest,
+                             preferred_element_type=jnp.float32)
+            csum_ref[b] += mirror
+
+
+def slot_products(blocks, rows_here, cols_here, live_count, row_tiles, column_tiles, rows_k):
+    slot_count, tile, _ = blocks.shape
+    sums_shape = lambda v: (v.shape[0], rows_k, v.shape[2])
+    group = group_width
+    groups = slot_count // group
+
+    def tile_map(g, rows, cols, count):
+        last = jnp.maximum(count[0] - 1, 0) // group
+        return (jnp.minimum(g, last), 0, 0)
+
+    def whole(g, rows, cols, count):
+        return (0, 0, 0)
+
+    grid_spec = pltpu.PrefetchScalarGridSpec(
+        num_scalar_prefetch=3,
+        grid=(groups,),
+        in_specs=[
+            pl.BlockSpec((group, tile, tile), tile_map),
+            pl.BlockSpec(row_tiles.shape, whole),
+            pl.BlockSpec(column_tiles.shape, whole),
+        ],
+        out_specs=[
+            pl.BlockSpec(sums_shape(row_tiles), whole),
+            pl.BlockSpec(sums_shape(column_tiles), whole),
+        ],
+    )
+    return pl.pallas_call(
+        functools.partial(_slots_kernel, group, rows_k),
+        grid_spec=grid_spec,
+        out_shape=(
+            jax.ShapeDtypeStruct(sums_shape(row_tiles), jnp.float32),
+            jax.ShapeDtypeStruct(sums_shape(column_tiles), jnp.float32),
+        ),
+        compiler_params=pltpu.CompilerParams(dimension_semantics=("arbitrary",)),
+    )(rows_here, cols_here, live_count.reshape(1), blocks, row_tiles, column_tiles)
+
+
+def to_tiles(vectors, tile):
+    return vectors.reshape(vectors.shape[0], -1, tile).transpose(1, 0, 2)
+
+
+def from_tiles(tiles):
+    return tiles.transpose(1, 0, 2).reshape(tiles.shape[1], -1)
+
+
+def tile_dot(left, right):
+    return jnp.einsum("tki,tli->kl", left, right, precision=highest)
+
+
+def dot_rows(left, right):
+    return jnp.dot(left, right.T, precision=highest)
+
+
+def local(n_row, n_col, tile_values, tile_row, tile_col, counts, diagonal, current, previous, previous_image):
+    k = current.shape[0]
+    tile = tile_values.shape[-1]
     slot_count = tile_values.shape[2]
-    blocks = tile_values.reshape(slot_count, tile_size, tile_size)
+    blocks = tile_values.reshape(slot_count, tile, tile)
     rows_here = tile_row.reshape(slot_count)
     cols_here = tile_col.reshape(slot_count)
     live_count = counts.reshape(())
-    x_tiles = vectors.reshape(vector_count, -1, tile_size).transpose(1, 0, 2)
-    row_tiles, column_tiles = gather_tiles(x_tiles, n_row, n_col)
-    slot_ids = jnp.arange(group_width, dtype=jnp.int32)
-
-    def visit(group_index, carry):
-        row_sum, column_sum = carry
-        first_slot = group_index * group_width
-        chosen = lax.dynamic_slice_in_dim(blocks, first_slot, group_width, 0)
-        rows_now = lax.dynamic_slice_in_dim(rows_here, first_slot, group_width, 0)
-        cols_now = lax.dynamic_slice_in_dim(cols_here, first_slot, group_width, 0)
-        weight = (first_slot + slot_ids < live_count).astype(jnp.float32)[:, None, None]
-        direct = (
-            jnp.einsum("sij,skj->ski", chosen, column_tiles[cols_now], precision=highest)
-            * weight
-        )
-        mirror = (
-            jnp.einsum("sij,ski->skj", chosen, row_tiles[rows_now], precision=highest)
-            * weight
-        )
-        return (row_sum.at[rows_now].add(direct), column_sum.at[cols_now].add(mirror))
-
-    groups = (live_count + group_width - 1) // group_width
-    row_sum, column_sum = lax.fori_loop(
-        0, groups, visit, (jnp.zeros_like(row_tiles), jnp.zeros_like(column_tiles))
-    )
-    base = (diagonal[None, :] * vectors).reshape(vector_count, -1, tile_size).transpose(1, 0, 2)
-    owned = reduce_tiles(base, row_sum, column_sum, n_row, n_col)
-    return owned.transpose(1, 0, 2).reshape(vector_count, -1)
-
-
-def dot_rows(left, right):
-    return jnp.dot(left, right.T, precision=highest)
-
-
-def local(n_row, n_col, tile_values, tile_row, tile_col, counts, diagonal, current, previous, previous_image):
-    op = functools.partial(apply_operator, n_row=n_row, n_col=n_col)
-    image = op(current, diagonal, tile_values, tile_row, tile_col, counts)
-    small_gram, small_proj = lax.psum(
-        (dot_rows(current, current), dot_rows(current, image)), ("row", "col")
-    )
+
+    row_cp, col_cp = gather_tiles(to_tiles(jnp.concatenate([current, previous], 0), tile), n_row, n_col, 0)
+    row_sum, col_sum = slot_products(blocks, rows_here, cols_here, live_count, row_cp, col_cp, k)
+    row_cur, col_cur = row_cp[:, :k], col_cp[:, :k]
+    scaled = diagonal[None, :] * current
+    small_gram = dot_rows(current, current)
+    proj_part = dot_rows(current, scaled) + tile_dot(row_cur, row_sum) + tile_dot(col_cur, col_sum)
+    image_tiles, small = reduce_tiles(
+        to_tiles(scaled, tile), row_sum, col_sum, pack_small((small_gram, proj_part)), n_row, n_col, 1
+    )
+    image = from_tiles(image_tiles)
+    small_gram, small_proj = unpack_small(small, (small_gram, proj_part))
+
     factor = jnp.linalg.cholesky(small_gram)
     ritz_matrix = jax.scipy.linalg.cho_solve((factor, True), small_proj)
     residual = image - jnp.dot(ritz_matrix.T, current, precision=highest)
-    residual_image = op(residual, diagonal, tile_values, tile_row, tile_col, counts)
+
+    row_res, col_res = gather_tiles(to_tiles(residual, tile), n_row, n_col, 3)
+    row_sum, col_sum = slot_products(blocks, rows_here, cols_here, live_count, row_res, col_res, k)
     search_basis = jnp.concatenate([current, residual, previous], 0)
-    basis_image = jnp.concatenate([image, residual_image, previous_image], 0)
-    correlation, mixed_terms = lax.psum(
-        (dot_rows(search_basis, search_basis), dot_rows(search_basis, basis_image)), ("row", "col")
-    )
+    row_basis = jnp.concatenate([row_cur, row_res, row_cp[:, k:]], 1)
+    col_basis = jnp.concatenate([col_cur, col_res, col_cp[:, k:]], 1)
+    scaled = diagonal[None, :] * residual
+    correlation = dot_rows(search_basis, search_basis)
+    residual_part = (
+        dot_rows(search_basis, scaled) + tile_dot(row_basis, row_sum) + tile_dot(col_basis, col_sum)
+    )
+    mixed_part = jnp.concatenate(
+        [dot_rows(search_basis, image), residual_part, dot_rows(search_basis, previous_image)], 1
+    )
+    image_tiles, small = reduce_tiles(
+        to_tiles(scaled, tile), row_sum, col_sum, pack_small((correlation, mixed_part)), n_row, n_col, 2
+    )
+    residual_image = from_tiles(image_tiles)
+    correlation, mixed_terms = unpack_small(small, (correlation, mixed_part))
     pencil = 0.5 * (mixed_terms + mixed_terms.T)
     lower_factor = jnp.linalg.cholesky(correlation)
     half_solve = jax.scipy.linalg.solve_triangular(lower_factor, pencil, lower=True)

time: 391 us -> 197 us (0.50)
  blocking collectives: 160 us -> 0 us
  matrix products: 26.2 us -> 11.4 us
  other arithmetic: 27.2 us -> 12.7 us
    psum x2 -> x0, blocking collectives: 160 us -> none  [the longest x1 82.2 us: local(): lax.psum((dot_rows(current, current), dot_rows(current, image)), ('row',...]
    pallas_call x2, Pallas kernels: 109 us -> 71.9 us  [reduce_tiles(): pl.pallas_call(functools.partial(_reduce_kernel, n_row, n_col), out_shape...]
    pallas_call x0 -> x2, Pallas kernels: none -> 21.7 us  [slot_products(): pl.pallas_call(functools.partial(_slots_kernel, group, rows_k), grid_spec...]
    pallas_call x2, Pallas kernels: 53.1 us -> 71 us  [gather_tiles(): pl.pallas_call(functools.partial(_gather_kernel, n_row, n_col), out_shape...]
    dot_general x12 -> x4, matrix products: 21.2 us -> 6.7 us  [tile_dot(): return jnp.einsum('tki,tli->kl', left, right, precision=highest)]
    scatter-add x12 -> x0, other arithmetic: 9.45 us -> none  [the longest x6 4.77 us: visit(): row_sum.at[rows_now].add(direct)]
    gather x12 -> x0, local copies, waits for them, and re-layouts: 6.66 us -> none  [the longest x6 3.33 us: visit(): column_tiles[cols_now]]
    select_n x6 -> x0, other arithmetic: 4.51 us -> none  [visit(): column_tiles[cols_now]]
where the time goes in v4:
time: 197 us; the launch traced here: 196 us
  Pallas kernels  165 us (84%)
  other arithmetic  12.7 us (6%)
  matrix products  11.4 us (6%)
  local copies, waits for them, and re-layouts  5.53 us (3%)
    pallas_call x2, Pallas kernels, reduce_tiles(): pl.pallas_call(functools.partial(_reduce_kernel, n_row, n_col), out_shape...  71.9 us
    pallas_call x2, Pallas kernels, gather_tiles(): pl.pallas_call(functools.partial(_gather_kernel, n_row, n_col), out_shape...  71 us
    pallas_call x2, Pallas kernels, slot_products(): pl.pallas_call(functools.partial(_slots_kernel, group, rows_k), grid_spec...  21.7 us
    dot_general x4, matrix products, tile_dot(): return jnp.einsum('tki,tli->kl', left, right, precision=highest)  6.7 us

profile of v4, /device:TPU:24, one launch (start us, length us, event | category | flops | bytes accessed | tf_op | source)
XLA Modules:
  0.0 195.8 jit_solution(1765362707292476198)
XLA Ops:
  1.3 0.9 fusion.53
  2.3 1.3 multiply_bitcast_fusion.base_ref
  3.7 1.3 bitcast_bitcast_fusion.x_ref
  5.0 44.1 %shard_map.111 = (f32[32,16,128]{2,1,0:T(8,128)}, f32[128,16,128]{2,1,0:T(8,128)}) custom-call(f32[4,16,128]{2,1,0:T(8,128)} %bitcast_bitcast_fusion.x_ref), custom_call_target="tpu_custom_call" | custom-call | tf_op jit(solution)/shard_map/pallas_call | solution.py:92
  49.2 1.0 fusion.51
  50.2 11.0 %shard_map.112 = (f32[32,8,128]{2,1,0:T(8,128)}, f32[128,8,128]{2,1,0:T(8,128)}) custom-call(s32[64]{0:T(128)} %bitcast.103, s32[64]{0:T(128)} %bitcast.105, s32[1]{0:T(128)} %bitcast.93.count_ref, f32[64,128,128]{2,1,0:T(8,128)} %bitcast.95, f32[32,16,128]{2,1,0:T(8,128)} %get-tuple-element.17.rowv_ref, f32[128,16,128]{2,1,0:T(8,128)} %get-tuple-element.18.colv_ref), custom_call_target="tpu_custom_call" | custom-call | tf_op jit(solution)/shard_map/pallas_call | solution.py:330
  61.1 1.3 convolution_bitcast_fusion.2
  62.4 2.3 %convolution_bitcast_fusion.1 = f32[8,8]{0,1:T(8,128)S(1)} fusion(f32[128,8,128]{2,1,0:T(8,128)} %get-tuple-element.20.csum_ref, f32[128,16,128]{2,1,0:T(8,128)S(1)} %copy-done.1), kind=kOutput, calls=%fused_computation.10 | convolution fusion | flops 12582912 | bytes 1048832 | tf_op jit(solution)/shard_map/tki,tli->kl/dot_general | solution.py:350
  65.1 0.7 fusion.36.small_ref
  65.8 33.8 %shard_map.113 = (f32[4,8,128]{2,1,0:T(8,128)}, f32[8,128]{1,0:T(8,128)}) custom-call(f32[4,8,128]{2,1,0:T(8,128)} %multiply_bitcast_fusion.base_ref, f32[32,8,128]{2,1,0:T(8,128)} %get-tuple-element.19.rsum_ref, f32[128,8,128]{2,1,0:T(8,128)} %get-tuple-element.20.csum_ref, f32[8,128]{1,0:T(8,128)} %fusion.36.small_ref), custom_call_target="tpu_custom_call" | custom-call | tf_op jit(solution)/shard_map/pallas_call | solution.py:249
  99.6 0.7 slice.58
  100.5 0.7 cholesky.30
  101.2 0.6 compare_reduce_fusion.1
  101.9 0.6 fusion.33
  102.5 0.6 custom-call.16
  103.5 0.9 convolution_subtract_fusion
  104.4 0.9 fusion.31
  105.7 0.6 multiply_bitcast_fusion.1.base_ref
  106.4 26.9 %shard_map.114 = (f32[32,8,128]{2,1,0:T(8,128)}, f32[128,8,128]{2,1,0:T(8,128)}) custom-call(f32[4,8,128]{2,1,0:T(8,128)} %bitcast.97), custom_call_target="tpu_custom_call" | custom-call | tf_op jit(solution)/shard_map/pallas_call | solution.py:92
  133.3 10.8 %shard_map.115 = (f32[32,8,128]{2,1,0:T(8,128)}, f32[128,8,128]{2,1,0:T(8,128)}) custom-call(s32[64]{0:T(128)} %bitcast.104, s32[64]{0:T(128)} %bitcast.106, s32[1]{0:T(128)} %bitcast.94.count_ref, f32[64,128,128]{2,1,0:T(8,128)} %bitcast.96, f32[32,8,128]{2,1,0:T(8,128)} %get-tuple-element.23.rowv_ref, f32[128,8,128]{2,1,0:T(8,128)} %get-tuple-element.24.colv_ref), custom_call_target="tpu_custom_call" | custom-call | tf_op jit(solution)/shard_map/pallas_call | solution.py:330
  144.1 2.7 %fusion.9 = f32[24,8]{0,1:T(8,128)S(1)} fusion(f32[128,8,128]{2,1,0:T(8,128)} %get-tuple-element.26.csum_ref, f32[128,8,128]{2,1,0:T(8,128)S(1)} %get-tuple-element.30, f32[128,8,128]{2,1,0:T(8,128)S(1)} %copy-done.2, f32[128,8,128]{2,1,0:T(8,128)S(1)} %get-tuple-element.29), kind=kOutput, calls=%fused_computation.15 | convolution fusion | flops 38535168 | bytes 2097920 | tf_op jit(solution)/shard_map/tki,tli->kl/dot_general | solution.py:350
  146.7 0.5 convolution_bitcast_fusion.4
  147.6 0.7 fusion.26.small_ref
  148.3 38.1 %shard_map.116 = (f32[4,8,128]{2,1,0:T(8,128)}, f32[16,128]{1,0:T(8,128)}) custom-call(f32[4,8,128]{2,1,0:T(8,128)} %multiply_bitcast_fusion.1.base_ref, f32[32,8,128]{2,1,0:T(8,128)} %get-tuple-element.25.rsum_ref, f32[128,8,128]{2,1,0:T(8,128)} %get-tuple-element.26.csum_ref, f32[16,128]{1,0:T(8,128)} %fusion.26.small_ref), custom_call_target="tpu_custom_call" | custom-call | tf_op jit(solution)/shard_map/pallas_call | solution.py:249
  186.3 0.8 fusion.52
  187.5 2.2 %cholesky.64 = f32[24,24]{1,0:T(8,128)S(1)} custom-call(f32[24,24]{1,0:T(8,128)S(1)} %fusion.25), custom_call_target="Cholesky" | custom-call | tf_op jit(solution)/shard_map/jit(cholesky)/cholesky | solution.py:401
  189.7 0.6 compare_reduce_fusion
  190.4 0.6 fusion.19
  191.0 1.8 custom-call.19
  193.1 0.8 fusion.23
  193.9 0.6 copy.51
  194.5 1.3 copy.52
  (49 shorter events, 2.3 us)
Async XLA Ops:
  0.6 104.7 %copy-start = (f32[8,512]{1,0:T(8,128)S(1)}, f32[8,512]{1,0:T(8,128)}, u32[]{:S(2)}) copy-start(f32[8,512]{1,0:T(8,128)} %param.17) | copy-start | bytes 49156
  50.1 11.0 %copy-start.3 = (f32[32,16,128]{2,1,0:T(8,128)S(1)}, f32[32,16,128]{2,1,0:T(8,128)}, u32[]{:S(2)}) copy-start(f32[32,16,128]{2,1,0:T(8,128)} %get-tuple-element.17.rowv_ref) | copy-start | bytes 786436
  50.2 12.3 %copy-start.1 = (f32[128,16,128]{2,1,0:T(8,128)S(1)}, f32[128,16,128]{2,1,0:T(8,128)}, u32[]{:S(2)}) copy-start(f32[128,16,128]{2,1,0:T(8,128)} %get-tuple-element.18.colv_ref) | copy-start | bytes 3145732
  50.2 14.6 %copy-start.4 = (f32[8,512]{1,0:T(8,128)S(1)}, f32[8,512]{1,0:T(8,128)}, u32[]{:S(2)}) copy-start(f32[8,512]{1,0:T(8,128)} %param.15) | copy-start | bytes 49156
  50.2 14.5 %copy-start.11 = (f32[512]{0:T(512)S(1)}, f32[512]{0:T(512)}, u32[]{:S(2)}) copy-start(f32[512]{0:T(512)} %param.14) | copy-start | bytes 6148
  64.7 39.7 %copy-start.9 = (f32[8,512]{1,0:T(8,128)S(1)}, f32[8,512]{1,0:T(8,128)}, u32[]{:S(2)}) copy-start(f32[8,512]{1,0:T(8,128)} %param.16) | copy-start | bytes 49156
  104.4 2.0 copy-start.7
  133.3 10.8 %copy-start.2 = (f32[128,8,128]{2,1,0:T(8,128)S(1)}, f32[128,8,128]{2,1,0:T(8,128)}, u32[]{:S(2)}) copy-start(f32[128,8,128]{2,1,0:T(8,128)} %get-tuple-element.24.colv_ref) | copy-start | bytes 1572868
  144.1 2.7 %copy-start.5 = (f32[32,8,128]{2,1,0:T(8,128)S(1)}, f32[32,8,128]{2,1,0:T(8,128)}, u32[]{:S(2)}) copy-start(f32[32,8,128]{2,1,0:T(8,128)} %get-tuple-element.23.rowv_ref) | copy-start | bytes 393220
  144.1 2.7 %copy-start.6 = (f32[32,8,128]{2,1,0:T(8,128)S(1)}, f32[32,8,128]{2,1,0:T(8,128)}, u32[]{:S(2)}) copy-start(f32[32,8,128]{2,1,0:T(8,128)} %get-tuple-element.25.rsum_ref) | copy-start | bytes 393220
  144.1 3.2 %copy-start.8 = (f32[8,512]{1,0:T(8,128)S(1)}, f32[8,512]{1,0:T(8,128)}, u32[]{:S(2)}) copy-start(f32[8,512]{1,0:T(8,128)} %copy-done.7) | copy-start | bytes 49156
  144.1 49.8 %copy-start.10 = (f32[4,8,128]{2,1,0:T(8,128)S(1)}, f32[4,8,128]{2,1,0:T(8,128)}, u32[]{:S(2)}) copy-start(f32[4,8,128]{2,1,0:T(8,128)} %get-tuple-element.21) | copy-start | bytes 49156

commit v5 on v4

--- a/solution.py
+++ b/solution.py
@@ -290,15 +290,23 @@
         def _():
             a = rows_ref[slot]
             b = cols_ref[slot]
-            block = tiles_ref[s]
-            direct = lax.dot_general(
-                colv_ref[b, pl.ds(0, rows_k), :], block, (((1,), (1,)), ((), ())),
-                precision=highest, preferred_element_type=jnp.float32,
-            )
+            block = split_bf16(tiles_ref[s])
+            direct = dot3(split_bf16(colv_ref[b, pl.ds(0, rows_k), :]), block, (((1,), (1,)), ((), ())))
             rsum_ref[a] += direct
-            mirror = jnp.dot(rowv_ref[a, pl.ds(0, rows_k), :], block, precision=highest,
-                             preferred_element_type=jnp.float32)
+            mirror = dot3(split_bf16(rowv_ref[a, pl.ds(0, rows_k), :]), block, (((1,), (0,)), ((), ())))
             csum_ref[b] += mirror
+
+
+def split_bf16(x):
+    high = x.astype(jnp.bfloat16)
+    return high, (x - high.astype(jnp.float32)).astype(jnp.bfloat16)
+
+
+def dot3(left, right, dims):
+    def one(x, y):
+        return lax.dot_general(x, y, dims, preferred_element_type=jnp.float32)
+
+    return one(left[0], right[0]) + (one(left[0], right[1]) + one(left[1], right[0]))
 
 
 def slot_products(blocks, rows_here, cols_here, live_count, row_tiles, column_tiles, rows_k):

time: 197 us -> 191 us (0.970)
  Pallas kernels: 165 us -> 157 us
    pallas_call x2, Pallas kernels: 71.9 us -> 66.1 us  [reduce_tiles(): pl.pallas_call(functools.partial(_reduce_kernel, n_row, n_col), out_shape...]
    pallas_call x2, Pallas kernels: 71 us -> 67.9 us  [gather_tiles(): pl.pallas_call(functools.partial(_gather_kernel, n_row, n_col), out_shape...]
where the time goes in v5:
time: 191 us; the launch traced here: 188 us
  Pallas kernels  157 us (82%)
  other arithmetic  12.7 us (7%)
  matrix products  11.4 us (6%)
  local copies, waits for them, and re-layouts  5.53 us (3%)
    pallas_call x2, Pallas kernels, gather_tiles(): pl.pallas_call(functools.partial(_gather_kernel, n_row, n_col), out_shape...  67.9 us
    pallas_call x2, Pallas kernels, reduce_tiles(): pl.pallas_call(functools.partial(_reduce_kernel, n_row, n_col), out_shape...  66.1 us
    pallas_call x2, Pallas kernels, slot_products(): pl.pallas_call(functools.partial(_slots_kernel, group, rows_k), grid_spec...  23.2 us
    dot_general x4, matrix products, tile_dot(): return jnp.einsum('tki,tli->kl', left, right, precision=highest)  6.7 us

profile of v5, /device:TPU:24, one launch (start us, length us, event | category | flops | bytes accessed | tf_op | source)
XLA Modules:
  0.0 188.4 jit_solution(8836941607488454776)
XLA Ops:
  1.3 0.9 fusion.53
  2.3 1.3 multiply_bitcast_fusion.base_ref
  3.7 1.3 bitcast_bitcast_fusion.x_ref
  5.0 44.1 %shard_map.111 = (f32[32,16,128]{2,1,0:T(8,128)}, f32[128,16,128]{2,1,0:T(8,128)}) custom-call(f32[4,16,128]{2,1,0:T(8,128)} %bitcast_bitcast_fusion.x_ref), custom_call_target="tpu_custom_call" | custom-call | tf_op jit(solution)/shard_map/pallas_call | solution.py:92
  49.2 1.0 fusion.51
  50.2 11.7 %shard_map.112 = (f32[32,8,128]{2,1,0:T(8,128)}, f32[128,8,128]{2,1,0:T(8,128)}) custom-call(s32[64]{0:T(128)} %bitcast.103, s32[64]{0:T(128)} %bitcast.105, s32[1]{0:T(128)} %bitcast.93.count_ref, f32[64,128,128]{2,1,0:T(8,128)} %bitcast.95, f32[32,16,128]{2,1,0:T(8,128)} %get-tuple-element.17.rowv_ref, f32[128,16,128]{2,1,0:T(8,128)} %get-tuple-element.18.colv_ref), custom_call_target="tpu_custom_call" | custom-call | tf_op jit(solution)/shard_map/pallas_call | solution.py:338
  61.9 1.3 convolution_bitcast_fusion.2
  63.1 2.3 %convolution_bitcast_fusion.1 = f32[8,8]{0,1:T(8,128)S(1)} fusion(f32[128,8,128]{2,1,0:T(8,128)} %get-tuple-element.20.csum_ref, f32[128,16,128]{2,1,0:T(8,128)S(1)} %copy-done.1), kind=kOutput, calls=%fused_computation.10 | convolution fusion | flops 12582912 | bytes 1048832 | tf_op jit(solution)/shard_map/tki,tli->kl/dot_general | solution.py:358
  65.8 0.7 fusion.36.small_ref
  66.5 30.2 %shard_map.113 = (f32[4,8,128]{2,1,0:T(8,128)}, f32[8,128]{1,0:T(8,128)}) custom-call(f32[4,8,128]{2,1,0:T(8,128)} %multiply_bitcast_fusion.base_ref, f32[32,8,128]{2,1,0:T(8,128)} %get-tuple-element.19.rsum_ref, f32[128,8,128]{2,1,0:T(8,128)} %get-tuple-element.20.csum_ref, f32[8,128]{1,0:T(8,128)} %fusion.36.small_ref), custom_call_target="tpu_custom_call" | custom-call | tf_op jit(solution)/shard_map/pallas_call | solution.py:249
  96.7 0.7 slice.58
  97.5 0.7 cholesky.30
  98.3 0.6 compare_reduce_fusion.1
  98.9 0.6 fusion.33
  99.6 0.6 custom-call.16
  100.6 0.9 convolution_subtract_fusion
  101.5 0.9 fusion.31
  102.8 0.6 multiply_bitcast_fusion.1.base_ref
  103.4 23.8 %shard_map.114 = (f32[32,8,128]{2,1,0:T(8,128)}, f32[128,8,128]{2,1,0:T(8,128)}) custom-call(f32[4,8,128]{2,1,0:T(8,128)} %bitcast.97), custom_call_target="tpu_custom_call" | custom-call | tf_op jit(solution)/shard_map/pallas_call | solution.py:92
  127.2 11.5 %shard_map.115 = (f32[32,8,128]{2,1,0:T(8,128)}, f32[128,8,128]{2,1,0:T(8,128)}) custom-call(s32[64]{0:T(128)} %bitcast.104, s32[64]{0:T(128)} %bitcast.106, s32[1]{0:T(128)} %bitcast.94.count_ref, f32[64,128,128]{2,1,0:T(8,128)} %bitcast.96, f32[32,8,128]{2,1,0:T(8,128)} %get-tuple-element.23.rowv_ref, f32[128,8,128]{2,1,0:T(8,128)} %get-tuple-element.24.colv_ref), custom_call_target="tpu_custom_call" | custom-call | tf_op jit(solution)/shard_map/pallas_call | solution.py:338
  138.7 2.7 %fusion.9 = f32[24,8]{0,1:T(8,128)S(1)} fusion(f32[128,8,128]{2,1,0:T(8,128)} %get-tuple-element.26.csum_ref, f32[128,8,128]{2,1,0:T(8,128)S(1)} %get-tuple-element.30, f32[128,8,128]{2,1,0:T(8,128)S(1)} %copy-done.2, f32[128,8,128]{2,1,0:T(8,128)S(1)} %get-tuple-element.29), kind=kOutput, calls=%fused_computation.15 | convolution fusion | flops 38535168 | bytes 2097920 | tf_op jit(solution)/shard_map/tki,tli->kl/dot_general | solution.py:358
  141.4 0.5 convolution_bitcast_fusion.4
  142.2 0.7 fusion.26.small_ref
  142.9 35.9 %shard_map.116 = (f32[4,8,128]{2,1,0:T(8,128)}, f32[16,128]{1,0:T(8,128)}) custom-call(f32[4,8,128]{2,1,0:T(8,128)} %multiply_bitcast_fusion.1.base_ref, f32[32,8,128]{2,1,0:T(8,128)} %get-tuple-element.25.rsum_ref, f32[128,8,128]{2,1,0:T(8,128)} %get-tuple-element.26.csum_ref, f32[16,128]{1,0:T(8,128)} %fusion.26.small_ref), custom_call_target="tpu_custom_call" | custom-call | tf_op jit(solution)/shard_map/pallas_call | solution.py:249
  178.9 0.8 fusion.52
  180.0 2.2 %cholesky.64 = f32[24,24]{1,0:T(8,128)S(1)} custom-call(f32[24,24]{1,0:T(8,128)S(1)} %fusion.25), custom_call_target="Cholesky" | custom-call | tf_op jit(solution)/shard_map/jit(cholesky)/cholesky | solution.py:409
  182.3 0.6 compare_reduce_fusion
  182.9 0.6 fusion.19
  183.6 1.8 custom-call.19
  185.6 0.8 fusion.23
  186.5 0.6 copy.51
  187.1 1.3 copy.52
  (49 shorter events, 2.3 us)
Async XLA Ops:
  0.6 101.7 %copy-start = (f32[8,512]{1,0:T(8,128)S(1)}, f32[8,512]{1,0:T(8,128)}, u32[]{:S(2)}) copy-start(f32[8,512]{1,0:T(8,128)} %param.17) | copy-start | bytes 49156
  50.1 11.7 %copy-start.3 = (f32[32,16,128]{2,1,0:T(8,128)S(1)}, f32[32,16,128]{2,1,0:T(8,128)}, u32[]{:S(2)}) copy-start(f32[32,16,128]{2,1,0:T(8,128)} %get-tuple-element.17.rowv_ref) | copy-start | bytes 786436
  50.2 13.0 %copy-start.1 = (f32[128,16,128]{2,1,0:T(8,128)S(1)}, f32[128,16,128]{2,1,0:T(8,128)}, u32[]{:S(2)}) copy-start(f32[128,16,128]{2,1,0:T(8,128)} %get-tuple-element.18.colv_ref) | copy-start | bytes 3145732
  50.2 15.3 %copy-start.4 = (f32[8,512]{1,0:T(8,128)S(1)}, f32[8,512]{1,0:T(8,128)}, u32[]{:S(2)}) copy-start(f32[8,512]{1,0:T(8,128)} %param.15) | copy-start | bytes 49156
  50.2 15.3 %copy-start.11 = (f32[512]{0:T(512)S(1)}, f32[512]{0:T(512)}, u32[]{:S(2)}) copy-start(f32[512]{0:T(512)} %param.14) | copy-start | bytes 6148
  65.4 36.0 %copy-start.9 = (f32[8,512]{1,0:T(8,128)S(1)}, f32[8,512]{1,0:T(8,128)}, u32[]{:S(2)}) copy-start(f32[8,512]{1,0:T(8,128)} %param.16) | copy-start | bytes 49156
  101.5 2.0 %copy-start.7 = (f32[8,512]{1,0:T(8,128)}, f32[8,512]{1,0:T(8,128)S(1)}, u32[]{:S(2)}) copy-start(f32[8,512]{1,0:T(8,128)S(1)} %convolution_subtract_fusion) | copy-start | bytes 49156
  127.2 11.5 %copy-start.2 = (f32[128,8,128]{2,1,0:T(8,128)S(1)}, f32[128,8,128]{2,1,0:T(8,128)}, u32[]{:S(2)}) copy-start(f32[128,8,128]{2,1,0:T(8,128)} %get-tuple-element.24.colv_ref) | copy-start | bytes 1572868
  138.7 2.7 %copy-start.5 = (f32[32,8,128]{2,1,0:T(8,128)S(1)}, f32[32,8,128]{2,1,0:T(8,128)}, u32[]{:S(2)}) copy-start(f32[32,8,128]{2,1,0:T(8,128)} %get-tuple-element.23.rowv_ref) | copy-start | bytes 393220
  138.7 2.7 %copy-start.6 = (f32[32,8,128]{2,1,0:T(8,128)S(1)}, f32[32,8,128]{2,1,0:T(8,128)}, u32[]{:S(2)}) copy-start(f32[32,8,128]{2,1,0:T(8,128)} %get-tuple-element.25.rsum_ref) | copy-start | bytes 393220
  138.7 3.2 %copy-start.8 = (f32[8,512]{1,0:T(8,128)S(1)}, f32[8,512]{1,0:T(8,128)}, u32[]{:S(2)}) copy-start(f32[8,512]{1,0:T(8,128)} %copy-done.7) | copy-start | bytes 49156
  138.7 47.7 %copy-start.10 = (f32[4,8,128]{2,1,0:T(8,128)S(1)}, f32[4,8,128]{2,1,0:T(8,128)}, u32[]{:S(2)}) copy-start(f32[4,8,128]{2,1,0:T(8,128)} %get-tuple-element.21) | copy-start | bytes 49156

commit v6 on v5

--- a/solution.py
+++ b/solution.py
@@ -108,10 +108,13 @@
     )(x_tiles)
 
 
-def _reduce_kernel(n_row, n_col, base_ref, rsum_ref, csum_ref, small_ref, out_ref, small_out,
-                   got_row, got_col, got_small_col, mid, got_small_row,
-                   send_row, recv_row, send_col, recv_col,
-                   send_small_col, recv_small_col, send_small_row, recv_small_row, local_sem):
+def _reduce_kernel(n_row, n_col, forward, base_ref, rsum_ref, csum_ref, small_ref, out_ref, small_out, *rest):
+    if forward:
+        img_row, img_col = rest[:2]
+        rest = rest[2:]
+    (got_row, got_col, got_small_col, mid, got_small_row,
+     send_row, recv_row, send_col, recv_col,
+     send_small_col, recv_small_col, send_small_row, recv_small_row, local_sem) = rest[:14]
     vt = base_ref.shape[0]
     r = lax.axis_index("row")
     c = lax.axis_index("col")
@@ -216,6 +219,45 @@
     own_col.wait()
     out_ref[...] = base_ref[...] + jnp.sum(got_row[...], axis=0) + jnp.sum(got_col[...], axis=0)
 
+    if forward:
+        send_fr, recv_fr, send_fc, recv_fc = rest[14:]
+
+        def fwd_row_copy(j, src):
+            return pltpu.make_async_remote_copy(
+                src_ref=out_ref,
+                dst_ref=img_row.at[pl.ds(src * vt, vt)],
+                send_sem=send_fr.at[j],
+                recv_sem=recv_fr.at[src],
+                device_id=(r, j),
+                device_id_type=MESH,
+            )
+
+        def fwd_col_copy(i, src):
+            return pltpu.make_async_remote_copy(
+                src_ref=out_ref,
+                dst_ref=img_col.at[pl.ds(src * vt, vt)],
+                send_sem=send_fc.at[i],
+                recv_sem=recv_fc.at[src],
+                device_id=(i, c),
+                device_id_type=MESH,
+            )
+
+        own_fr = pltpu.make_async_copy(out_ref, img_row.at[pl.ds(c * vt, vt)], local_sem.at[4])
+        own_fc = pltpu.make_async_copy(out_ref, img_col.at[pl.ds(r * vt, vt)], local_sem.at[5])
+        own_fr.start()
+        own_fc.start()
+
+        def start_fr(k, carry):
+            fwd_row_copy(lax.rem(c + k, n_col), c).start()
+            return carry
+
+        def start_fc(k, carry):
+            fwd_col_copy(lax.rem(r + k, n_row), r).start()
+            return carry
+
+        lax.fori_loop(1, n_row, start_fc, 0)
+        lax.fori_loop(1, n_col, start_fr, 0)
+
     def wait_small_row(k, carry):
         small_row_copy(lax.rem(r + k, n_row), r).wait_send()
         small_row_copy(r, lax.rem(r + n_row - k, n_row)).wait_recv()
@@ -224,6 +266,22 @@
     lax.fori_loop(1, n_row, wait_small_row, 0)
     own_mid.wait()
     small_out[...] = jnp.sum(got_small_row[...], axis=0)
+
+    if forward:
+        def wait_fr(k, carry):
+            fwd_row_copy(lax.rem(c + k, n_col), c).wait_send()
+            fwd_row_copy(c, lax.rem(c + n_col - k, n_col)).wait_recv()
+            return carry
+
+        def wait_fc(k, carry):
+            fwd_col_copy(lax.rem(r + k, n_row), r).wait_send()
+            fwd_col_copy(r, lax.rem(r + n_row - k, n_row)).wait_recv()
+            return carry
+
+        lax.fori_loop(1, n_col, wait_fr, 0)
+        lax.fori_loop(1, n_row, wait_fc, 0)
+        own_fr.wait()
+        own_fc.wait()
 
 
 def pack_small(values):
@@ -242,18 +300,31 @@
     return out
 
 
-def reduce_tiles(base_tiles, row_sum, col_sum, small, n_row, n_col, collective_id):
+def reduce_tiles(base_tiles, row_sum, col_sum, small, n_row, n_col, collective_id, forward=False):
     vt, k, t = base_tiles.shape
     s = small.shape[0]
     vmem = pl.BlockSpec(memory_space=pltpu.VMEM)
+    out_shape = [
+        jax.ShapeDtypeStruct((vt, k, t), base_tiles.dtype),
+        jax.ShapeDtypeStruct((s, 128), jnp.float32),
+    ]
+    extra_sems = []
+    if forward:
+        out_shape += [
+            jax.ShapeDtypeStruct((n_col * vt, k, t), base_tiles.dtype),
+            jax.ShapeDtypeStruct((n_row * vt, k, t), base_tiles.dtype),
+        ]
+        extra_sems = [
+            pltpu.SemaphoreType.DMA((n_col,)),
+            pltpu.SemaphoreType.DMA((n_col,)),
+            pltpu.SemaphoreType.DMA((n_row,)),
+            pltpu.SemaphoreType.DMA((n_row,)),
+        ]
     return pl.pallas_call(
-        functools.partial(_reduce_kernel, n_row, n_col),
-        out_shape=(
-            jax.ShapeDtypeStruct((vt, k, t), base_tiles.dtype),
-            jax.ShapeDtypeStruct((s, 128), jnp.float32),
-        ),
+        functools.partial(_reduce_kernel, n_row, n_col, forward),
+        out_shape=tuple(out_shape),
         in_specs=[vmem, vmem, vmem, vmem],
-        out_specs=(vmem, vmem),
+        out_specs=tuple(vmem for _ in out_shape),
         scratch_shapes=[
             pltpu.VMEM((n_col, vt, k, t), jnp.float32),
             pltpu.VMEM((n_row, vt, k, t), jnp.float32),
@@ -268,8 +339,8 @@
             pltpu.SemaphoreType.DMA((n_col,)),
             pltpu.SemaphoreType.DMA((n_row,)),
             pltpu.SemaphoreType.DMA((n_row,)),
-            pltpu.SemaphoreType.DMA((4,)),
-        ],
+            pltpu.SemaphoreType.DMA((6,)),
+        ] + extra_sems,
         compiler_params=pltpu.CompilerParams(collective_id=collective_id, has_side_effects=True),
     )(base_tiles, row_sum, col_sum, small)
 
@@ -377,8 +448,9 @@
     scaled = diagonal[None, :] * current
     small_gram = dot_rows(current, current)
     proj_part = dot_rows(current, scaled) + tile_dot(row_cur, row_sum) + tile_dot(col_cur, col_sum)
-    image_tiles, small = reduce_tiles(
-        to_tiles(scaled, tile), row_sum, col_sum, pack_small((small_gram, proj_part)), n_row, n_col, 1
+    image_tiles, small, row_img, col_img = reduce_tiles(
+        to_tiles(scaled, tile), row_sum, col_sum, pack_small((small_gram, proj_part)), n_row, n_col, 1,
+        forward=True,
     )
     image = from_tiles(image_tiles)
     small_gram, small_proj = unpack_small(small, (small_gram, proj_part))
@@ -387,7 +459,11 @@
     ritz_matrix = jax.scipy.linalg.cho_solve((factor, True), small_proj)
     residual = image - jnp.dot(ritz_matrix.T, current, precision=highest)
 
-    row_res, col_res = gather_tiles(to_tiles(residual, tile), n_row, n_col, 3)
+    def residual_of(img_tiles, cur_tiles):
+        return img_tiles - jnp.einsum("lk,tli->tki", ritz_matrix, cur_tiles, precision=highest)
+
+    row_res = residual_of(row_img, row_cur)
+    col_res = residual_of(col_img, col_cur)
     row_sum, col_sum = slot_products(blocks, rows_here, cols_here, live_count, row_res, col_res, k)
     search_basis = jnp.concatenate([current, residual, previous], 0)
     row_basis = jnp.concatenate([row_cur, row_res, row_cp[:, k:]], 1)

time: 191 us -> 184 us (0.963)
  Pallas kernels: 157 us -> 146 us
  matrix products: 11.4 us -> 14.3 us
    pallas_call x2 -> x1, Pallas kernels: 67.9 us -> 44.2 us  [gather_tiles(): pl.pallas_call(functools.partial(_gather_kernel, n_row, n_col), out_shape...]
    pallas_call x2, Pallas kernels: 66.1 us -> 84.5 us  [reduce_tiles(): pl.pallas_call(functools.partial(_reduce_kernel, n_row, n_col, forward),...]
    pallas_call x2, Pallas kernels: 23.2 us -> 17.5 us  [slot_products(): pl.pallas_call(functools.partial(_slots_kernel, group, rows_k), grid_spec...]
    dot_general x0 -> x2, matrix products: none -> 4.35 us  [residual_of(): jnp.einsum('lk,tli->tki', ritz_matrix, cur_tiles, precision=highest)]
where the time goes in v6:
time: 184 us; the launch traced here: 180 us
  Pallas kernels  146 us (79%)
  matrix products  14.3 us (8%)
  other arithmetic  12.7 us (7%)
  local copies, waits for them, and re-layouts  5.51 us (3%)
    pallas_call x2, Pallas kernels, reduce_tiles(): pl.pallas_call(functools.partial(_reduce_kernel, n_row, n_col, forward),...  84.5 us
    pallas_call x1, Pallas kernels, gather_tiles(): pl.pallas_call(functools.partial(_gather_kernel, n_row, n_col), out_shape...  44.2 us
    pallas_call x2, Pallas kernels, slot_products(): pl.pallas_call(functools.partial(_slots_kernel, group, rows_k), grid_spec...  17.5 us
    dot_general x4, matrix products, tile_dot(): return jnp.einsum('tki,tli->kl', left, right, precision=highest)  6.7 us
    dot_general x2, matrix products, residual_of(): jnp.einsum('lk,tli->tki', ritz_matrix, cur_tiles, precision=highest)  4.35 us

profile of v6, /device:TPU:24, one launch (start us, length us, event | category | flops | bytes accessed | tf_op | source)
XLA Modules:
  0.0 180.2 jit_solution(13012219190881349129)
XLA Ops:
  1.3 0.9 fusion.59
  2.3 1.3 multiply_bitcast_fusion.base_ref
  3.7 1.3 bitcast_bitcast_fusion.x_ref
  5.0 44.2 %shard_map.111 = (f32[32,16,128]{2,1,0:T(8,128)}, f32[128,16,128]{2,1,0:T(8,128)}) custom-call(f32[4,16,128]{2,1,0:T(8,128)} %bitcast_bitcast_fusion.x_ref), custom_call_target="tpu_custom_call" | custom-call | tf_op jit(solution)/shard_map/pallas_call | solution.py:92
  49.2 1.0 fusion.57
  50.2 8.9 %shard_map.112 = (f32[32,8,128]{2,1,0:T(8,128)}, f32[128,8,128]{2,1,0:T(8,128)}) custom-call(s32[64]{0:T(128)} %bitcast.113, s32[64]{0:T(128)} %bitcast.115, s32[1]{0:T(128)} %bitcast.104.count_ref, f32[64,128,128]{2,1,0:T(8,128)} %bitcast.106, f32[32,16,128]{2,1,0:T(8,128)} %get-tuple-element.17.rowv_ref, f32[128,16,128]{2,1,0:T(8,128)} %get-tuple-element.18.colv_ref), custom_call_target="tpu_custom_call" | custom-call | tf_op jit(solution)/shard_map/pallas_call | solution.py:409
  59.1 1.3 convolution_bitcast_fusion.4
  60.3 2.3 %convolution_bitcast_fusion.3 = f32[8,8]{0,1:T(8,128)S(1)} fusion(f32[128,8,128]{2,1,0:T(8,128)} %get-tuple-element.20.csum_ref, f32[128,16,128]{2,1,0:T(8,128)S(1)} %copy-done.1), kind=kOutput, calls=%fused_computation.14 | convolution fusion | flops 12582912 | bytes 1048832 | tf_op jit(solution)/shard_map/tki,tli->kl/dot_general | solution.py:429
  63.0 0.7 fusion.38.small_ref
  63.6 45.0 %shard_map.113 = (f32[4,8,128]{2,1,0:T(8,128)}, f32[8,128]{1,0:T(8,128)}, f32[32,8,128]{2,1,0:T(8,128)}, f32[128,8,128]{2,1,0:T(8,128)}) custom-call(f32[4,8,128]{2,1,0:T(8,128)} %multiply_bitcast_fusion.base_ref, f32[32,8,128]{2,1,0:T(8,128)} %get-tuple-element.19.rsum_ref, f32[128,8,128]{2,1,0:T(8,128)} %get-tuple-element.20.csum_ref, ...), custom_call_target="tpu_custom_call" | custom-call | tf_op jit(solution)/shard_map/pallas_call | solution.py:323
  108.6 0.8 slice.58
  109.5 0.7 cholesky.30
  110.2 0.6 compare_reduce_fusion.1
  110.9 0.6 fusion.35
  111.5 0.6 custom-call.16
  112.5 1.9 %fusion.7.rowv_ref = f32[32,8,128]{2,1,0:T(8,128)} fusion(f32[32,8,128]{2,1,0:T(8,128)} %get-tuple-element.23, f32[8,8]{1,0:T(8,128)S(1)} %fusion.40, f32[32,16,128]{2,1,0:T(8,128)S(1)} %copy-done.3), kind=kOutput, calls=%fused_computation.9 | convolution fusion | flops 3178496 | bytes 397312 | tf_op jit(solution)/shard_map/lk,tli->tki/dot_general | solution.py:463
  114.4 2.5 %fusion.6.colv_ref = f32[128,8,128]{2,1,0:T(8,128)} fusion(f32[128,8,128]{2,1,0:T(8,128)} %get-tuple-element.24, f32[8,8]{1,0:T(8,128)S(1)} %fusion.40, f32[128,16,128]{2,1,0:T(8,128)S(1)} %copy-done.1), kind=kOutput, calls=%fused_computation.7 | convolution fusion | flops 12713984 | bytes 1576960 | tf_op jit(solution)/shard_map/lk,tli->tki/dot_general | solution.py:463
  117.7 0.6 multiply_bitcast_fusion.1.base_ref
  118.4 8.6 %shard_map.114 = (f32[32,8,128]{2,1,0:T(8,128)}, f32[128,8,128]{2,1,0:T(8,128)}) custom-call(s32[64]{0:T(128)} %bitcast.114, s32[64]{0:T(128)} %bitcast.116, s32[1]{0:T(128)} %bitcast.105.count_ref, f32[64,128,128]{2,1,0:T(8,128)} %bitcast.107, f32[32,8,128]{2,1,0:T(8,128)} %fusion.7.rowv_ref, f32[128,8,128]{2,1,0:T(8,128)} %fusion.6.colv_ref), custom_call_target="tpu_custom_call" | custom-call | tf_op jit(solution)/shard_map/pallas_call | solution.py:409
  127.0 2.7 %fusion.11 = f32[24,8]{0,1:T(8,128)S(1)} fusion(f32[128,8,128]{2,1,0:T(8,128)} %get-tuple-element.26.csum_ref, f32[128,8,128]{2,1,0:T(8,128)S(1)} %get-tuple-element.30, f32[128,8,128]{2,1,0:T(8,128)S(1)} %copy-done.2, f32[128,8,128]{2,1,0:T(8,128)S(1)} %get-tuple-element.29), kind=kOutput, calls=%fused_computation.19 | convolution fusion | flops 38535168 | bytes 2097920 | tf_op jit(solution)/shard_map/tki,tli->kl/dot_general | solution.py:429
  129.7 0.5 convolution_bitcast_fusion.6
  130.5 0.7 fusion.28.small_ref
  131.2 39.5 %shard_map.115 = (f32[4,8,128]{2,1,0:T(8,128)}, f32[16,128]{1,0:T(8,128)}) custom-call(f32[4,8,128]{2,1,0:T(8,128)} %multiply_bitcast_fusion.1.base_ref, f32[32,8,128]{2,1,0:T(8,128)} %get-tuple-element.25.rsum_ref, f32[128,8,128]{2,1,0:T(8,128)} %get-tuple-element.26.csum_ref, f32[16,128]{1,0:T(8,128)} %fusion.28.small_ref), custom_call_target="tpu_custom_call" | custom-call | tf_op jit(solution)/shard_map/pallas_call | solution.py:323
  170.7 0.8 fusion.58
  171.8 2.2 %cholesky.64 = f32[24,24]{1,0:T(8,128)S(1)} custom-call(f32[24,24]{1,0:T(8,128)S(1)} %fusion.27), custom_call_target="Cholesky" | custom-call | tf_op jit(solution)/shard_map/jit(cholesky)/cholesky | solution.py:485
  174.1 0.6 compare_reduce_fusion
  174.7 0.6 fusion.21
  175.4 1.8 %custom-call.19 = f32[1,24,24]{1,2,0:T(8,128)S(1)} custom-call(f32[1,24,24]{2,1,0:T(8,128)S(1)} %fusion.21), custom_call_target="InvertDiagBlocksLowerTriangular" | custom-call | tf_op jit(solution)/shard_map/jit(_solve_triangular)/triangular_solve | solution.py:487
  177.2 0.2 convolution_bitcast_fusion.2
  177.4 0.8 fusion.25
  178.3 0.6 copy.59
  178.9 1.3 copy.60
  (48 shorter events, 2.4 us)
Async XLA Ops:
  0.6 116.7 %copy-start = (f32[8,512]{1,0:T(8,128)S(1)}, f32[8,512]{1,0:T(8,128)}, u32[]{:S(2)}) copy-start(f32[8,512]{1,0:T(8,128)} %param.17) | copy-start | bytes 49156
  50.2 8.9 %copy-start.3 = (f32[32,16,128]{2,1,0:T(8,128)S(1)}, f32[32,16,128]{2,1,0:T(8,128)}, u32[]{:S(2)}) copy-start(f32[32,16,128]{2,1,0:T(8,128)} %get-tuple-element.17.rowv_ref) | copy-start | bytes 786436
  50.2 10.2 %copy-start.1 = (f32[128,16,128]{2,1,0:T(8,128)S(1)}, f32[128,16,128]{2,1,0:T(8,128)}, u32[]{:S(2)}) copy-start(f32[128,16,128]{2,1,0:T(8,128)} %get-tuple-element.18.colv_ref) | copy-start | bytes 3145732
  50.2 12.5 %copy-start.4 = (f32[8,512]{1,0:T(8,128)S(1)}, f32[8,512]{1,0:T(8,128)}, u32[]{:S(2)}) copy-start(f32[8,512]{1,0:T(8,128)} %param.15) | copy-start | bytes 49156
  50.2 12.5 %copy-start.10 = (f32[512]{0:T(512)S(1)}, f32[512]{0:T(512)}, u32[]{:S(2)}) copy-start(f32[512]{0:T(512)} %param.14) | copy-start | bytes 6148
  114.4 2.5 %copy-start.9 = (f32[4,8,128]{2,1,0:T(8,128)S(1)}, f32[4,8,128]{2,1,0:T(8,128)}, u32[]{:S(2)}) copy-start(f32[4,8,128]{2,1,0:T(8,128)} %get-tuple-element.21) | copy-start | bytes 49156
  114.4 2.7 %copy-start.8 = (f32[8,512]{1,0:T(8,128)S(1)}, f32[8,512]{1,0:T(8,128)}, u32[]{:S(2)}) copy-start(f32[8,512]{1,0:T(8,128)} %param.16) | copy-start | bytes 49156
  117.1 13.0 %copy-start.7 = (f32[8,512]{1,0:T(8,128)}, f32[8,512]{1,0:T(8,128)S(1)}, u32[]{:S(2)}) copy-start(f32[8,512]{1,0:T(8,128)S(1)} %convolution_subtract_fusion) | copy-start | bytes 49156
  118.4 8.6 %copy-start.2 = (f32[128,8,128]{2,1,0:T(8,128)S(1)}, f32[128,8,128]{2,1,0:T(8,128)}, u32[]{:S(2)}) copy-start(f32[128,8,128]{2,1,0:T(8,128)} %fusion.6.colv_ref) | copy-start | bytes 1572868
  127.0 2.7 %copy-start.5 = (f32[32,8,128]{2,1,0:T(8,128)S(1)}, f32[32,8,128]{2,1,0:T(8,128)}, u32[]{:S(2)}) copy-start(f32[32,8,128]{2,1,0:T(8,128)} %fusion.7.rowv_ref) | copy-start | bytes 393220
  127.0 2.7 %copy-start.6 = (f32[32,8,128]{2,1,0:T(8,128)S(1)}, f32[32,8,128]{2,1,0:T(8,128)}, u32[]{:S(2)}) copy-start(f32[32,8,128]{2,1,0:T(8,128)} %get-tuple-element.25.rsum_ref) | copy-start | bytes 393220

commit v7 on v6

--- a/solution.py
+++ b/solution.py
@@ -377,7 +377,9 @@
     def one(x, y):
         return lax.dot_general(x, y, dims, preferred_element_type=jnp.float32)
 
-    return one(left[0], right[0]) + (one(left[0], right[1]) + one(left[1], right[0]))
+    rows = left[0].shape[0]
+    both = one(jnp.concatenate([left[0], left[1]], axis=0), right[0])
+    return both[:rows] + (both[rows:] + one(left[0], right[1]))
 
 
 def slot_products(blocks, rows_here, cols_here, live_count, row_tiles, column_tiles, rows_k):
@@ -460,7 +462,8 @@
     residual = image - jnp.dot(ritz_matrix.T, current, precision=highest)
 
     def residual_of(img_tiles, cur_tiles):
-        return img_tiles - jnp.einsum("lk,tli->tki", ritz_matrix, cur_tiles, precision=highest)
+        fitted = sum(ritz_matrix[l][None, :, None] * cur_tiles[:, l:l + 1, :] for l in range(k))
+        return img_tiles - fitted
 
     row_res = residual_of(row_img, row_cur)
     col_res = residual_of(col_img, col_cur)

time: 184 us -> 176 us (0.957)
  matrix products: 14.3 us -> 10.1 us
  Pallas kernels: 146 us -> 143 us
    dot_general x2 -> x0, matrix products: 4.35 us -> none  [residual_of(): jnp.einsum('lk,tli->tki', ritz_matrix, cur_tiles, precision=highest)]
    pallas_call x2, Pallas kernels: 17.5 us -> 14.8 us  [slot_products(): pl.pallas_call(functools.partial(_slots_kernel, group, rows_k), grid_spec...]
    slice x0 -> x2, other arithmetic: none -> 1.97 us  [local(): row_cur, col_cur = (row_cp[:, :k], col_cp[:, :k])]
where the time goes in v7:
time: 176 us; the launch traced here: 174 us
  Pallas kernels  143 us (81%)
  other arithmetic  13.9 us (8%)
  matrix products  10.1 us (6%)
  local copies, waits for them, and re-layouts  5.01 us (3%)
    pallas_call x2, Pallas kernels, reduce_tiles(): pl.pallas_call(functools.partial(_reduce_kernel, n_row, n_col, forward),...  84.1 us
    pallas_call x1, Pallas kernels, gather_tiles(): pl.pallas_call(functools.partial(_gather_kernel, n_row, n_col), out_shape...  44.1 us
    pallas_call x2, Pallas kernels, slot_products(): pl.pallas_call(functools.partial(_slots_kernel, group, rows_k), grid_spec...  14.8 us
    dot_general x4, matrix products, tile_dot(): return jnp.einsum('tki,tli->kl', left, right, precision=highest)  7.58 us

profile of v7, /device:TPU:24, one launch (start us, length us, event | category | flops | bytes accessed | tf_op | source)
XLA Modules:
  0.0 173.6 jit_solution(3136247053253544620)
XLA Ops:
  0.6 1.3 bitcast_bitcast_fusion.x_ref
  2.0 44.1 %shard_map.111 = (f32[32,16,128]{2,1,0:T(8,128)}, f32[128,16,128]{2,1,0:T(8,128)}) custom-call(f32[4,16,128]{2,1,0:T(8,128)} %bitcast_bitcast_fusion.x_ref), custom_call_target="tpu_custom_call" | custom-call | tf_op jit(solution)/shard_map/pallas_call | solution.py:92
  46.8 7.5 %shard_map.112 = (f32[32,8,128]{2,1,0:T(8,128)}, f32[128,8,128]{2,1,0:T(8,128)}) custom-call(s32[64]{0:T(128)} %bitcast.147, s32[64]{0:T(128)} %bitcast.149, s32[1]{0:T(128)} %bitcast.122.count_ref, f32[64,128,128]{2,1,0:T(8,128)} %bitcast.124, f32[32,16,128]{2,1,0:T(8,128)} %get-tuple-element.17.rowv_ref, f32[128,16,128]{2,1,0:T(8,128)} %get-tuple-element.18.colv_ref), custom_call_target="tpu_custom_call" | custom-call | tf_op jit(solution)/shard_map/pallas_call | solution.py:411
  54.4 1.3 convolution_bitcast_fusion.2
  55.6 2.3 %convolution_bitcast_fusion.1 = f32[8,8]{0,1:T(8,128)S(1)} fusion(f32[128,8,128]{2,1,0:T(8,128)} %get-tuple-element.20.csum_ref, f32[128,16,128]{2,1,0:T(8,128)S(1)} %copy-done.1), kind=kOutput, calls=%fused_computation.10 | convolution fusion | flops 12582912 | bytes 1048832 | tf_op jit(solution)/shard_map/tki,tli->kl/dot_general | solution.py:431
  58.5 0.7 fusion.36.small_ref
  59.2 0.6 multiply_bitcast_fusion.base_ref
  59.8 47.3 %shard_map.113 = (f32[4,8,128]{2,1,0:T(8,128)}, f32[8,128]{1,0:T(8,128)}, f32[32,8,128]{2,1,0:T(8,128)}, f32[128,8,128]{2,1,0:T(8,128)}) custom-call(f32[4,8,128]{2,1,0:T(8,128)} %multiply_bitcast_fusion.base_ref, f32[32,8,128]{2,1,0:T(8,128)} %get-tuple-element.19.rsum_ref, f32[128,8,128]{2,1,0:T(8,128)} %get-tuple-element.20.csum_ref, ...), custom_call_target="tpu_custom_call" | custom-call | tf_op jit(solution)/shard_map/pallas_call | solution.py:323
  107.1 0.8 slice.154
  108.0 0.7 cholesky.30
  108.8 0.6 compare_reduce_fusion.1
  109.4 0.6 fusion.33
  110.1 0.6 custom-call.16
  111.1 0.4 fusion.51
  111.4 1.2 fusion.50
  112.7 0.8 fusion.52
  113.5 7.3 %shard_map.114 = (f32[32,8,128]{2,1,0:T(8,128)}, f32[128,8,128]{2,1,0:T(8,128)}) custom-call(s32[64]{0:T(128)} %bitcast.148, s32[64]{0:T(128)} %bitcast.150, s32[1]{0:T(128)} %bitcast.123.count_ref, f32[64,128,128]{2,1,0:T(8,128)} %bitcast.125, f32[32,8,128]{2,1,0:T(8,128)} %get-tuple-element.60.rowv_ref, f32[128,8,128]{2,1,0:T(8,128)} %get-tuple-element.59.colv_ref), custom_call_target="tpu_custom_call" | custom-call | tf_op jit(solution)/shard_map/pallas_call | solution.py:411
  120.8 1.4 convolution_bitcast_fusion.4
  122.2 2.6 %fusion.9 = f32[24,8]{0,1:T(8,128)S(1)} fusion(f32[128,8,128]{2,1,0:T(8,128)} %get-tuple-element.26.csum_ref, f32[128,8,128]{2,1,0:T(8,128)S(1)} %get-tuple-element.30, f32[128,8,128]{2,1,0:T(8,128)S(1)} %copy-done.2, f32[128,8,128]{2,1,0:T(8,128)S(1)} %get-tuple-element.29), kind=kOutput, calls=%fused_computation.15 | convolution fusion | flops 38535168 | bytes 2097920 | tf_op jit(solution)/shard_map/tki,tli->kl/dot_general | solution.py:431
  124.8 0.2 convolution_subtract_fusion
  126.0 0.7 fusion.26.small_ref
  126.7 0.6 multiply_bitcast_fusion.1.base_ref
  127.3 36.8 %shard_map.115 = (f32[4,8,128]{2,1,0:T(8,128)}, f32[16,128]{1,0:T(8,128)}) custom-call(f32[4,8,128]{2,1,0:T(8,128)} %multiply_bitcast_fusion.1.base_ref, f32[32,8,128]{2,1,0:T(8,128)} %get-tuple-element.25.rsum_ref, f32[128,8,128]{2,1,0:T(8,128)} %get-tuple-element.26.csum_ref, f32[16,128]{1,0:T(8,128)} %fusion.26.small_ref), custom_call_target="tpu_custom_call" | custom-call | tf_op jit(solution)/shard_map/pallas_call | solution.py:323
  164.0 0.8 fusion.54
  165.0 2.2 %cholesky.64 = f32[24,24]{1,0:T(8,128)S(1)} custom-call(f32[24,24]{1,0:T(8,128)S(1)} %fusion.25), custom_call_target="Cholesky" | custom-call | tf_op jit(solution)/shard_map/jit(cholesky)/cholesky | solution.py:488
  167.3 0.6 compare_reduce_fusion
  167.9 0.6 fusion.19
  168.6 1.8 %custom-call.19 = f32[1,24,24]{1,2,0:T(8,128)S(1)} custom-call(f32[1,24,24]{2,1,0:T(8,128)S(1)} %fusion.19), custom_call_target="InvertDiagBlocksLowerTriangular" | custom-call | tf_op jit(solution)/shard_map/jit(_solve_triangular)/triangular_solve | solution.py:490
  170.6 0.2 convolution_bitcast_fusion
  170.8 0.8 fusion.23
  171.6 0.6 copy.51
  172.2 1.3 copy.52
  (51 shorter events, 2.4 us)
Async XLA Ops:
  0.6 124.7 %copy-start = (f32[8,512]{1,0:T(8,128)S(1)}, f32[8,512]{1,0:T(8,128)}, u32[]{:S(2)}) copy-start(f32[8,512]{1,0:T(8,128)} %param.17) | copy-start | bytes 49156
  46.8 7.6 %copy-start.3 = (f32[32,16,128]{2,1,0:T(8,128)S(1)}, f32[32,16,128]{2,1,0:T(8,128)}, u32[]{:S(2)}) copy-start(f32[32,16,128]{2,1,0:T(8,128)} %get-tuple-element.17.rowv_ref) | copy-start | bytes 786436
  46.8 8.8 %copy-start.1 = (f32[128,16,128]{2,1,0:T(8,128)S(1)}, f32[128,16,128]{2,1,0:T(8,128)}, u32[]{:S(2)}) copy-start(f32[128,16,128]{2,1,0:T(8,128)} %get-tuple-element.18.colv_ref) | copy-start | bytes 3145732
  46.8 11.1 %copy-start.4 = (f32[8,512]{1,0:T(8,128)S(1)}, f32[8,512]{1,0:T(8,128)}, u32[]{:S(2)}) copy-start(f32[8,512]{1,0:T(8,128)} %param.15) | copy-start | bytes 49156
  46.8 11.1 %copy-start.11 = (f32[512]{0:T(512)S(1)}, f32[512]{0:T(512)}, u32[]{:S(2)}) copy-start(f32[512]{0:T(512)} %param.14) | copy-start | bytes 6148
  107.1 4.3 %copy-start.6 = (f32[128,8,128]{2,1,0:T(8,128)S(1)}, f32[128,8,128]{2,1,0:T(8,128)}, u32[]{:S(2)}) copy-start(f32[128,8,128]{2,1,0:T(8,128)} %get-tuple-element.24) | copy-start | bytes 1572868
  111.4 1.3 copy-start.10
  113.5 7.3 %copy-start.5 = (f32[32,8,128]{2,1,0:T(8,128)S(1)}, f32[32,8,128]{2,1,0:T(8,128)}, u32[]{:S(2)}) copy-start(f32[32,8,128]{2,1,0:T(8,128)} %get-tuple-element.60.rowv_ref) | copy-start | bytes 393220
  113.5 8.7 %copy-start.2 = (f32[128,8,128]{2,1,0:T(8,128)S(1)}, f32[128,8,128]{2,1,0:T(8,128)}, u32[]{:S(2)}) copy-start(f32[128,8,128]{2,1,0:T(8,128)} %get-tuple-element.59.colv_ref) | copy-start | bytes 1572868
  120.8 4.0 %copy-start.9 = (f32[4,8,128]{2,1,0:T(8,128)S(1)}, f32[4,8,128]{2,1,0:T(8,128)}, u32[]{:S(2)}) copy-start(f32[4,8,128]{2,1,0:T(8,128)} %get-tuple-element.21) | copy-start | bytes 49156
  120.8 4.2 %copy-start.8 = (f32[8,512]{1,0:T(8,128)S(1)}, f32[8,512]{1,0:T(8,128)}, u32[]{:S(2)}) copy-start(f32[8,512]{1,0:T(8,128)} %param.16) | copy-start | bytes 49156
  125.0 48.5 %copy-start.7 = (f32[8,512]{1,0:T(8,128)}, f32[8,512]{1,0:T(8,128)S(1)}, u32[]{:S(2)}) copy-start(f32[8,512]{1,0:T(8,128)S(1)} %convolution_subtract_fusion) | copy-start | bytes 49156

commit v8 on v7

--- a/solution.py
+++ b/solution.py
@@ -345,7 +345,7 @@
     )(base_tiles, row_sum, col_sum, small)
 
 
-def _slots_kernel(group, rows_k, rows_ref, cols_ref, count_ref, tiles_ref, rowv_ref, colv_ref,
+def _slots_kernel(group, rows_k, rows_ref, cols_ref, count_ref, high_ref, low_ref, rowv_ref, colv_ref,
                   rsum_ref, csum_ref):
     g = pl.program_id(0)
 
@@ -361,7 +361,7 @@
         def _():
             a = rows_ref[slot]
             b = cols_ref[slot]
-            block = split_bf16(tiles_ref[s])
+            block = (high_ref[s], low_ref[s])
             direct = dot3(split_bf16(colv_ref[b, pl.ds(0, rows_k), :]), block, (((1,), (1,)), ((), ())))
             rsum_ref[a] += direct
             mirror = dot3(split_bf16(rowv_ref[a, pl.ds(0, rows_k), :]), block, (((1,), (0,)), ((), ())))
@@ -373,6 +373,11 @@
     return high, (x - high.astype(jnp.float32)).astype(jnp.bfloat16)
 
 
+def split_tiles(x):
+    high = lax.reduce_precision(x, exponent_bits=8, mantissa_bits=7)
+    return high.astype(jnp.bfloat16), (x - high).astype(jnp.bfloat16)
+
+
 def dot3(left, right, dims):
     def one(x, y):
         return lax.dot_general(x, y, dims, preferred_element_type=jnp.float32)
@@ -383,7 +388,7 @@
 
 
 def slot_products(blocks, rows_here, cols_here, live_count, row_tiles, column_tiles, rows_k):
-    slot_count, tile, _ = blocks.shape
+    slot_count, tile, _ = blocks[0].shape
     sums_shape = lambda v: (v.shape[0], rows_k, v.shape[2])
     group = group_width
     groups = slot_count // group
@@ -399,6 +404,7 @@
         num_scalar_prefetch=3,
         grid=(groups,),
         in_specs=[
+            pl.BlockSpec((group, tile, tile), tile_map),
             pl.BlockSpec((group, tile, tile), tile_map),
             pl.BlockSpec(row_tiles.shape, whole),
             pl.BlockSpec(column_tiles.shape, whole),
@@ -416,7 +422,7 @@
             jax.ShapeDtypeStruct(sums_shape(column_tiles), jnp.float32),
         ),
         compiler_params=pltpu.CompilerParams(dimension_semantics=("arbitrary",)),
-    )(rows_here, cols_here, live_count.reshape(1), blocks, row_tiles, column_tiles)
+    )(rows_here, cols_here, live_count.reshape(1), blocks[0], blocks[1], row_tiles, column_tiles)
 
 
 def to_tiles(vectors, tile):
@@ -439,7 +445,7 @@
     k = current.shape[0]
     tile = tile_values.shape[-1]
     slot_count = tile_values.shape[2]
-    blocks = tile_values.reshape(slot_count, tile, tile)
+    blocks = split_tiles(tile_values.reshape(slot_count, tile, tile))
     rows_here = tile_row.reshape(slot_count)
     cols_here = tile_col.reshape(slot_count)
     live_count = counts.reshape(())

time: 176 us -> 189 us (1.074)
  other arithmetic: 13.9 us -> 20.4 us
  Pallas kernels: 143 us -> 148 us
    convert_element_type x0 -> x1, other arithmetic: none -> 5.34 us  [split_tiles(): return (high.astype(jnp.bfloat16), (x - high).astype(jnp.bfloat16))]
    pallas_call x2, Pallas kernels: 14.8 us -> 17.4 us  [slot_products(): pl.pallas_call(functools.partial(_slots_kernel, group, rows_k), grid_spec...]
    pallas_call x2, Pallas kernels: 84.1 us -> 86.7 us  [reduce_tiles(): pl.pallas_call(functools.partial(_reduce_kernel, n_row, n_col, forward),...]
where the time goes in v8:
time: 189 us; the launch traced here: 187 us
  Pallas kernels  148 us (78%)
  other arithmetic  20.4 us (11%)
  matrix products  11.5 us (6%)
  local copies, waits for them, and re-layouts  4.96 us (3%)
    pallas_call x2, Pallas kernels, reduce_tiles(): pl.pallas_call(functools.partial(_reduce_kernel, n_row, n_col, forward),...  86.7 us
    pallas_call x1, Pallas kernels, gather_tiles(): pl.pallas_call(functools.partial(_gather_kernel, n_row, n_col), out_shape...  44.1 us
    pallas_call x2, Pallas kernels, slot_products(): pl.pallas_call(functools.partial(_slots_kernel, group, rows_k), grid_spec...  17.4 us
    dot_general x4, matrix products, tile_dot(): return jnp.einsum('tki,tli->kl', left, right, precision=highest)  7.57 us
    convert_element_type x1, other arithmetic, split_tiles(): return (high.astype(jnp.bfloat16), (x - high).astype(jnp.bfloat16))  5.34 us

profile of v8, /device:TPU:24, one launch (start us, length us, event | category | flops | bytes accessed | tf_op | source)
XLA Modules:
  0.0 186.6 jit_solution(14046059826307784692)
XLA Ops:
  0.6 1.3 bitcast_bitcast_fusion.x_ref
  2.0 44.1 %shard_map.111 = (f32[32,16,128]{2,1,0:T(8,128)}, f32[128,16,128]{2,1,0:T(8,128)}) custom-call(f32[4,16,128]{2,1,0:T(8,128)} %bitcast_bitcast_fusion.x_ref), custom_call_target="tpu_custom_call" | custom-call | tf_op jit(solution)/shard_map/pallas_call | solution.py:92
  46.1 5.3 %fusion = (bf16[64,128,128]{2,1,0:T(8,128)(2,1)}, bf16[64,128,128]{2,1,0:T(8,128)(2,1)}) fusion(f32[1,1,64,128,128]{4,3,2,1,0:T(8,128)} %param.10), kind=kLoop, calls=%fused_computation.2 | loop fusion | flops 4194304 | bytes 8388608 | tf_op jit(solution)/shard_map/convert_element_type | solution.py:378
  52.2 8.8 %shard_map.112 = (f32[32,8,128]{2,1,0:T(8,128)}, f32[128,8,128]{2,1,0:T(8,128)}) custom-call(s32[64]{0:T(128)} %bitcast.147, s32[64]{0:T(128)} %bitcast.149, s32[1]{0:T(128)} %bitcast.124.count_ref, bf16[64,128,128]{2,1,0:T(8,128)(2,1)} %get-tuple-element.30.high_ref, bf16[64,128,128]{2,1,0:T(8,128)(2,1)} %get-tuple-element.29.low_ref, ...), custom_call_target="tpu_custom_call" | custom-call | tf_op jit(solution)/shard_map/pallas_call | solution.py:417
  61.0 1.3 convolution_bitcast_fusion.2
  62.3 2.3 %convolution_bitcast_fusion.1 = f32[8,8]{0,1:T(8,128)S(1)} fusion(f32[128,8,128]{2,1,0:T(8,128)} %get-tuple-element.20.csum_ref, f32[128,16,128]{2,1,0:T(8,128)S(1)} %copy-done.1), kind=kOutput, calls=%fused_computation.13 | convolution fusion | flops 12582912 | bytes 1048832 | tf_op jit(solution)/shard_map/tki,tli->kl/dot_general | solution.py:437
  65.2 0.7 fusion.37.small_ref
  65.8 0.6 multiply_bitcast_fusion.base_ref
  66.4 44.1 %shard_map.113 = (f32[4,8,128]{2,1,0:T(8,128)}, f32[8,128]{1,0:T(8,128)}, f32[32,8,128]{2,1,0:T(8,128)}, f32[128,8,128]{2,1,0:T(8,128)}) custom-call(f32[4,8,128]{2,1,0:T(8,128)} %multiply_bitcast_fusion.base_ref, f32[32,8,128]{2,1,0:T(8,128)} %get-tuple-element.19.rsum_ref, f32[128,8,128]{2,1,0:T(8,128)} %get-tuple-element.20.csum_ref, ...), custom_call_target="tpu_custom_call" | custom-call | tf_op jit(solution)/shard_map/pallas_call | solution.py:323
  110.6 0.8 slice.154
  111.4 0.7 cholesky.30
  112.2 0.6 compare_reduce_fusion.1
  112.8 0.6 fusion.34
  113.5 0.6 custom-call.16
  114.4 0.9 convolution_subtract_fusion
  115.4 0.9 fusion.32
  116.6 2.3 %fusion.51 = (f32[128,8,128]{2,1,0:T(8,128)S(1)}, f32[128,8,128]{2,1,0:T(8,128)S(1)}, f32[128,8,128]{2,1,0:T(8,128)}) fusion(f32[128,16,128]{2,1,0:T(8,128)S(1)} %copy-done.1, f32[128,8,128]{2,1,0:T(8,128)} %get-tuple-element.24, f32[128,128]{1,0:T(8,128)S(1)} %bitcast.127, f32[8]{0:T(128)S(1)} %get-tuple-element.54, f32[128,128]{1,0:T(8,128)S(1)} %bitcast.128, ...), kind=kLoop, calls=%fused_computation.90 | loop fusion | flops 2097152 | bytes 3670272 | tf_op jit(solution)/shard_map/slice | solution.py:455
  119.0 0.8 fusion.53
  119.8 8.6 %shard_map.114 = (f32[32,8,128]{2,1,0:T(8,128)}, f32[128,8,128]{2,1,0:T(8,128)}) custom-call(s32[64]{0:T(128)} %bitcast.148, s32[64]{0:T(128)} %bitcast.150, s32[1]{0:T(128)} %bitcast.125.count_ref, bf16[64,128,128]{2,1,0:T(8,128)(2,1)} %get-tuple-element.30.high_ref, bf16[64,128,128]{2,1,0:T(8,128)(2,1)} %get-tuple-element.29.low_ref, ...), custom_call_target="tpu_custom_call" | custom-call | tf_op jit(solution)/shard_map/pallas_call | solution.py:417
  128.4 1.4 convolution_bitcast_fusion.4
  129.8 2.6 %fusion.10 = f32[24,8]{0,1:T(8,128)S(1)} fusion(f32[128,8,128]{2,1,0:T(8,128)} %get-tuple-element.26.csum_ref, f32[128,8,128]{2,1,0:T(8,128)S(1)} %get-tuple-element.32, f32[128,8,128]{2,1,0:T(8,128)S(1)} %copy-done.2, f32[128,8,128]{2,1,0:T(8,128)S(1)} %get-tuple-element.31), kind=kOutput, calls=%fused_computation.18 | convolution fusion | flops 38535168 | bytes 2097920 | tf_op jit(solution)/shard_map/tki,tli->kl/dot_general | solution.py:437
  133.2 0.7 fusion.27.small_ref
  133.9 0.6 multiply_bitcast_fusion.1.base_ref
  134.5 42.6 %shard_map.115 = (f32[4,8,128]{2,1,0:T(8,128)}, f32[16,128]{1,0:T(8,128)}) custom-call(f32[4,8,128]{2,1,0:T(8,128)} %multiply_bitcast_fusion.1.base_ref, f32[32,8,128]{2,1,0:T(8,128)} %get-tuple-element.25.rsum_ref, f32[128,8,128]{2,1,0:T(8,128)} %get-tuple-element.26.csum_ref, f32[16,128]{1,0:T(8,128)} %fusion.27.small_ref), custom_call_target="tpu_custom_call" | custom-call | tf_op jit(solution)/shard_map/pallas_call | solution.py:323
  177.1 0.8 fusion.55
  178.1 2.2 %cholesky.64 = f32[24,24]{1,0:T(8,128)S(1)} custom-call(f32[24,24]{1,0:T(8,128)S(1)} %fusion.26), custom_call_target="Cholesky" | custom-call | tf_op jit(solution)/shard_map/jit(cholesky)/cholesky | solution.py:494
  180.3 0.6 compare_reduce_fusion
  181.0 0.6 fusion.20
  181.6 1.8 custom-call.19
  183.8 0.8 fusion.24
  184.7 0.6 copy.51
  185.3 1.3 copy.52
  (50 shorter events, 2.8 us)
Async XLA Ops:
  0.6 131.9 %copy-start = (f32[8,512]{1,0:T(8,128)S(1)}, f32[8,512]{1,0:T(8,128)}, u32[]{:S(2)}) copy-start(f32[8,512]{1,0:T(8,128)} %param.17) | copy-start | bytes 49156
  52.1 8.9 %copy-start.3 = (f32[32,16,128]{2,1,0:T(8,128)S(1)}, f32[32,16,128]{2,1,0:T(8,128)}, u32[]{:S(2)}) copy-start(f32[32,16,128]{2,1,0:T(8,128)} %get-tuple-element.17.rowv_ref) | copy-start | bytes 786436
  52.1 10.2 %copy-start.1 = (f32[128,16,128]{2,1,0:T(8,128)S(1)}, f32[128,16,128]{2,1,0:T(8,128)}, u32[]{:S(2)}) copy-start(f32[128,16,128]{2,1,0:T(8,128)} %get-tuple-element.18.colv_ref) | copy-start | bytes 3145732
  52.2 12.5 %copy-start.4 = (f32[8,512]{1,0:T(8,128)S(1)}, f32[8,512]{1,0:T(8,128)}, u32[]{:S(2)}) copy-start(f32[8,512]{1,0:T(8,128)} %param.15) | copy-start | bytes 49156
  52.2 12.4 %copy-start.10 = (f32[512]{0:T(512)S(1)}, f32[512]{0:T(512)}, u32[]{:S(2)}) copy-start(f32[512]{0:T(512)} %param.14) | copy-start | bytes 6148
  61.0 54.3 %copy-start.7 = (f32[8,512]{1,0:T(8,128)S(1)}, f32[8,512]{1,0:T(8,128)}, u32[]{:S(2)}) copy-start(f32[8,512]{1,0:T(8,128)} %param.16) | copy-start | bytes 49156
  115.4 18.5 %copy-start.6 = (f32[8,512]{1,0:T(8,128)}, f32[8,512]{1,0:T(8,128)S(1)}, u32[]{:S(2)}) copy-start(f32[8,512]{1,0:T(8,128)S(1)} %convolution_subtract_fusion) | copy-start | bytes 49156
  116.6 2.4 %copy-start.9 = (f32[32,8,128]{2,1,0:T(8,128)S(1)}, f32[32,8,128]{2,1,0:T(8,128)}, u32[]{:S(2)}) copy-start(f32[32,8,128]{2,1,0:T(8,128)} %get-tuple-element.23) | copy-start | bytes 393220
  119.8 8.6 %copy-start.5 = (f32[32,8,128]{2,1,0:T(8,128)S(1)}, f32[32,8,128]{2,1,0:T(8,128)}, u32[]{:S(2)}) copy-start(f32[32,8,128]{2,1,0:T(8,128)} %get-tuple-element.62.rowv_ref) | copy-start | bytes 393220
  119.8 10.0 %copy-start.2 = (f32[128,8,128]{2,1,0:T(8,128)S(1)}, f32[128,8,128]{2,1,0:T(8,128)}, u32[]{:S(2)}) copy-start(f32[128,8,128]{2,1,0:T(8,128)} %get-tuple-element.61.colv_ref) | copy-start | bytes 1572868
  128.4 56.3 %copy-start.8 = (f32[4,8,128]{2,1,0:T(8,128)S(1)}, f32[4,8,128]{2,1,0:T(8,128)}, u32[]{:S(2)}) copy-start(f32[4,8,128]{2,1,0:T(8,128)} %get-tuple-element.21) | copy-start | bytes 49156

commit v9 on v7

--- a/solution.py
+++ b/solution.py
@@ -428,7 +428,7 @@
 
 
 def tile_dot(left, right):
-    return jnp.einsum("tki,tli->kl", left, right, precision=highest)
+    return jnp.sum(left[:, :, None, :] * right[:, None, :, :], axis=(0, 3))
 
 
 def dot_rows(left, right):

time: 176 us -> 190 us (1.080)
  the two profiles are of different devices: /device:TPU:24 before, /device:TPU:33 now
where the time goes in v9:
time: 190 us; the launch traced here: 188 us
  Pallas kernels  151 us (79%)
  other arithmetic  20.7 us (11%)
  local copies, waits for them, and re-layouts  9.94 us (5%)
  matrix products  5.44 us (3%)
    pallas_call x2, Pallas kernels, reduce_tiles(): pl.pallas_call(functools.partial(_reduce_kernel, n_row, n_col, forward),...  87.4 us
    pallas_call x1, Pallas kernels, gather_tiles(): pl.pallas_call(functools.partial(_gather_kernel, n_row, n_col), out_shape...  44 us
    pallas_call x2, Pallas kernels, slot_products(): pl.pallas_call(functools.partial(_slots_kernel, group, rows_k), grid_spec...  19.4 us
    reduce_sum x4, other arithmetic, tile_dot(): return jnp.sum(left[:, :, None, :] * right[:, None, :, :], axis=(0, 3))  3.99 us

profile of v9, /device:TPU:33, one launch (start us, length us, event | category | flops | bytes accessed | tf_op | source)
XLA Modules:
  0.0 188.4 jit_solution(8180377945098659757)
XLA Ops:
  1.3 0.9 fusion.37
  2.2 0.7 reshape.109
  2.9 1.3 multiply_bitcast_fusion.base_ref
  4.2 1.3 bitcast_bitcast_fusion.x_ref
  5.6 44.0 %shard_map.111 = (f32[32,16,128]{2,1,0:T(8,128)}, f32[128,16,128]{2,1,0:T(8,128)}) custom-call(f32[4,16,128]{2,1,0:T(8,128)} %bitcast_bitcast_fusion.x_ref), custom_call_target="tpu_custom_call" | custom-call | tf_op jit(solution)/shard_map/pallas_call | solution.py:92
  49.6 2.5 %fusion.35 = (f32[32,1,128]{2,1,0:T(1,128)S(1)}, f32[32,1,128]{2,1,0:T(1,128)S(1)}, f32[32,1,128]{2,1,0:T(1,128)S(1)}, f32[32,1,128]{2,1,0:T(1,128)S(1)}, f32[32...) fusion(f32[32,16,128]{2,1,0:T(8,128)} %get-tuple-element.17.rowv_ref), kind=kLoop, calls=%fused_computation.77 | loop fusion | bytes 262144 | tf_op jit(solution)/shard_map/slice | solution.py:465
  52.1 1.1 fusion.34
  53.2 9.8 %shard_map.112 = (f32[32,8,128]{2,1,0:T(8,128)}, f32[128,8,128]{2,1,0:T(8,128)}) custom-call(s32[64]{0:T(128)} %bitcast.135, s32[64]{0:T(128)} %bitcast.137, s32[1]{0:T(128)} %bitcast.110.count_ref, f32[64,128,128]{2,1,0:T(8,128)} %bitcast.112, f32[32,16,128]{2,1,0:T(8,128)} %get-tuple-element.17.rowv_ref, f32[128,16,128]{2,1,0:T(8,128)} %get-tuple-element.18.colv_ref), custom_call_target="tpu_custom_call" | custom-call | tf_op jit(solution)/shard_map/pallas_call | solution.py:411
  63.0 1.1 multiply_reduce_fusion.3
  64.1 0.7 copy.26
  65.8 0.8 fusion.2
  66.8 1.3 fusion.22.small_ref
  68.1 46.2 %shard_map.113 = (f32[4,8,128]{2,1,0:T(8,128)}, f32[8,128]{1,0:T(8,128)}, f32[32,8,128]{2,1,0:T(8,128)}, f32[128,8,128]{2,1,0:T(8,128)}) custom-call(f32[4,8,128]{2,1,0:T(8,128)} %multiply_bitcast_fusion.base_ref, f32[32,8,128]{2,1,0:T(8,128)} %get-tuple-element.19.rsum_ref, f32[128,8,128]{2,1,0:T(8,128)} %get-tuple-element.20.csum_ref, ...), custom_call_target="tpu_custom_call" | custom-call | tf_op jit(solution)/shard_map/pallas_call | solution.py:323
  114.4 0.8 slice.154
  115.2 0.7 cholesky.30
  116.0 0.6 compare_reduce_fusion.1
  116.6 0.6 fusion.19
  118.2 2.2 %add_subtract_fusion.colv_ref = f32[128,8,128]{2,1,0:T(8,128)} fusion(f32[128,8,128]{2,1,0:T(8,128)} %get-tuple-element.24, f32[128,128]{1,0:T(8,128)S(1)} %bitcast.115, f32[8]{0:T(128)S(1)} %get-tuple-element.52, f32[128,128]{1,0:T(8,128)S(1)} %bitcast.116, f32[8]{0:T(128)S(1)} %get-tuple-element.53, f32[128,128]{1,0:T(8,128)S(1)} %bitcast.117, ...), kind=kLoop, calls=%fused_computation.12 | loop fusion | flops 2097152 | bytes 1573120 | tf_op jit(solution)/shard_map/sub | solution.py:466
  120.4 1.1 add_subtract_fusion.1.rowv_ref
  121.5 0.9 convolution_subtract_fusion
  122.5 0.9 fusion.17
  124.4 9.6 %shard_map.114 = (f32[32,8,128]{2,1,0:T(8,128)}, f32[128,8,128]{2,1,0:T(8,128)}) custom-call(s32[64]{0:T(128)} %bitcast.136, s32[64]{0:T(128)} %bitcast.138, s32[1]{0:T(128)} %bitcast.111.count_ref, f32[64,128,128]{2,1,0:T(8,128)} %bitcast.113, f32[32,8,128]{2,1,0:T(8,128)} %copy-done.6, f32[128,8,128]{2,1,0:T(8,128)} %add_subtract_fusion.colv_ref), custom_call_target="tpu_custom_call" | custom-call | tf_op jit(solution)/shard_map/pallas_call | solution.py:411
  134.0 1.3 multiply_reduce_fusion.2
  135.5 1.1 multiply_reduce_fusion
  137.0 0.7 fusion.12.small_ref
  137.7 41.2 %shard_map.115 = (f32[4,8,128]{2,1,0:T(8,128)}, f32[16,128]{1,0:T(8,128)}) custom-call(f32[4,8,128]{2,1,0:T(8,128)} %multiply_bitcast_fusion.1.base_ref, f32[32,8,128]{2,1,0:T(8,128)} %get-tuple-element.25.rsum_ref, f32[128,8,128]{2,1,0:T(8,128)} %get-tuple-element.26.csum_ref, f32[16,128]{1,0:T(8,128)} %fusion.12.small_ref), custom_call_target="tpu_custom_call" | custom-call | tf_op jit(solution)/shard_map/pallas_call | solution.py:323
  178.9 0.8 fusion.36
  180.1 2.2 %cholesky.64 = f32[24,24]{1,0:T(8,128)S(1)} custom-call(f32[24,24]{1,0:T(8,128)S(1)} %fusion.11), custom_call_target="Cholesky" | custom-call | tf_op jit(solution)/shard_map/jit(cholesky)/cholesky | solution.py:488
  183.0 0.6 fusion.5
  183.6 1.8 custom-call.19
  185.7 0.8 fusion.9
  187.1 1.3 copy.44
  (57 shorter events, 5.7 us)
Async XLA Ops:
  0.6 122.7 %copy-start = (f32[8,512]{1,0:T(8,128)S(1)}, f32[8,512]{1,0:T(8,128)}, u32[]{:S(2)}) copy-start(f32[8,512]{1,0:T(8,128)} %param.17) | copy-start | bytes 49156
  52.1 12.7 %copy-start.1 = (f32[128,16,128]{2,1,0:T(8,128)S(1)}, f32[128,16,128]{2,1,0:T(8,128)}, u32[]{:S(2)}) copy-start(f32[128,16,128]{2,1,0:T(8,128)} %get-tuple-element.18.colv_ref) | copy-start | bytes 3145732
  63.0 2.3 %copy-start.3 = (f32[128,8,128]{2,1,0:T(8,128)S(1)}, f32[128,8,128]{2,1,0:T(8,128)}, u32[]{:S(2)}) copy-start(f32[128,8,128]{2,1,0:T(8,128)} %get-tuple-element.20.csum_ref) | copy-start | bytes 1572868
  63.0 2.8 %copy-start.5 = (f32[8,512]{1,0:T(8,128)S(1)}, f32[8,512]{1,0:T(8,128)}, u32[]{:S(2)}) copy-start(f32[8,512]{1,0:T(8,128)} %param.15) | copy-start | bytes 49156
  65.1 57.3 %copy-start.8 = (f32[8,512]{1,0:T(8,128)S(1)}, f32[8,512]{1,0:T(8,128)}, u32[]{:S(2)}) copy-start(f32[8,512]{1,0:T(8,128)} %param.16) | copy-start | bytes 49156
  65.2 58.6 %copy-start.10 = (f32[512]{0:T(512)S(1)}, f32[512]{0:T(512)}, u32[]{:S(2)}) copy-start(f32[512]{0:T(512)} %param.14) | copy-start | bytes 6148
  121.5 2.9 %copy-start.6 = (f32[32,8,128]{2,1,0:T(8,128)}, f32[32,8,128]{2,1,0:T(8,128)S(1)}, u32[]{:S(2)}) copy-start(f32[32,8,128]{2,1,0:T(8,128)S(1)} %add_subtract_fusion.1.rowv_ref) | copy-start | bytes 393220
  122.4 14.2 %copy-start.7 = (f32[8,512]{1,0:T(8,128)}, f32[8,512]{1,0:T(8,128)S(1)}, u32[]{:S(2)}) copy-start(f32[8,512]{1,0:T(8,128)S(1)} %convolution_subtract_fusion) | copy-start | bytes 49156
  123.5 11.9 %copy-start.2 = (f32[128,8,128]{2,1,0:T(8,128)S(1)}, f32[128,8,128]{2,1,0:T(8,128)}, u32[]{:S(2)}) copy-start(f32[128,8,128]{2,1,0:T(8,128)} %add_subtract_fusion.colv_ref) | copy-start | bytes 1572868
  134.0 1.5 copy-start.4
  135.4 51.1 %copy-start.9 = (f32[4,8,128]{2,1,0:T(8,128)S(1)}, f32[4,8,128]{2,1,0:T(8,128)}, u32[]{:S(2)}) copy-start(f32[4,8,128]{2,1,0:T(8,128)} %get-tuple-element.21) | copy-start | bytes 49156

commit v10 on v7

--- a/solution.py
+++ b/solution.py
@@ -361,11 +361,15 @@
         def _():
             a = rows_ref[slot]
             b = cols_ref[slot]
-            block = split_bf16(tiles_ref[s])
-            direct = dot3(split_bf16(colv_ref[b, pl.ds(0, rows_k), :]), block, (((1,), (1,)), ((), ())))
-            rsum_ref[a] += direct
-            mirror = dot3(split_bf16(rowv_ref[a, pl.ds(0, rows_k), :]), block, (((1,), (0,)), ((), ())))
-            csum_ref[b] += mirror
+            high, low = split_bf16(tiles_ref[s])
+            rsum_ref[a] += dot3(
+                split_bf16(colv_ref[b, pl.ds(0, rows_k), :]),
+                jnp.concatenate([high, low], axis=0), (((1,), (1,)), ((), ())),
+            )
+            csum_ref[b] += dot3(
+                split_bf16(rowv_ref[a, pl.ds(0, rows_k), :]),
+                jnp.concatenate([high, low], axis=1), (((1,), (0,)), ((), ())),
+            )
 
 
 def split_bf16(x):
@@ -374,12 +378,12 @@
 
 
 def dot3(left, right, dims):
-    def one(x, y):
-        return lax.dot_general(x, y, dims, preferred_element_type=jnp.float32)
-
     rows = left[0].shape[0]
-    both = one(jnp.concatenate([left[0], left[1]], axis=0), right[0])
-    return both[:rows] + (both[rows:] + one(left[0], right[1]))
+    both = lax.dot_general(
+        jnp.concatenate([left[0], left[1]], axis=0), right, dims, preferred_element_type=jnp.float32
+    )
+    width = both.shape[1] // 2
+    return both[:rows, :width] + (both[rows:, :width] + both[:rows, width:])
 
 
 def slot_products(blocks, rows_here, cols_here, live_count, row_tiles, column_tiles, rows_k):

time: 176 us -> 178 us (1.011)
    pallas_call x2, Pallas kernels: 14.8 us -> 19.8 us  [slot_products(): pl.pallas_call(functools.partial(_slots_kernel, group, rows_k), grid_spec...]
    pallas_call x2, Pallas kernels: 84.1 us -> 80.2 us  [reduce_tiles(): pl.pallas_call(functools.partial(_reduce_kernel, n_row, n_col, forward),...]
where the time goes in v10:
time: 178 us; the launch traced here: 175 us
  Pallas kernels  144 us (81%)
  other arithmetic  13.9 us (8%)
  matrix products  10.1 us (6%)
  local copies, waits for them, and re-layouts  5 us (3%)
    pallas_call x2, Pallas kernels, reduce_tiles(): pl.pallas_call(functools.partial(_reduce_kernel, n_row, n_col, forward),...  80.2 us
    pallas_call x1, Pallas kernels, gather_tiles(): pl.pallas_call(functools.partial(_gather_kernel, n_row, n_col), out_shape...  44.1 us
    pallas_call x2, Pallas kernels, slot_products(): pl.pallas_call(functools.partial(_slots_kernel, group, rows_k), grid_spec...  19.8 us
    dot_general x4, matrix products, tile_dot(): return jnp.einsum('tki,tli->kl', left, right, precision=highest)  7.58 us

profile of v10, /device:TPU:24, one launch (start us, length us, event | category | flops | bytes accessed | tf_op | source)
XLA Modules:
  0.0 174.7 jit_solution(15135014969715188501)
XLA Ops:
  0.6 1.3 bitcast_bitcast_fusion.x_ref
  2.0 44.1 %shard_map.111 = (f32[32,16,128]{2,1,0:T(8,128)}, f32[128,16,128]{2,1,0:T(8,128)}) custom-call(f32[4,16,128]{2,1,0:T(8,128)} %bitcast_bitcast_fusion.x_ref), custom_call_target="tpu_custom_call" | custom-call | tf_op jit(solution)/shard_map/pallas_call | solution.py:92
  46.8 10.1 %shard_map.112 = (f32[32,8,128]{2,1,0:T(8,128)}, f32[128,8,128]{2,1,0:T(8,128)}) custom-call(s32[64]{0:T(128)} %bitcast.147, s32[64]{0:T(128)} %bitcast.149, s32[1]{0:T(128)} %bitcast.122.count_ref, f32[64,128,128]{2,1,0:T(8,128)} %bitcast.124, f32[32,16,128]{2,1,0:T(8,128)} %get-tuple-element.17.rowv_ref, f32[128,16,128]{2,1,0:T(8,128)} %get-tuple-element.18.colv_ref), custom_call_target="tpu_custom_call" | custom-call | tf_op jit(solution)/shard_map/pallas_call | solution.py:415
  56.9 1.3 convolution_bitcast_fusion.2
  58.1 2.3 %convolution_bitcast_fusion.1 = f32[8,8]{0,1:T(8,128)S(1)} fusion(f32[128,8,128]{2,1,0:T(8,128)} %get-tuple-element.20.csum_ref, f32[128,16,128]{2,1,0:T(8,128)S(1)} %copy-done.1), kind=kOutput, calls=%fused_computation.10 | convolution fusion | flops 12582912 | bytes 1048832 | tf_op jit(solution)/shard_map/tki,tli->kl/dot_general | solution.py:435
  61.0 0.7 fusion.36.small_ref
  61.7 0.6 multiply_bitcast_fusion.base_ref
  62.3 44.3 %shard_map.113 = (f32[4,8,128]{2,1,0:T(8,128)}, f32[8,128]{1,0:T(8,128)}, f32[32,8,128]{2,1,0:T(8,128)}, f32[128,8,128]{2,1,0:T(8,128)}) custom-call(f32[4,8,128]{2,1,0:T(8,128)} %multiply_bitcast_fusion.base_ref, f32[32,8,128]{2,1,0:T(8,128)} %get-tuple-element.19.rsum_ref, f32[128,8,128]{2,1,0:T(8,128)} %get-tuple-element.20.csum_ref, ...), custom_call_target="tpu_custom_call" | custom-call | tf_op jit(solution)/shard_map/pallas_call | solution.py:323
  106.7 0.8 slice.154
  107.6 0.7 cholesky.30
  108.3 0.6 compare_reduce_fusion.1
  109.0 0.6 fusion.33
  109.6 0.6 custom-call.16
  110.6 0.4 fusion.51
  111.0 1.2 fusion.50
  112.2 0.8 fusion.52
  113.1 9.8 %shard_map.114 = (f32[32,8,128]{2,1,0:T(8,128)}, f32[128,8,128]{2,1,0:T(8,128)}) custom-call(s32[64]{0:T(128)} %bitcast.148, s32[64]{0:T(128)} %bitcast.150, s32[1]{0:T(128)} %bitcast.123.count_ref, f32[64,128,128]{2,1,0:T(8,128)} %bitcast.125, f32[32,8,128]{2,1,0:T(8,128)} %get-tuple-element.60.rowv_ref, f32[128,8,128]{2,1,0:T(8,128)} %get-tuple-element.59.colv_ref), custom_call_target="tpu_custom_call" | custom-call | tf_op jit(solution)/shard_map/pallas_call | solution.py:415
  122.9 1.4 convolution_bitcast_fusion.4
  124.3 2.6 %fusion.9 = f32[24,8]{0,1:T(8,128)S(1)} fusion(f32[128,8,128]{2,1,0:T(8,128)} %get-tuple-element.26.csum_ref, f32[128,8,128]{2,1,0:T(8,128)S(1)} %get-tuple-element.30, f32[128,8,128]{2,1,0:T(8,128)S(1)} %copy-done.2, f32[128,8,128]{2,1,0:T(8,128)S(1)} %get-tuple-element.29), kind=kOutput, calls=%fused_computation.15 | convolution fusion | flops 38535168 | bytes 2097920 | tf_op jit(solution)/shard_map/tki,tli->kl/dot_general | solution.py:435
  126.9 0.2 convolution_subtract_fusion
  128.1 0.7 fusion.26.small_ref
  128.7 0.6 multiply_bitcast_fusion.1.base_ref
  129.3 35.9 %shard_map.115 = (f32[4,8,128]{2,1,0:T(8,128)}, f32[16,128]{1,0:T(8,128)}) custom-call(f32[4,8,128]{2,1,0:T(8,128)} %multiply_bitcast_fusion.1.base_ref, f32[32,8,128]{2,1,0:T(8,128)} %get-tuple-element.25.rsum_ref, f32[128,8,128]{2,1,0:T(8,128)} %get-tuple-element.26.csum_ref, f32[16,128]{1,0:T(8,128)} %fusion.26.small_ref), custom_call_target="tpu_custom_call" | custom-call | tf_op jit(solution)/shard_map/pallas_call | solution.py:323
  165.2 0.8 fusion.54
  166.2 2.2 %cholesky.64 = f32[24,24]{1,0:T(8,128)S(1)} custom-call(f32[24,24]{1,0:T(8,128)S(1)} %fusion.25), custom_call_target="Cholesky" | custom-call | tf_op jit(solution)/shard_map/jit(cholesky)/cholesky | solution.py:492
  168.4 0.6 compare_reduce_fusion
  169.1 0.6 fusion.19
  169.7 1.8 %custom-call.19 = f32[1,24,24]{1,2,0:T(8,128)S(1)} custom-call(f32[1,24,24]{2,1,0:T(8,128)S(1)} %fusion.19), custom_call_target="InvertDiagBlocksLowerTriangular" | custom-call | tf_op jit(solution)/shard_map/jit(_solve_triangular)/triangular_solve | solution.py:494
  171.8 0.2 convolution_bitcast_fusion
  172.0 0.8 fusion.23
  172.8 0.6 copy.51
  173.4 1.3 copy.52
  (51 shorter events, 2.4 us)
Async XLA Ops:
  0.6 126.8 %copy-start = (f32[8,512]{1,0:T(8,128)S(1)}, f32[8,512]{1,0:T(8,128)}, u32[]{:S(2)}) copy-start(f32[8,512]{1,0:T(8,128)} %param.17) | copy-start | bytes 49156
  46.8 10.1 %copy-start.3 = (f32[32,16,128]{2,1,0:T(8,128)S(1)}, f32[32,16,128]{2,1,0:T(8,128)}, u32[]{:S(2)}) copy-start(f32[32,16,128]{2,1,0:T(8,128)} %get-tuple-element.17.rowv_ref) | copy-start | bytes 786436
  46.8 11.3 %copy-start.1 = (f32[128,16,128]{2,1,0:T(8,128)S(1)}, f32[128,16,128]{2,1,0:T(8,128)}, u32[]{:S(2)}) copy-start(f32[128,16,128]{2,1,0:T(8,128)} %get-tuple-element.18.colv_ref) | copy-start | bytes 3145732
  46.8 13.7 %copy-start.4 = (f32[8,512]{1,0:T(8,128)S(1)}, f32[8,512]{1,0:T(8,128)}, u32[]{:S(2)}) copy-start(f32[8,512]{1,0:T(8,128)} %param.15) | copy-start | bytes 49156
  46.8 13.6 %copy-start.11 = (f32[512]{0:T(512)S(1)}, f32[512]{0:T(512)}, u32[]{:S(2)}) copy-start(f32[512]{0:T(512)} %param.14) | copy-start | bytes 6148
  106.7 4.3 %copy-start.6 = (f32[128,8,128]{2,1,0:T(8,128)S(1)}, f32[128,8,128]{2,1,0:T(8,128)}, u32[]{:S(2)}) copy-start(f32[128,8,128]{2,1,0:T(8,128)} %get-tuple-element.24) | copy-start | bytes 1572868
  111.0 1.3 copy-start.10
  113.1 9.8 %copy-start.5 = (f32[32,8,128]{2,1,0:T(8,128)S(1)}, f32[32,8,128]{2,1,0:T(8,128)}, u32[]{:S(2)}) copy-start(f32[32,8,128]{2,1,0:T(8,128)} %get-tuple-element.60.rowv_ref) | copy-start | bytes 393220
  113.1 11.2 %copy-start.2 = (f32[128,8,128]{2,1,0:T(8,128)S(1)}, f32[128,8,128]{2,1,0:T(8,128)}, u32[]{:S(2)}) copy-start(f32[128,8,128]{2,1,0:T(8,128)} %get-tuple-element.59.colv_ref) | copy-start | bytes 1572868
  122.9 4.0 %copy-start.9 = (f32[4,8,128]{2,1,0:T(8,128)S(1)}, f32[4,8,128]{2,1,0:T(8,128)}, u32[]{:S(2)}) copy-start(f32[4,8,128]{2,1,0:T(8,128)} %get-tuple-element.21) | copy-start | bytes 49156
  122.9 4.2 %copy-start.8 = (f32[8,512]{1,0:T(8,128)S(1)}, f32[8,512]{1,0:T(8,128)}, u32[]{:S(2)}) copy-start(f32[8,512]{1,0:T(8,128)} %param.16) | copy-start | bytes 49156
  127.1 47.6 %copy-start.7 = (f32[8,512]{1,0:T(8,128)}, f32[8,512]{1,0:T(8,128)S(1)}, u32[]{:S(2)}) copy-start(f32[8,512]{1,0:T(8,128)S(1)} %convolution_subtract_fusion) | copy-start | bytes 49156

commit v11 on v10

--- a/solution.py
+++ b/solution.py
@@ -29,7 +29,7 @@
 
 
 def _gather_kernel(n_row, n_col, x_ref, rowv_ref, colv_ref, send_row, recv_row, send_col, recv_col, local_sem):
-    vt = x_ref.shape[0]
+    vt = x_ref.shape[1]
     r = lax.axis_index("row")
     c = lax.axis_index("col")
     _barrier(n_row, n_col, r, c)
@@ -37,7 +37,7 @@
     def row_copy(j, src):
         return pltpu.make_async_remote_copy(
             src_ref=x_ref,
-            dst_ref=rowv_ref.at[pl.ds(src * vt, vt)],
+            dst_ref=rowv_ref.at[:, pl.ds(src * vt, vt)],
             send_sem=send_row.at[j],
             recv_sem=recv_row.at[src],
             device_id=(r, j),
@@ -47,15 +47,15 @@
     def col_copy(i, src):
         return pltpu.make_async_remote_copy(
             src_ref=x_ref,
-            dst_ref=colv_ref.at[pl.ds(src * vt, vt)],
+            dst_ref=colv_ref.at[:, pl.ds(src * vt, vt)],
             send_sem=send_col.at[i],
             recv_sem=recv_col.at[src],
             device_id=(i, c),
             device_id_type=MESH,
         )
 
-    own_row = pltpu.make_async_copy(x_ref, rowv_ref.at[pl.ds(c * vt, vt)], local_sem.at[0])
-    own_col = pltpu.make_async_copy(x_ref, colv_ref.at[pl.ds(r * vt, vt)], local_sem.at[1])
+    own_row = pltpu.make_async_copy(x_ref, rowv_ref.at[:, pl.ds(c * vt, vt)], local_sem.at[0])
+    own_col = pltpu.make_async_copy(x_ref, colv_ref.at[:, pl.ds(r * vt, vt)], local_sem.at[1])
     own_row.start()
     own_col.start()
 
@@ -87,13 +87,13 @@
 
 
 def gather_tiles(x_tiles, n_row, n_col, collective_id):
-    vt, k, t = x_tiles.shape
+    k, vt = x_tiles.shape
     vmem = pl.BlockSpec(memory_space=pltpu.VMEM)
     return pl.pallas_call(
         functools.partial(_gather_kernel, n_row, n_col),
         out_shape=(
-            jax.ShapeDtypeStruct((n_col * vt, k, t), x_tiles.dtype),
-            jax.ShapeDtypeStruct((n_row * vt, k, t), x_tiles.dtype),
+            jax.ShapeDtypeStruct((k, n_col * vt), x_tiles.dtype),
+            jax.ShapeDtypeStruct((k, n_row * vt), x_tiles.dtype),
         ),
         in_specs=[vmem],
         out_specs=(vmem, vmem),
@@ -115,7 +115,7 @@
     (got_row, got_col, got_small_col, mid, got_small_row,
      send_row, recv_row, send_col, recv_col,
      send_small_col, recv_small_col, send_small_row, recv_small_row, local_sem) = rest[:14]
-    vt = base_ref.shape[0]
+    vt = base_ref.shape[1]
     r = lax.axis_index("row")
     c = lax.axis_index("col")
     _barrier(n_row, n_col, r, c)
@@ -142,7 +142,7 @@
 
     def row_copy(j, src):
         return pltpu.make_async_remote_copy(
-            src_ref=rsum_ref.at[pl.ds(j * vt, vt)],
+            src_ref=rsum_ref.at[:, pl.ds(j * vt, vt)],
             dst_ref=got_row.at[src],
             send_sem=send_row.at[j],
             recv_sem=recv_row.at[src],
@@ -152,7 +152,7 @@
 
     def col_copy(i, src):
         return pltpu.make_async_remote_copy(
-            src_ref=csum_ref.at[pl.ds(i * vt, vt)],
+            src_ref=csum_ref.at[:, pl.ds(i * vt, vt)],
             dst_ref=got_col.at[src],
             send_sem=send_col.at[i],
             recv_sem=recv_col.at[src],
@@ -169,8 +169,8 @@
 
     lax.fori_loop(1, n_col, start_small_col, 0)
 
-    own_row = pltpu.make_async_copy(rsum_ref.at[pl.ds(c * vt, vt)], got_row.at[c], local_sem.at[0])
-    own_col = pltpu.make_async_copy(csum_ref.at[pl.ds(r * vt, vt)], got_col.at[r], local_sem.at[1])
+    own_row = pltpu.make_async_copy(rsum_ref.at[:, pl.ds(c * vt, vt)], got_row.at[c], local_sem.at[0])
+    own_col = pltpu.make_async_copy(csum_ref.at[:, pl.ds(r * vt, vt)], got_col.at[r], local_sem.at[1])
     own_row.start()
     own_col.start()
 
@@ -225,7 +225,7 @@
         def fwd_row_copy(j, src):
             return pltpu.make_async_remote_copy(
                 src_ref=out_ref,
-                dst_ref=img_row.at[pl.ds(src * vt, vt)],
+                dst_ref=img_row.at[:, pl.ds(src * vt, vt)],
                 send_sem=send_fr.at[j],
                 recv_sem=recv_fr.at[src],
                 device_id=(r, j),
@@ -235,15 +235,15 @@
         def fwd_col_copy(i, src):
             return pltpu.make_async_remote_copy(
                 src_ref=out_ref,
-                dst_ref=img_col.at[pl.ds(src * vt, vt)],
+                dst_ref=img_col.at[:, pl.ds(src * vt, vt)],
                 send_sem=send_fc.at[i],
                 recv_sem=recv_fc.at[src],
                 device_id=(i, c),
                 device_id_type=MESH,
             )
 
-        own_fr = pltpu.make_async_copy(out_ref, img_row.at[pl.ds(c * vt, vt)], local_sem.at[4])
-        own_fc = pltpu.make_async_copy(out_ref, img_col.at[pl.ds(r * vt, vt)], local_sem.at[5])
+        own_fr = pltpu.make_async_copy(out_ref, img_row.at[:, pl.ds(c * vt, vt)], local_sem.at[4])
+        own_fc = pltpu.make_async_copy(out_ref, img_col.at[:, pl.ds(r * vt, vt)], local_sem.at[5])
         own_fr.start()
         own_fc.start()
 
@@ -301,18 +301,18 @@
 
 
 def reduce_tiles(base_tiles, row_sum, col_sum, small, n_row, n_col, collective_id, forward=False):
-    vt, k, t = base_tiles.shape
+    k, vt = base_tiles.shape
     s = small.shape[0]
     vmem = pl.BlockSpec(memory_space=pltpu.VMEM)
     out_shape = [
-        jax.ShapeDtypeStruct((vt, k, t), base_tiles.dtype),
+        jax.ShapeDtypeStruct((k, vt), base_tiles.dtype),
         jax.ShapeDtypeStruct((s, 128), jnp.float32),
     ]
     extra_sems = []
     if forward:
         out_shape += [
-            jax.ShapeDtypeStruct((n_col * vt, k, t), base_tiles.dtype),
-            jax.ShapeDtypeStruct((n_row * vt, k, t), base_tiles.dtype),
+            jax.ShapeDtypeStruct((k, n_col * vt), base_tiles.dtype),
+            jax.ShapeDtypeStruct((k, n_row * vt), base_tiles.dtype),
         ]
         extra_sems = [
             pltpu.SemaphoreType.DMA((n_col,)),
@@ -326,8 +326,8 @@
         in_specs=[vmem, vmem, vmem, vmem],
         out_specs=tuple(vmem for _ in out_shape),
         scratch_shapes=[
-            pltpu.VMEM((n_col, vt, k, t), jnp.float32),
-            pltpu.VMEM((n_row, vt, k, t), jnp.float32),
+            pltpu.VMEM((n_col, k, vt), jnp.float32),
+            pltpu.VMEM((n_row, k, vt), jnp.float32),
             pltpu.VMEM((n_col, s, 128), jnp.float32),
             pltpu.VMEM((s, 128), jnp.float32),
             pltpu.VMEM((n_row, s, 128), jnp.float32),
@@ -345,7 +345,7 @@
     )(base_tiles, row_sum, col_sum, small)
 
 
-def _slots_kernel(group, rows_k, rows_ref, cols_ref, count_ref, tiles_ref, rowv_ref, colv_ref,
+def _slots_kernel(group, rows_k, tile, rows_ref, cols_ref, count_ref, tiles_ref, rowv_ref, colv_ref,
                   rsum_ref, csum_ref):
     g = pl.program_id(0)
 
@@ -359,15 +359,15 @@
 
         @pl.when(slot < count_ref[0])
         def _():
-            a = rows_ref[slot]
-            b = cols_ref[slot]
+            a = pl.multiple_of(rows_ref[slot] * tile, tile)
+            b = pl.multiple_of(cols_ref[slot] * tile, tile)
             high, low = split_bf16(tiles_ref[s])
-            rsum_ref[a] += dot3(
-                split_bf16(colv_ref[b, pl.ds(0, rows_k), :]),
+            rsum_ref[:, pl.ds(a, tile)] += dot3(
+                split_bf16(colv_ref[pl.ds(0, rows_k), pl.ds(b, tile)]),
                 jnp.concatenate([high, low], axis=0), (((1,), (1,)), ((), ())),
             )
-            csum_ref[b] += dot3(
-                split_bf16(rowv_ref[a, pl.ds(0, rows_k), :]),
+            csum_ref[:, pl.ds(b, tile)] += dot3(
+                split_bf16(rowv_ref[pl.ds(0, rows_k), pl.ds(a, tile)]),
                 jnp.concatenate([high, low], axis=1), (((1,), (0,)), ((), ())),
             )
 
@@ -388,7 +388,7 @@
 
 def slot_products(blocks, rows_here, cols_here, live_count, row_tiles, column_tiles, rows_k):
     slot_count, tile, _ = blocks.shape
-    sums_shape = lambda v: (v.shape[0], rows_k, v.shape[2])
+    sums_shape = lambda v: (rows_k, v.shape[1])
     group = group_width
     groups = slot_count // group
 
@@ -397,7 +397,7 @@
         return (jnp.minimum(g, last), 0, 0)
 
     def whole(g, rows, cols, count):
-        return (0, 0, 0)
+        return (0, 0)
 
     grid_spec = pltpu.PrefetchScalarGridSpec(
         num_scalar_prefetch=3,
@@ -413,7 +413,7 @@
         ],
     )
     return pl.pallas_call(
-        functools.partial(_slots_kernel, group, rows_k),
+        functools.partial(_slots_kernel, group, rows_k, tile),
         grid_spec=grid_spec,
         out_shape=(
             jax.ShapeDtypeStruct(sums_shape(row_tiles), jnp.float32),
@@ -423,16 +423,8 @@
     )(rows_here, cols_here, live_count.reshape(1), blocks, row_tiles, column_tiles)
 
 
-def to_tiles(vectors, tile):
-    return vectors.reshape(vectors.shape[0], -1, tile).transpose(1, 0, 2)
-
-
-def from_tiles(tiles):
-    return tiles.transpose(1, 0, 2).reshape(tiles.shape[1], -1)
-
-
 def tile_dot(left, right):
-    return jnp.einsum("tki,tli->kl", left, right, precision=highest)
+    return jnp.dot(left, right.T, precision=highest)
 
 
 def dot_rows(left, right):
@@ -448,17 +440,17 @@
     cols_here = tile_col.reshape(slot_count)
     live_count = counts.reshape(())
 
-    row_cp, col_cp = gather_tiles(to_tiles(jnp.concatenate([current, previous], 0), tile), n_row, n_col, 0)
+    row_cp, col_cp = gather_tiles(jnp.concatenate([current, previous], 0), n_row, n_col, 0)
     row_sum, col_sum = slot_products(blocks, rows_here, cols_here, live_count, row_cp, col_cp, k)
-    row_cur, col_cur = row_cp[:, :k], col_cp[:, :k]
+    row_cur, col_cur = row_cp[:k], col_cp[:k]
     scaled = diagonal[None, :] * current
     small_gram = dot_rows(current, current)
     proj_part = dot_rows(current, scaled) + tile_dot(row_cur, row_sum) + tile_dot(col_cur, col_sum)
     image_tiles, small, row_img, col_img = reduce_tiles(
-        to_tiles(scaled, tile), row_sum, col_sum, pack_small((small_gram, proj_part)), n_row, n_col, 1,
+        scaled, row_sum, col_sum, pack_small((small_gram, proj_part)), n_row, n_col, 1,
         forward=True,
     )
-    image = from_tiles(image_tiles)
+    image = image_tiles
     small_gram, small_proj = unpack_small(small, (small_gram, proj_part))
 
     factor = jnp.linalg.cholesky(small_gram)
@@ -466,15 +458,15 @@
     residual = image - jnp.dot(ritz_matrix.T, current, precision=highest)
 
     def residual_of(img_tiles, cur_tiles):
-        fitted = sum(ritz_matrix[l][None, :, None] * cur_tiles[:, l:l + 1, :] for l in range(k))
+        fitted = sum(ritz_matrix[l][:, None] * cur_tiles[l:l + 1, :] for l in range(k))
         return img_tiles - fitted
 
     row_res = residual_of(row_img, row_cur)
     col_res = residual_of(col_img, col_cur)
     row_sum, col_sum = slot_products(blocks, rows_here, cols_here, live_count, row_res, col_res, k)
     search_basis = jnp.concatenate([current, residual, previous], 0)
-    row_basis = jnp.concatenate([row_cur, row_res, row_cp[:, k:]], 1)
-    col_basis = jnp.concatenate([col_cur, col_res, col_cp[:, k:]], 1)
+    row_basis = jnp.concatenate([row_cur, row_res, row_cp[k:]], 0)
+    col_basis = jnp.concatenate([col_cur, col_res, col_cp[k:]], 0)
     scaled = diagonal[None, :] * residual
     correlation = dot_rows(search_basis, search_basis)
     residual_part = (
@@ -484,9 +476,9 @@
         [dot_rows(search_basis, image), residual_part, dot_rows(search_basis, previous_image)], 1
     )
     image_tiles, small = reduce_tiles(
-        to_tiles(scaled, tile), row_sum, col_sum, pack_small((correlation, mixed_part)), n_row, n_col, 2
-    )
-    residual_image = from_tiles(image_tiles)
+        scaled, row_sum, col_sum, pack_small((correlation, mixed_part)), n_row, n_col, 2
+    )
+    residual_image = image_tiles
     correlation, mixed_terms = unpack_small(small, (correlation, mixed_part))
     pencil = 0.5 * (mixed_terms + mixed_terms.T)
     lower_factor = jnp.linalg.cholesky(correlation)

time: 178 us -> 174 us (0.978)
  Pallas kernels: 144 us -> 142 us
    pallas_call x2, Pallas kernels: 19.8 us -> 14.4 us  [slot_products(): pl.pallas_call(functools.partial(_slots_kernel, group, rows_k, tile), gri...]
    pallas_call x2, Pallas kernels: 80.2 us -> 83.1 us  [reduce_tiles(): pl.pallas_call(functools.partial(_reduce_kernel, n_row, n_col, forward),...]
    transpose x3 -> x0, other arithmetic: 2.56 us -> none  [to_tiles(): return vectors.reshape(vectors.shape[0], -1, tile).transpose(1, 0, 2)]
where the time goes in v11:
time: 174 us; the launch traced here: 172 us
  Pallas kernels  142 us (82%)
  other arithmetic  13.3 us (8%)
  matrix products  10.1 us (6%)
  local copies, waits for them, and re-layouts  5.01 us (3%)
    pallas_call x2, Pallas kernels, reduce_tiles(): pl.pallas_call(functools.partial(_reduce_kernel, n_row, n_col, forward),...  83.1 us
    pallas_call x1, Pallas kernels, gather_tiles(): pl.pallas_call(functools.partial(_gather_kernel, n_row, n_col), out_shape...  44.1 us
    pallas_call x2, Pallas kernels, slot_products(): pl.pallas_call(functools.partial(_slots_kernel, group, rows_k, tile), gri...  14.4 us
    dot_general x4, matrix products, tile_dot(): return jnp.dot(left, right.T, precision=highest)  7.66 us

profile of v11, /device:TPU:24, one launch (start us, length us, event | category | flops | bytes accessed | tf_op | source)
XLA Modules:
  0.0 171.7 jit_solution(4508510271707144249)
XLA Ops:
  0.6 1.4 pad_maximum_fusion.1.x_ref
  2.0 44.1 %shard_map.111 = (f32[16,4096]{1,0:T(8,128)}, f32[16,16384]{1,0:T(8,128)}) custom-call(f32[16,512]{1,0:T(8,128)} %pad_maximum_fusion.1.x_ref), custom_call_target="tpu_custom_call" | custom-call | tf_op jit(solution)/shard_map/pallas_call | solution.py:92
  46.8 7.4 %shard_map.112 = (f32[8,4096]{1,0:T(8,128)}, f32[8,16384]{1,0:T(8,128)}) custom-call(s32[64]{0:T(128)} %bitcast.111, s32[64]{0:T(128)} %bitcast.113, s32[1]{0:T(128)} %bitcast.90.count_ref, f32[64,128,128]{2,1,0:T(8,128)} %bitcast.92, f32[16,4096]{1,0:T(8,128)} %get-tuple-element.17.rowv_ref, f32[16,16384]{1,0:T(8,128)} %get-tuple-element.18.colv_ref), custom_call_target="tpu_custom_call" | custom-call | tf_op jit(solution)/shard_map/pallas_call | solution.py:415
  54.3 1.3 convolution_add_fusion.2
  55.6 2.3 %convolution_add_fusion.1 = f32[8,8]{0,1:T(8,128)S(1)} fusion(f32[8,8]{0,1:T(8,128)S(1)} %convolution_add_fusion.2, f32[8,16384]{1,0:T(8,128)} %get-tuple-element.20.csum_ref, f32[16,16384]{1,0:T(8,128)S(1)} %copy-done.1), kind=kOutput, calls=%fused_computation.10 | convolution fusion | flops 12582976 | bytes 1052928 | tf_op jit(solution)/shard_map/dot_general | solution.py:427
  58.4 0.7 fusion.28.small_ref
  59.0 0.6 broadcast_multiply_fusion.1.base_ref
  59.6 45.9 %shard_map.113 = (f32[8,512]{1,0:T(8,128)}, f32[8,128]{1,0:T(8,128)}, f32[8,4096]{1,0:T(8,128)}, f32[8,16384]{1,0:T(8,128)}) custom-call(f32[8,512]{1,0:T(8,128)} %broadcast_multiply_fusion.1.base_ref, f32[8,4096]{1,0:T(8,128)} %get-tuple-element.19.rsum_ref, f32[8,16384]{1,0:T(8,128)} %get-tuple-element.20.csum_ref, f32[8,128]{1,0:T(8,128)} %fusion.28.small_ref), custom_call_target="tpu_custom_call" | custom-call | tf_op jit(solution)/shard_map/pallas_call | solution.py:323
  105.6 0.8 slice.154
  106.5 0.7 cholesky.30
  107.3 0.6 compare_reduce_fusion.1
  107.9 0.6 fusion.25
  108.6 0.6 custom-call.16
  109.2 0.2 fusion.26
  109.6 0.4 fusion.43
  109.9 1.2 fusion.42
  111.2 0.8 fusion.44
  112.0 7.1 %shard_map.114 = (f32[8,4096]{1,0:T(8,128)}, f32[8,16384]{1,0:T(8,128)}) custom-call(s32[64]{0:T(128)} %bitcast.112, s32[64]{0:T(128)} %bitcast.114, s32[1]{0:T(128)} %bitcast.91.count_ref, f32[64,128,128]{2,1,0:T(8,128)} %bitcast.93, f32[8,4096]{1,0:T(8,128)} %get-tuple-element.62.rowv_ref, f32[8,16384]{1,0:T(8,128)} %get-tuple-element.61.colv_ref), custom_call_target="tpu_custom_call" | custom-call | tf_op jit(solution)/shard_map/pallas_call | solution.py:415
  119.1 1.4 fusion.7
  120.5 2.6 %fusion = f32[24,8]{0,1:T(8,128)S(1)} fusion(f32[8,16384]{1,0:T(8,128)} %get-tuple-element.26.csum_ref, f32[8,16384]{1,0:T(8,128)S(1)} %get-tuple-element.30, f32[8,16384]{1,0:T(8,128)S(1)} %copy-done.2, f32[8,16384]{1,0:T(8,128)S(1)} %get-tuple-element.29), kind=kOutput, calls=%fused_computation | convolution fusion | flops 38535168 | bytes 2097920 | tf_op jit(solution)/shard_map/dot_general | solution.py:427
  123.1 0.2 broadcast_multiply_fusion
  124.3 0.7 fusion.20.small_ref
  125.0 37.1 %shard_map.115 = (f32[8,512]{1,0:T(8,128)}, f32[16,128]{1,0:T(8,128)}) custom-call(f32[8,512]{1,0:T(8,128)} %copy-done.9, f32[8,4096]{1,0:T(8,128)} %get-tuple-element.25.rsum_ref, f32[8,16384]{1,0:T(8,128)} %get-tuple-element.26.csum_ref, f32[16,128]{1,0:T(8,128)} %fusion.20.small_ref), custom_call_target="tpu_custom_call" | custom-call | tf_op jit(solution)/shard_map/pallas_call | solution.py:323
  162.1 0.8 fusion.46
  163.1 2.2 %cholesky.64 = f32[24,24]{1,0:T(8,128)S(1)} custom-call(f32[24,24]{1,0:T(8,128)S(1)} %fusion.19), custom_call_target="Cholesky" | custom-call | tf_op jit(solution)/shard_map/jit(cholesky)/cholesky | solution.py:484
  165.4 0.6 compare_reduce_fusion
  166.0 0.6 fusion.13
  166.7 1.8 %custom-call.19 = f32[1,24,24]{1,2,0:T(8,128)S(1)} custom-call(f32[1,24,24]{2,1,0:T(8,128)S(1)} %fusion.13), custom_call_target="InvertDiagBlocksLowerTriangular" | custom-call | tf_op jit(solution)/shard_map/jit(_solve_triangular)/triangular_solve | solution.py:486
  168.7 0.2 convolution_bitcast_fusion
  168.9 0.8 fusion.17
  169.7 0.6 copy.34
  170.3 1.3 copy.35
  (52 shorter events, 2.2 us)
Async XLA Ops:
  0.6 123.1 %copy-start = (f32[8,512]{1,0:T(8,128)S(1)}, f32[8,512]{1,0:T(8,128)}, u32[]{:S(2)}) copy-start(f32[8,512]{1,0:T(8,128)} %param.17) | copy-start | bytes 49156
  46.8 7.4 %copy-start.4 = (f32[8,512]{1,0:T(8,128)S(1)}, f32[8,512]{1,0:T(8,128)}, u32[]{:S(2)}) copy-start(f32[8,512]{1,0:T(8,128)} %param.15) | copy-start | bytes 49156
  46.8 7.4 %copy-start.12 = (f32[512]{0:T(512)S(1)}, f32[512]{0:T(512)}, u32[]{:S(2)}) copy-start(f32[512]{0:T(512)} %param.14) | copy-start | bytes 6148
  46.8 7.5 %copy-start.3 = (f32[16,4096]{1,0:T(8,128)S(1)}, f32[16,4096]{1,0:T(8,128)}, u32[]{:S(2)}) copy-start(f32[16,4096]{1,0:T(8,128)} %get-tuple-element.17.rowv_ref) | copy-start | bytes 786436
  46.8 8.8 %copy-start.1 = (f32[16,16384]{1,0:T(8,128)S(1)}, f32[16,16384]{1,0:T(8,128)}, u32[]{:S(2)}) copy-start(f32[16,16384]{1,0:T(8,128)} %get-tuple-element.18.colv_ref) | copy-start | bytes 3145732
  105.6 4.3 %copy-start.6 = (f32[8,16384]{1,0:T(8,128)S(1)}, f32[8,16384]{1,0:T(8,128)}, u32[]{:S(2)}) copy-start(f32[8,16384]{1,0:T(8,128)} %get-tuple-element.24) | copy-start | bytes 1572868
  109.9 1.3 copy-start.11
  112.0 7.1 %copy-start.5 = (f32[8,4096]{1,0:T(8,128)S(1)}, f32[8,4096]{1,0:T(8,128)}, u32[]{:S(2)}) copy-start(f32[8,4096]{1,0:T(8,128)} %get-tuple-element.62.rowv_ref) | copy-start | bytes 393220
  112.0 8.5 %copy-start.2 = (f32[8,16384]{1,0:T(8,128)S(1)}, f32[8,16384]{1,0:T(8,128)}, u32[]{:S(2)}) copy-start(f32[8,16384]{1,0:T(8,128)} %get-tuple-element.61.colv_ref) | copy-start | bytes 1572868
  119.1 4.0 %copy-start.10 = (f32[8,512]{1,0:T(8,128)S(1)}, f32[8,512]{1,0:T(8,128)}, u32[]{:S(2)}) copy-start(f32[8,512]{1,0:T(8,128)} %get-tuple-element.67) | copy-start | bytes 49156
  119.1 4.3 %copy-start.7 = (f32[8,512]{1,0:T(8,128)S(1)}, f32[8,512]{1,0:T(8,128)}, u32[]{:S(2)}) copy-start(f32[8,512]{1,0:T(8,128)} %param.16) | copy-start | bytes 49156
  123.3 1.7 copy-start.9
  123.3 48.3 %copy-start.8 = (f32[8,512]{1,0:T(8,128)}, f32[8,512]{1,0:T(8,128)S(1)}, u32[]{:S(2)}) copy-start(f32[8,512]{1,0:T(8,128)S(1)} %get-tuple-element.68) | copy-start | bytes 49156

commit v12 on v11

--- a/solution.py
+++ b/solution.py
@@ -169,6 +169,25 @@
 
     lax.fori_loop(1, n_col, start_small_col, 0)
 
+
+    def wait_small_col(k, carry):
+        small_col_copy(lax.rem(c + k, n_col), c).wait_send()
+        small_col_copy(c, lax.rem(c + n_col - k, n_col)).wait_recv()
+        return carry
+
+    lax.fori_loop(1, n_col, wait_small_col, 0)
+    own_small.wait()
+    mid[...] = jnp.sum(got_small_col[...], axis=0)
+
+    own_mid = pltpu.make_async_copy(mid, got_small_row.at[r], local_sem.at[3])
+    own_mid.start()
+
+    def start_small_row(k, carry):
+        small_row_copy(lax.rem(r + k, n_row), r).start()
+        return carry
+
+    lax.fori_loop(1, n_row, start_small_row, 0)
+
     own_row = pltpu.make_async_copy(rsum_ref.at[:, pl.ds(c * vt, vt)], got_row.at[c], local_sem.at[0])
     own_col = pltpu.make_async_copy(csum_ref.at[:, pl.ds(r * vt, vt)], got_col.at[r], local_sem.at[1])
     own_row.start()
@@ -184,24 +203,6 @@
 
     lax.fori_loop(1, n_row, start_row, 0)
     lax.fori_loop(1, n_col, start_col, 0)
-
-    def wait_small_col(k, carry):
-        small_col_copy(lax.rem(c + k, n_col), c).wait_send()
-        small_col_copy(c, lax.rem(c + n_col - k, n_col)).wait_recv()
-        return carry
-
-    lax.fori_loop(1, n_col, wait_small_col, 0)
-    own_small.wait()
-    mid[...] = jnp.sum(got_small_col[...], axis=0)
-
-    own_mid = pltpu.make_async_copy(mid, got_small_row.at[r], local_sem.at[3])
-    own_mid.start()
-
-    def start_small_row(k, carry):
-        small_row_copy(lax.rem(r + k, n_row), r).start()
-        return carry
-
-    lax.fori_loop(1, n_row, start_small_row, 0)
 
     def wait_col(k, carry):
         row_copy(lax.rem(c + k, n_col), c).wait_send()

time: 174 us -> 183 us (1.052)
  Pallas kernels: 142 us -> 151 us
    pallas_call x2, Pallas kernels: 83.1 us -> 93.1 us  [reduce_tiles(): pl.pallas_call(functools.partial(_reduce_kernel, n_row, n_col, forward),...]
where the time goes in v12:
time: 183 us; the launch traced here: 181 us
  Pallas kernels  151 us (83%)
  other arithmetic  13.3 us (7%)
  matrix products  10.1 us (6%)
  local copies, waits for them, and re-layouts  5.02 us (3%)
    pallas_call x2, Pallas kernels, reduce_tiles(): pl.pallas_call(functools.partial(_reduce_kernel, n_row, n_col, forward),...  93.1 us
    pallas_call x1, Pallas kernels, gather_tiles(): pl.pallas_call(functools.partial(_gather_kernel, n_row, n_col), out_shape...  44.1 us
    pallas_call x2, Pallas kernels, slot_products(): pl.pallas_call(functools.partial(_slots_kernel, group, rows_k, tile), gri...  13.5 us
    dot_general x4, matrix products, tile_dot(): return jnp.dot(left, right.T, precision=highest)  7.66 us

profile of v12, /device:TPU:24, one launch (start us, length us, event | category | flops | bytes accessed | tf_op | source)
XLA Modules:
  0.0 180.8 jit_solution(12130359506551847691)
XLA Ops:
  0.6 1.4 pad_maximum_fusion.1.x_ref
  2.0 44.1 %shard_map.111 = (f32[16,4096]{1,0:T(8,128)}, f32[16,16384]{1,0:T(8,128)}) custom-call(f32[16,512]{1,0:T(8,128)} %pad_maximum_fusion.1.x_ref), custom_call_target="tpu_custom_call" | custom-call | tf_op jit(solution)/shard_map/pallas_call | solution.py:92
  46.8 6.9 %shard_map.112 = (f32[8,4096]{1,0:T(8,128)}, f32[8,16384]{1,0:T(8,128)}) custom-call(s32[64]{0:T(128)} %bitcast.111, s32[64]{0:T(128)} %bitcast.113, s32[1]{0:T(128)} %bitcast.90.count_ref, f32[64,128,128]{2,1,0:T(8,128)} %bitcast.92, f32[16,4096]{1,0:T(8,128)} %get-tuple-element.17.rowv_ref, f32[16,16384]{1,0:T(8,128)} %get-tuple-element.18.colv_ref), custom_call_target="tpu_custom_call" | custom-call | tf_op jit(solution)/shard_map/pallas_call | solution.py:416
  53.9 1.3 convolution_add_fusion.2
  55.2 2.3 %convolution_add_fusion.1 = f32[8,8]{0,1:T(8,128)S(1)} fusion(f32[8,8]{0,1:T(8,128)S(1)} %convolution_add_fusion.2, f32[8,16384]{1,0:T(8,128)} %get-tuple-element.20.csum_ref, f32[16,16384]{1,0:T(8,128)S(1)} %copy-done.1), kind=kOutput, calls=%fused_computation.10 | convolution fusion | flops 12582976 | bytes 1052928 | tf_op jit(solution)/shard_map/dot_general | solution.py:428
  57.9 0.7 fusion.28.small_ref
  58.6 0.6 broadcast_multiply_fusion.1.base_ref
  59.2 52.3 %shard_map.113 = (f32[8,512]{1,0:T(8,128)}, f32[8,128]{1,0:T(8,128)}, f32[8,4096]{1,0:T(8,128)}, f32[8,16384]{1,0:T(8,128)}) custom-call(f32[8,512]{1,0:T(8,128)} %broadcast_multiply_fusion.1.base_ref, f32[8,4096]{1,0:T(8,128)} %get-tuple-element.19.rsum_ref, f32[8,16384]{1,0:T(8,128)} %get-tuple-element.20.csum_ref, f32[8,128]{1,0:T(8,128)} %fusion.28.small_ref), custom_call_target="tpu_custom_call" | custom-call | tf_op jit(solution)/shard_map/pallas_call | solution.py:324
  111.6 0.8 slice.154
  112.5 0.7 cholesky.30
  113.2 0.6 compare_reduce_fusion.1
  113.9 0.6 fusion.25
  114.5 0.6 custom-call.16
  115.2 0.2 fusion.26
  115.5 0.4 fusion.43
  115.9 1.2 fusion.42
  117.2 0.8 fusion.44
  118.0 6.6 %shard_map.114 = (f32[8,4096]{1,0:T(8,128)}, f32[8,16384]{1,0:T(8,128)}) custom-call(s32[64]{0:T(128)} %bitcast.112, s32[64]{0:T(128)} %bitcast.114, s32[1]{0:T(128)} %bitcast.91.count_ref, f32[64,128,128]{2,1,0:T(8,128)} %bitcast.93, f32[8,4096]{1,0:T(8,128)} %get-tuple-element.62.rowv_ref, f32[8,16384]{1,0:T(8,128)} %get-tuple-element.61.colv_ref), custom_call_target="tpu_custom_call" | custom-call | tf_op jit(solution)/shard_map/pallas_call | solution.py:416
  124.6 1.4 fusion.7
  126.0 2.6 %fusion = f32[24,8]{0,1:T(8,128)S(1)} fusion(f32[8,16384]{1,0:T(8,128)} %get-tuple-element.26.csum_ref, f32[8,16384]{1,0:T(8,128)S(1)} %get-tuple-element.30, f32[8,16384]{1,0:T(8,128)S(1)} %copy-done.2, f32[8,16384]{1,0:T(8,128)S(1)} %get-tuple-element.29), kind=kOutput, calls=%fused_computation | convolution fusion | flops 38535168 | bytes 2097920 | tf_op jit(solution)/shard_map/dot_general | solution.py:428
  128.6 0.2 broadcast_multiply_fusion
  129.8 0.7 fusion.20.small_ref
  130.5 40.8 %shard_map.115 = (f32[8,512]{1,0:T(8,128)}, f32[16,128]{1,0:T(8,128)}) custom-call(f32[8,512]{1,0:T(8,128)} %copy-done.9, f32[8,4096]{1,0:T(8,128)} %get-tuple-element.25.rsum_ref, f32[8,16384]{1,0:T(8,128)} %get-tuple-element.26.csum_ref, f32[16,128]{1,0:T(8,128)} %fusion.20.small_ref), custom_call_target="tpu_custom_call" | custom-call | tf_op jit(solution)/shard_map/pallas_call | solution.py:324
  171.3 0.8 fusion.46
  172.3 2.2 %cholesky.64 = f32[24,24]{1,0:T(8,128)S(1)} custom-call(f32[24,24]{1,0:T(8,128)S(1)} %fusion.19), custom_call_target="Cholesky" | custom-call | tf_op jit(solution)/shard_map/jit(cholesky)/cholesky | solution.py:485
  174.5 0.6 compare_reduce_fusion
  175.2 0.6 fusion.13
  175.8 1.8 %custom-call.19 = f32[1,24,24]{1,2,0:T(8,128)S(1)} custom-call(f32[1,24,24]{2,1,0:T(8,128)S(1)} %fusion.13), custom_call_target="InvertDiagBlocksLowerTriangular" | custom-call | tf_op jit(solution)/shard_map/jit(_solve_triangular)/triangular_solve | solution.py:487
  177.8 0.2 convolution_bitcast_fusion
  178.0 0.8 fusion.17
  178.9 0.6 copy.34
  179.5 1.3 copy.35
  (52 shorter events, 2.2 us)
Async XLA Ops:
  0.6 128.6 %copy-start = (f32[8,512]{1,0:T(8,128)S(1)}, f32[8,512]{1,0:T(8,128)}, u32[]{:S(2)}) copy-start(f32[8,512]{1,0:T(8,128)} %param.17) | copy-start | bytes 49156
  46.8 7.0 %copy-start.4 = (f32[8,512]{1,0:T(8,128)S(1)}, f32[8,512]{1,0:T(8,128)}, u32[]{:S(2)}) copy-start(f32[8,512]{1,0:T(8,128)} %param.15) | copy-start | bytes 49156
  46.8 6.9 %copy-start.12 = (f32[512]{0:T(512)S(1)}, f32[512]{0:T(512)}, u32[]{:S(2)}) copy-start(f32[512]{0:T(512)} %param.14) | copy-start | bytes 6148
  46.8 7.1 %copy-start.3 = (f32[16,4096]{1,0:T(8,128)S(1)}, f32[16,4096]{1,0:T(8,128)}, u32[]{:S(2)}) copy-start(f32[16,4096]{1,0:T(8,128)} %get-tuple-element.17.rowv_ref) | copy-start | bytes 786436
  46.8 8.4 %copy-start.1 = (f32[16,16384]{1,0:T(8,128)S(1)}, f32[16,16384]{1,0:T(8,128)}, u32[]{:S(2)}) copy-start(f32[16,16384]{1,0:T(8,128)} %get-tuple-element.18.colv_ref) | copy-start | bytes 3145732
  111.6 4.3 %copy-start.6 = (f32[8,16384]{1,0:T(8,128)S(1)}, f32[8,16384]{1,0:T(8,128)}, u32[]{:S(2)}) copy-start(f32[8,16384]{1,0:T(8,128)} %get-tuple-element.24) | copy-start | bytes 1572868
  115.9 1.3 copy-start.11
  118.0 6.6 %copy-start.5 = (f32[8,4096]{1,0:T(8,128)S(1)}, f32[8,4096]{1,0:T(8,128)}, u32[]{:S(2)}) copy-start(f32[8,4096]{1,0:T(8,128)} %get-tuple-element.62.rowv_ref) | copy-start | bytes 393220
  118.0 8.0 %copy-start.2 = (f32[8,16384]{1,0:T(8,128)S(1)}, f32[8,16384]{1,0:T(8,128)}, u32[]{:S(2)}) copy-start(f32[8,16384]{1,0:T(8,128)} %get-tuple-element.61.colv_ref) | copy-start | bytes 1572868
  124.6 4.0 %copy-start.10 = (f32[8,512]{1,0:T(8,128)S(1)}, f32[8,512]{1,0:T(8,128)}, u32[]{:S(2)}) copy-start(f32[8,512]{1,0:T(8,128)} %get-tuple-element.67) | copy-start | bytes 49156
  124.6 4.3 %copy-start.7 = (f32[8,512]{1,0:T(8,128)S(1)}, f32[8,512]{1,0:T(8,128)}, u32[]{:S(2)}) copy-start(f32[8,512]{1,0:T(8,128)} %param.16) | copy-start | bytes 49156
  128.9 1.7 copy-start.9
  128.9 51.9 %copy-start.8 = (f32[8,512]{1,0:T(8,128)}, f32[8,512]{1,0:T(8,128)S(1)}, u32[]{:S(2)}) copy-start(f32[8,512]{1,0:T(8,128)S(1)} %get-tuple-element.68) | copy-start | bytes 49156

commit v13 on v11

--- a/solution.py
+++ b/solution.py
@@ -362,10 +362,14 @@
             a = pl.multiple_of(rows_ref[slot] * tile, tile)
             b = pl.multiple_of(cols_ref[slot] * tile, tile)
             high, low = split_bf16(tiles_ref[s])
-            rsum_ref[:, pl.ds(a, tile)] += dot3(
-                split_bf16(colv_ref[pl.ds(0, rows_k), pl.ds(b, tile)]),
-                jnp.concatenate([high, low], axis=0), (((1,), (1,)), ((), ())),
+            col_high, col_low = split_bf16(colv_ref[pl.ds(0, rows_k), pl.ds(b, tile)].T)
+            both = jnp.dot(
+                jnp.concatenate([high, low], axis=0), jnp.concatenate([col_high, col_low], axis=1),
+                preferred_element_type=jnp.float32,
             )
+            rsum_ref[:, pl.ds(a, tile)] += (
+                both[:tile, :rows_k] + (both[:tile, rows_k:] + both[tile:, :rows_k])
+            ).T
             csum_ref[:, pl.ds(b, tile)] += dot3(
                 split_bf16(rowv_ref[pl.ds(0, rows_k), pl.ds(a, tile)]),
                 jnp.concatenate([high, low], axis=1), (((1,), (0,)), ((), ())),

time: 174 us -> 215 us (1.24)
  Pallas kernels: 142 us -> 183 us
    pallas_call x2, Pallas kernels: 14.4 us -> 47.9 us  [slot_products(): pl.pallas_call(functools.partial(_slots_kernel, group, rows_k, tile), gri...]
    pallas_call x2, Pallas kernels: 83.1 us -> 91 us  [reduce_tiles(): pl.pallas_call(functools.partial(_reduce_kernel, n_row, n_col, forward),...]
where the time goes in v13:
time: 215 us; the launch traced here: 213 us
  Pallas kernels  183 us (85%)
  other arithmetic  13.3 us (6%)
  matrix products  10.1 us (5%)
  local copies, waits for them, and re-layouts  5.02 us (2%)
    pallas_call x2, Pallas kernels, reduce_tiles(): pl.pallas_call(functools.partial(_reduce_kernel, n_row, n_col, forward),...  91 us
    pallas_call x2, Pallas kernels, slot_products(): pl.pallas_call(functools.partial(_slots_kernel, group, rows_k, tile), gri...  47.9 us
    pallas_call x1, Pallas kernels, gather_tiles(): pl.pallas_call(functools.partial(_gather_kernel, n_row, n_col), out_shape...  44.1 us
    dot_general x4, matrix products, tile_dot(): return jnp.dot(left, right.T, precision=highest)  7.66 us

profile of v13, /device:TPU:24, one launch (start us, length us, event | category | flops | bytes accessed | tf_op | source)
XLA Modules:
  0.0 213.1 jit_solution(11951359776648576207)
XLA Ops:
  0.6 1.4 pad_maximum_fusion.1.x_ref
  2.0 44.1 %shard_map.111 = (f32[16,4096]{1,0:T(8,128)}, f32[16,16384]{1,0:T(8,128)}) custom-call(f32[16,512]{1,0:T(8,128)} %pad_maximum_fusion.1.x_ref), custom_call_target="tpu_custom_call" | custom-call | tf_op jit(solution)/shard_map/pallas_call | solution.py:92
  46.8 24.1 %shard_map.112 = (f32[8,4096]{1,0:T(8,128)}, f32[8,16384]{1,0:T(8,128)}) custom-call(s32[64]{0:T(128)} %bitcast.111, s32[64]{0:T(128)} %bitcast.113, s32[1]{0:T(128)} %bitcast.90.count_ref, f32[64,128,128]{2,1,0:T(8,128)} %bitcast.92, f32[16,4096]{1,0:T(8,128)} %get-tuple-element.17.rowv_ref, f32[16,16384]{1,0:T(8,128)} %get-tuple-element.18.colv_ref), custom_call_target="tpu_custom_call" | custom-call | tf_op jit(solution)/shard_map/pallas_call | solution.py:419
  71.1 1.3 convolution_add_fusion.2
  72.4 2.3 %convolution_add_fusion.1 = f32[8,8]{0,1:T(8,128)S(1)} fusion(f32[8,8]{0,1:T(8,128)S(1)} %convolution_add_fusion.2, f32[8,16384]{1,0:T(8,128)} %get-tuple-element.20.csum_ref, f32[16,16384]{1,0:T(8,128)S(1)} %copy-done.1), kind=kOutput, calls=%fused_computation.10 | convolution fusion | flops 12582976 | bytes 1052928 | tf_op jit(solution)/shard_map/dot_general | solution.py:431
  75.1 0.7 fusion.28.small_ref
  75.8 0.6 broadcast_multiply_fusion.1.base_ref
  76.4 50.1 %shard_map.113 = (f32[8,512]{1,0:T(8,128)}, f32[8,128]{1,0:T(8,128)}, f32[8,4096]{1,0:T(8,128)}, f32[8,16384]{1,0:T(8,128)}) custom-call(f32[8,512]{1,0:T(8,128)} %broadcast_multiply_fusion.1.base_ref, f32[8,4096]{1,0:T(8,128)} %get-tuple-element.19.rsum_ref, f32[8,16384]{1,0:T(8,128)} %get-tuple-element.20.csum_ref, f32[8,128]{1,0:T(8,128)} %fusion.28.small_ref), custom_call_target="tpu_custom_call" | custom-call | tf_op jit(solution)/shard_map/pallas_call | solution.py:323
  126.5 0.8 slice.154
  127.4 0.7 cholesky.30
  128.2 0.6 compare_reduce_fusion.1
  128.8 0.6 fusion.25
  129.5 0.6 custom-call.16
  130.1 0.2 fusion.26
  130.5 0.4 fusion.43
  130.9 1.2 fusion.42
  132.1 0.8 fusion.44
  132.9 23.8 %shard_map.114 = (f32[8,4096]{1,0:T(8,128)}, f32[8,16384]{1,0:T(8,128)}) custom-call(s32[64]{0:T(128)} %bitcast.112, s32[64]{0:T(128)} %bitcast.114, s32[1]{0:T(128)} %bitcast.91.count_ref, f32[64,128,128]{2,1,0:T(8,128)} %bitcast.93, f32[8,4096]{1,0:T(8,128)} %get-tuple-element.62.rowv_ref, f32[8,16384]{1,0:T(8,128)} %get-tuple-element.61.colv_ref), custom_call_target="tpu_custom_call" | custom-call | tf_op jit(solution)/shard_map/pallas_call | solution.py:419
  156.8 1.4 fusion.7
  158.2 2.6 %fusion = f32[24,8]{0,1:T(8,128)S(1)} fusion(f32[8,16384]{1,0:T(8,128)} %get-tuple-element.26.csum_ref, f32[8,16384]{1,0:T(8,128)S(1)} %get-tuple-element.30, f32[8,16384]{1,0:T(8,128)S(1)} %copy-done.2, f32[8,16384]{1,0:T(8,128)S(1)} %get-tuple-element.29), kind=kOutput, calls=%fused_computation | convolution fusion | flops 38535168 | bytes 2097920 | tf_op jit(solution)/shard_map/dot_general | solution.py:431
  160.8 0.2 broadcast_multiply_fusion
  162.0 0.7 fusion.20.small_ref
  162.7 40.9 %shard_map.115 = (f32[8,512]{1,0:T(8,128)}, f32[16,128]{1,0:T(8,128)}) custom-call(f32[8,512]{1,0:T(8,128)} %copy-done.9, f32[8,4096]{1,0:T(8,128)} %get-tuple-element.25.rsum_ref, f32[8,16384]{1,0:T(8,128)} %get-tuple-element.26.csum_ref, f32[16,128]{1,0:T(8,128)} %fusion.20.small_ref), custom_call_target="tpu_custom_call" | custom-call | tf_op jit(solution)/shard_map/pallas_call | solution.py:323
  203.5 0.8 fusion.46
  204.6 2.2 %cholesky.64 = f32[24,24]{1,0:T(8,128)S(1)} custom-call(f32[24,24]{1,0:T(8,128)S(1)} %fusion.19), custom_call_target="Cholesky" | custom-call | tf_op jit(solution)/shard_map/jit(cholesky)/cholesky | solution.py:488
  206.8 0.6 compare_reduce_fusion
  207.4 0.6 fusion.13
  208.1 1.8 custom-call.19
  210.1 0.2 convolution_bitcast_fusion
  210.3 0.8 fusion.17
  211.1 0.6 copy.34
  211.7 1.3 copy.35
  (52 shorter events, 2.2 us)
Async XLA Ops:
  0.6 160.7 %copy-start = (f32[8,512]{1,0:T(8,128)S(1)}, f32[8,512]{1,0:T(8,128)}, u32[]{:S(2)}) copy-start(f32[8,512]{1,0:T(8,128)} %param.17) | copy-start | bytes 49156
  46.8 24.2 %copy-start.4 = (f32[8,512]{1,0:T(8,128)S(1)}, f32[8,512]{1,0:T(8,128)}, u32[]{:S(2)}) copy-start(f32[8,512]{1,0:T(8,128)} %param.15) | copy-start | bytes 49156
  46.8 24.1 %copy-start.12 = (f32[512]{0:T(512)S(1)}, f32[512]{0:T(512)}, u32[]{:S(2)}) copy-start(f32[512]{0:T(512)} %param.14) | copy-start | bytes 6148
  46.8 24.3 %copy-start.3 = (f32[16,4096]{1,0:T(8,128)S(1)}, f32[16,4096]{1,0:T(8,128)}, u32[]{:S(2)}) copy-start(f32[16,4096]{1,0:T(8,128)} %get-tuple-element.17.rowv_ref) | copy-start | bytes 786436
  46.8 25.6 %copy-start.1 = (f32[16,16384]{1,0:T(8,128)S(1)}, f32[16,16384]{1,0:T(8,128)}, u32[]{:S(2)}) copy-start(f32[16,16384]{1,0:T(8,128)} %get-tuple-element.18.colv_ref) | copy-start | bytes 3145732
  126.5 4.3 %copy-start.6 = (f32[8,16384]{1,0:T(8,128)S(1)}, f32[8,16384]{1,0:T(8,128)}, u32[]{:S(2)}) copy-start(f32[8,16384]{1,0:T(8,128)} %get-tuple-element.24) | copy-start | bytes 1572868
  130.8 1.3 copy-start.11
  132.9 23.8 %copy-start.5 = (f32[8,4096]{1,0:T(8,128)S(1)}, f32[8,4096]{1,0:T(8,128)}, u32[]{:S(2)}) copy-start(f32[8,4096]{1,0:T(8,128)} %get-tuple-element.62.rowv_ref) | copy-start | bytes 393220
  132.9 25.2 %copy-start.2 = (f32[8,16384]{1,0:T(8,128)S(1)}, f32[8,16384]{1,0:T(8,128)}, u32[]{:S(2)}) copy-start(f32[8,16384]{1,0:T(8,128)} %get-tuple-element.61.colv_ref) | copy-start | bytes 1572868
  156.8 4.0 %copy-start.10 = (f32[8,512]{1,0:T(8,128)S(1)}, f32[8,512]{1,0:T(8,128)}, u32[]{:S(2)}) copy-start(f32[8,512]{1,0:T(8,128)} %get-tuple-element.67) | copy-start | bytes 49156
  156.8 4.3 %copy-start.7 = (f32[8,512]{1,0:T(8,128)S(1)}, f32[8,512]{1,0:T(8,128)}, u32[]{:S(2)}) copy-start(f32[8,512]{1,0:T(8,128)} %param.16) | copy-start | bytes 49156
  161.0 1.7 copy-start.9
  161.0 52.0 %copy-start.8 = (f32[8,512]{1,0:T(8,128)}, f32[8,512]{1,0:T(8,128)S(1)}, u32[]{:S(2)}) copy-start(f32[8,512]{1,0:T(8,128)S(1)} %get-tuple-element.68) | copy-start | bytes 49156

commit v14 on v11

--- a/solution.py
+++ b/solution.py
@@ -427,6 +427,10 @@
     return jnp.dot(left, right.T, precision=highest)
 
 
+def lower_solve(factor, rhs, transpose_a=False):
+    return lax.linalg.triangular_solve(factor, rhs, left_side=True, lower=True, transpose_a=transpose_a)
+
+
 def dot_rows(left, right):
     return jnp.dot(left, right.T, precision=highest)
 
@@ -453,8 +457,8 @@
     image = image_tiles
     small_gram, small_proj = unpack_small(small, (small_gram, proj_part))
 
-    factor = jnp.linalg.cholesky(small_gram)
-    ritz_matrix = jax.scipy.linalg.cho_solve((factor, True), small_proj)
+    factor = lax.linalg.cholesky(small_gram, symmetrize_input=False)
+    ritz_matrix = lower_solve(factor, lower_solve(factor, small_proj), transpose_a=True)
     residual = image - jnp.dot(ritz_matrix.T, current, precision=highest)
 
     def residual_of(img_tiles, cur_tiles):
@@ -481,9 +485,9 @@
     residual_image = image_tiles
     correlation, mixed_terms = unpack_small(small, (correlation, mixed_part))
     pencil = 0.5 * (mixed_terms + mixed_terms.T)
-    lower_factor = jnp.linalg.cholesky(correlation)
-    half_solve = jax.scipy.linalg.solve_triangular(lower_factor, pencil, lower=True)
-    reduced = jax.scipy.linalg.solve_triangular(lower_factor, half_solve.T, lower=True)
+    lower_factor = lax.linalg.cholesky(correlation, symmetrize_input=False)
+    half_solve = lower_solve(lower_factor, pencil)
+    reduced = lower_solve(lower_factor, half_solve.T)
     return (image, residual, residual_image, reduced)
 
 

time: 174 us -> 176 us (1.011)
  Pallas kernels: 142 us -> 144 us
    pallas_call x2, Pallas kernels: 83.1 us -> 85.2 us  [reduce_tiles(): pl.pallas_call(functools.partial(_reduce_kernel, n_row, n_col, forward),...]
where the time goes in v14:
time: 176 us; the launch traced here: 174 us
  Pallas kernels  144 us (82%)
  other arithmetic  13.3 us (8%)
  matrix products  10.1 us (6%)
  local copies, waits for them, and re-layouts  4.88 us (3%)
    pallas_call x2, Pallas kernels, reduce_tiles(): pl.pallas_call(functools.partial(_reduce_kernel, n_row, n_col, forward),...  85.2 us
    pallas_call x1, Pallas kernels, gather_tiles(): pl.pallas_call(functools.partial(_gather_kernel, n_row, n_col), out_shape...  44.1 us
    pallas_call x2, Pallas kernels, slot_products(): pl.pallas_call(functools.partial(_slots_kernel, group, rows_k, tile), gri...  15 us
    dot_general x4, matrix products, tile_dot(): return jnp.dot(left, right.T, precision=highest)  7.66 us
    another operation x4, other arithmetic, lower_solve(): lax.linalg.triangular_solve(factor, rhs, left_side=True, lower=True, tran...  3.76 us

profile of v14, /device:TPU:24, one launch (start us, length us, event | category | flops | bytes accessed | tf_op | source)
XLA Modules:
  0.0 174.2 jit_solution(17406770234277016728)
XLA Ops:
  0.6 1.4 pad_maximum_fusion.1.x_ref
  2.0 44.1 %shard_map.111 = (f32[16,4096]{1,0:T(8,128)}, f32[16,16384]{1,0:T(8,128)}) custom-call(f32[16,512]{1,0:T(8,128)} %pad_maximum_fusion.1.x_ref), custom_call_target="tpu_custom_call" | custom-call | tf_op jit(solution)/shard_map/pallas_call | solution.py:92
  46.8 7.6 %shard_map.112 = (f32[8,4096]{1,0:T(8,128)}, f32[8,16384]{1,0:T(8,128)}) custom-call(s32[64]{0:T(128)} %bitcast.103, s32[64]{0:T(128)} %bitcast.105, s32[1]{0:T(128)} %bitcast.82.count_ref, f32[64,128,128]{2,1,0:T(8,128)} %bitcast.84, f32[16,4096]{1,0:T(8,128)} %get-tuple-element.17.rowv_ref, f32[16,16384]{1,0:T(8,128)} %get-tuple-element.18.colv_ref), custom_call_target="tpu_custom_call" | custom-call | tf_op jit(solution)/shard_map/pallas_call | solution.py:415
  54.6 1.3 convolution_add_fusion.2
  55.9 2.3 %convolution_add_fusion.1 = f32[8,8]{0,1:T(8,128)S(1)} fusion(f32[8,8]{0,1:T(8,128)S(1)} %convolution_add_fusion.2, f32[8,16384]{1,0:T(8,128)} %get-tuple-element.20.csum_ref, f32[16,16384]{1,0:T(8,128)S(1)} %copy-done.1), kind=kOutput, calls=%fused_computation.10 | convolution fusion | flops 12582976 | bytes 1052928 | tf_op jit(solution)/shard_map/dot_general | solution.py:427
  58.6 0.7 fusion.27.small_ref
  59.3 0.6 broadcast_multiply_fusion.1.base_ref
  59.9 46.7 %shard_map.113 = (f32[8,512]{1,0:T(8,128)}, f32[8,128]{1,0:T(8,128)}, f32[8,4096]{1,0:T(8,128)}, f32[8,16384]{1,0:T(8,128)}) custom-call(f32[8,512]{1,0:T(8,128)} %broadcast_multiply_fusion.1.base_ref, f32[8,4096]{1,0:T(8,128)} %get-tuple-element.19.rsum_ref, f32[8,16384]{1,0:T(8,128)} %get-tuple-element.20.csum_ref, f32[8,128]{1,0:T(8,128)} %fusion.27.small_ref), custom_call_target="tpu_custom_call" | custom-call | tf_op jit(solution)/shard_map/pallas_call | solution.py:323
  106.7 0.8 slice.144
  107.5 0.7 cholesky.30
  108.2 0.6 compare_reduce_fusion.1
  108.9 0.6 fusion.24
  109.5 0.6 custom-call.12
  110.2 0.2 fusion.25
  110.5 0.4 fusion.41
  110.9 1.2 fusion.40
  112.2 0.8 fusion.42
  113.0 7.3 %shard_map.114 = (f32[8,4096]{1,0:T(8,128)}, f32[8,16384]{1,0:T(8,128)}) custom-call(s32[64]{0:T(128)} %bitcast.104, s32[64]{0:T(128)} %bitcast.106, s32[1]{0:T(128)} %bitcast.83.count_ref, f32[64,128,128]{2,1,0:T(8,128)} %bitcast.85, f32[8,4096]{1,0:T(8,128)} %get-tuple-element.62.rowv_ref, f32[8,16384]{1,0:T(8,128)} %get-tuple-element.61.colv_ref), custom_call_target="tpu_custom_call" | custom-call | tf_op jit(solution)/shard_map/pallas_call | solution.py:415
  120.3 1.4 fusion.7
  121.7 2.6 %fusion = f32[24,8]{0,1:T(8,128)S(1)} fusion(f32[8,16384]{1,0:T(8,128)} %get-tuple-element.26.csum_ref, f32[8,16384]{1,0:T(8,128)S(1)} %get-tuple-element.30, f32[8,16384]{1,0:T(8,128)S(1)} %copy-done.2, f32[8,16384]{1,0:T(8,128)S(1)} %get-tuple-element.29), kind=kOutput, calls=%fused_computation | convolution fusion | flops 38535168 | bytes 2097920 | tf_op jit(solution)/shard_map/dot_general | solution.py:427
  124.4 0.2 broadcast_multiply_fusion
  125.5 0.7 fusion.19.small_ref
  126.2 38.5 %shard_map.115 = (f32[8,512]{1,0:T(8,128)}, f32[16,128]{1,0:T(8,128)}) custom-call(f32[8,512]{1,0:T(8,128)} %copy-done.9, f32[8,4096]{1,0:T(8,128)} %get-tuple-element.25.rsum_ref, f32[8,16384]{1,0:T(8,128)} %get-tuple-element.26.csum_ref, f32[16,128]{1,0:T(8,128)} %fusion.19.small_ref), custom_call_target="tpu_custom_call" | custom-call | tf_op jit(solution)/shard_map/pallas_call | solution.py:323
  164.7 0.8 fusion.44
  165.7 2.2 %cholesky.64 = f32[24,24]{1,0:T(8,128)S(1)} custom-call(f32[24,24]{1,0:T(8,128)S(1)} %reshape.90), custom_call_target="Cholesky" | custom-call | tf_op jit(solution)/shard_map/cholesky | solution.py:488
  167.9 0.6 compare_reduce_fusion
  168.5 0.6 fusion.13
  169.2 1.8 %custom-call.15 = f32[1,24,24]{1,2,0:T(8,128)S(1)} custom-call(f32[1,24,24]{2,1,0:T(8,128)S(1)} %fusion.13), custom_call_target="InvertDiagBlocksLowerTriangular" | custom-call | tf_op jit(solution)/shard_map/triangular_solve/custom-call.4 | solution.py:431
  171.2 0.2 convolution_bitcast_fusion
  171.4 0.8 fusion.17
  172.2 0.6 copy.28
  172.8 1.3 copy.29
  (48 shorter events, 2.1 us)
Async XLA Ops:
  0.6 124.3 %copy-start = (f32[8,512]{1,0:T(8,128)S(1)}, f32[8,512]{1,0:T(8,128)}, u32[]{:S(2)}) copy-start(f32[8,512]{1,0:T(8,128)} %param.17) | copy-start | bytes 49156
  46.8 7.7 %copy-start.4 = (f32[8,512]{1,0:T(8,128)S(1)}, f32[8,512]{1,0:T(8,128)}, u32[]{:S(2)}) copy-start(f32[8,512]{1,0:T(8,128)} %param.15) | copy-start | bytes 49156
  46.8 7.7 %copy-start.12 = (f32[512]{0:T(512)S(1)}, f32[512]{0:T(512)}, u32[]{:S(2)}) copy-start(f32[512]{0:T(512)} %param.14) | copy-start | bytes 6148
  46.8 7.8 %copy-start.3 = (f32[16,4096]{1,0:T(8,128)S(1)}, f32[16,4096]{1,0:T(8,128)}, u32[]{:S(2)}) copy-start(f32[16,4096]{1,0:T(8,128)} %get-tuple-element.17.rowv_ref) | copy-start | bytes 786436
  46.8 9.1 %copy-start.1 = (f32[16,16384]{1,0:T(8,128)S(1)}, f32[16,16384]{1,0:T(8,128)}, u32[]{:S(2)}) copy-start(f32[16,16384]{1,0:T(8,128)} %get-tuple-element.18.colv_ref) | copy-start | bytes 3145732
  106.6 4.2 %copy-start.6 = (f32[8,16384]{1,0:T(8,128)S(1)}, f32[8,16384]{1,0:T(8,128)}, u32[]{:S(2)}) copy-start(f32[8,16384]{1,0:T(8,128)} %get-tuple-element.24) | copy-start | bytes 1572868
  110.9 1.3 copy-start.11
  113.0 7.3 %copy-start.5 = (f32[8,4096]{1,0:T(8,128)S(1)}, f32[8,4096]{1,0:T(8,128)}, u32[]{:S(2)}) copy-start(f32[8,4096]{1,0:T(8,128)} %get-tuple-element.62.rowv_ref) | copy-start | bytes 393220
  113.0 8.8 %copy-start.2 = (f32[8,16384]{1,0:T(8,128)S(1)}, f32[8,16384]{1,0:T(8,128)}, u32[]{:S(2)}) copy-start(f32[8,16384]{1,0:T(8,128)} %get-tuple-element.61.colv_ref) | copy-start | bytes 1572868
  120.3 4.0 %copy-start.10 = (f32[8,512]{1,0:T(8,128)S(1)}, f32[8,512]{1,0:T(8,128)}, u32[]{:S(2)}) copy-start(f32[8,512]{1,0:T(8,128)} %get-tuple-element.67) | copy-start | bytes 49156
  120.3 4.3 %copy-start.7 = (f32[8,512]{1,0:T(8,128)S(1)}, f32[8,512]{1,0:T(8,128)}, u32[]{:S(2)}) copy-start(f32[8,512]{1,0:T(8,128)} %param.16) | copy-start | bytes 49156
  124.6 1.7 copy-start.9
  124.6 49.6 %copy-start.8 = (f32[8,512]{1,0:T(8,128)}, f32[8,512]{1,0:T(8,128)S(1)}, u32[]{:S(2)}) copy-start(f32[8,512]{1,0:T(8,128)S(1)} %get-tuple-element.68) | copy-start | bytes 49156

commit v15 on v14

--- a/solution.py
+++ b/solution.py
@@ -8,7 +8,7 @@
 from jax.sharding import PartitionSpec as P
 
 highest = lax.Precision.HIGHEST
-group_width = 8
+group_width = 16
 MESH = pl.DeviceIdType.MESH
 
 

time: 176 us -> 175 us (level)
  Pallas kernels: 144 us -> 142 us
    pallas_call x2, Pallas kernels: 85.2 us -> 82 us  [reduce_tiles(): pl.pallas_call(functools.partial(_reduce_kernel, n_row, n_col, forward),...]
where the time goes in v15:
time: 175 us; the launch traced here: 172 us
  Pallas kernels  142 us (81%)
  other arithmetic  13.3 us (8%)
  matrix products  10.1 us (6%)
  local copies, waits for them, and re-layouts  4.87 us (3%)
    pallas_call x2, Pallas kernels, reduce_tiles(): pl.pallas_call(functools.partial(_reduce_kernel, n_row, n_col, forward),...  82 us
    pallas_call x1, Pallas kernels, gather_tiles(): pl.pallas_call(functools.partial(_gather_kernel, n_row, n_col), out_shape...  44.1 us
    pallas_call x2, Pallas kernels, slot_products(): pl.pallas_call(functools.partial(_slots_kernel, group, rows_k, tile), gri...  16.2 us
    dot_general x4, matrix products, tile_dot(): return jnp.dot(left, right.T, precision=highest)  7.66 us
    another operation x4, other arithmetic, lower_solve(): lax.linalg.triangular_solve(factor, rhs, left_side=True, lower=True, tran...  3.76 us

profile of v15, /device:TPU:24, one launch (start us, length us, event | category | flops | bytes accessed | tf_op | source)
XLA Modules:
  0.0 172.2 jit_solution(1254379360986205234)
XLA Ops:
  0.6 1.4 pad_maximum_fusion.1.x_ref
  2.0 44.1 %shard_map.111 = (f32[16,4096]{1,0:T(8,128)}, f32[16,16384]{1,0:T(8,128)}) custom-call(f32[16,512]{1,0:T(8,128)} %pad_maximum_fusion.1.x_ref), custom_call_target="tpu_custom_call" | custom-call | tf_op jit(solution)/shard_map/pallas_call | solution.py:92
  46.8 8.2 %shard_map.112 = (f32[8,4096]{1,0:T(8,128)}, f32[8,16384]{1,0:T(8,128)}) custom-call(s32[64]{0:T(128)} %bitcast.103, s32[64]{0:T(128)} %bitcast.105, s32[1]{0:T(128)} %bitcast.82.count_ref, f32[64,128,128]{2,1,0:T(8,128)} %bitcast.84, f32[16,4096]{1,0:T(8,128)} %get-tuple-element.17.rowv_ref, f32[16,16384]{1,0:T(8,128)} %get-tuple-element.18.colv_ref), custom_call_target="tpu_custom_call" | custom-call | tf_op jit(solution)/shard_map/pallas_call | solution.py:415
  55.2 1.3 convolution_add_fusion.2
  56.5 2.3 %convolution_add_fusion.1 = f32[8,8]{0,1:T(8,128)S(1)} fusion(f32[8,8]{0,1:T(8,128)S(1)} %convolution_add_fusion.2, f32[8,16384]{1,0:T(8,128)} %get-tuple-element.20.csum_ref, f32[16,16384]{1,0:T(8,128)S(1)} %copy-done.1), kind=kOutput, calls=%fused_computation.10 | convolution fusion | flops 12582976 | bytes 1052928 | tf_op jit(solution)/shard_map/dot_general | solution.py:427
  59.2 0.7 fusion.27.small_ref
  59.9 0.6 broadcast_multiply_fusion.1.base_ref
  60.5 46.0 %shard_map.113 = (f32[8,512]{1,0:T(8,128)}, f32[8,128]{1,0:T(8,128)}, f32[8,4096]{1,0:T(8,128)}, f32[8,16384]{1,0:T(8,128)}) custom-call(f32[8,512]{1,0:T(8,128)} %broadcast_multiply_fusion.1.base_ref, f32[8,4096]{1,0:T(8,128)} %get-tuple-element.19.rsum_ref, f32[8,16384]{1,0:T(8,128)} %get-tuple-element.20.csum_ref, f32[8,128]{1,0:T(8,128)} %fusion.27.small_ref), custom_call_target="tpu_custom_call" | custom-call | tf_op jit(solution)/shard_map/pallas_call | solution.py:323
  106.5 0.8 slice.144
  107.4 0.7 cholesky.30
  108.1 0.6 compare_reduce_fusion.1
  108.7 0.6 fusion.24
  109.4 0.6 custom-call.12
  110.0 0.2 fusion.25
  110.4 0.4 fusion.41
  110.8 1.2 fusion.40
  112.0 0.8 fusion.42
  112.8 8.0 %shard_map.114 = (f32[8,4096]{1,0:T(8,128)}, f32[8,16384]{1,0:T(8,128)}) custom-call(s32[64]{0:T(128)} %bitcast.104, s32[64]{0:T(128)} %bitcast.106, s32[1]{0:T(128)} %bitcast.83.count_ref, f32[64,128,128]{2,1,0:T(8,128)} %bitcast.85, f32[8,4096]{1,0:T(8,128)} %get-tuple-element.62.rowv_ref, f32[8,16384]{1,0:T(8,128)} %get-tuple-element.61.colv_ref), custom_call_target="tpu_custom_call" | custom-call | tf_op jit(solution)/shard_map/pallas_call | solution.py:415
  120.9 1.4 fusion.7
  122.3 2.6 %fusion = f32[24,8]{0,1:T(8,128)S(1)} fusion(f32[8,16384]{1,0:T(8,128)} %get-tuple-element.26.csum_ref, f32[8,16384]{1,0:T(8,128)S(1)} %get-tuple-element.30, f32[8,16384]{1,0:T(8,128)S(1)} %copy-done.2, f32[8,16384]{1,0:T(8,128)S(1)} %get-tuple-element.29), kind=kOutput, calls=%fused_computation | convolution fusion | flops 38535168 | bytes 2097920 | tf_op jit(solution)/shard_map/dot_general | solution.py:427
  124.9 0.2 broadcast_multiply_fusion
  126.1 0.7 fusion.19.small_ref
  126.8 36.0 %shard_map.115 = (f32[8,512]{1,0:T(8,128)}, f32[16,128]{1,0:T(8,128)}) custom-call(f32[8,512]{1,0:T(8,128)} %copy-done.9, f32[8,4096]{1,0:T(8,128)} %get-tuple-element.25.rsum_ref, f32[8,16384]{1,0:T(8,128)} %get-tuple-element.26.csum_ref, f32[16,128]{1,0:T(8,128)} %fusion.19.small_ref), custom_call_target="tpu_custom_call" | custom-call | tf_op jit(solution)/shard_map/pallas_call | solution.py:323
  162.8 0.8 fusion.44
  163.7 2.2 %cholesky.64 = f32[24,24]{1,0:T(8,128)S(1)} custom-call(f32[24,24]{1,0:T(8,128)S(1)} %reshape.90), custom_call_target="Cholesky" | custom-call | tf_op jit(solution)/shard_map/cholesky | solution.py:488
  165.9 0.6 compare_reduce_fusion
  166.6 0.6 fusion.13
  167.2 1.8 %custom-call.15 = f32[1,24,24]{1,2,0:T(8,128)S(1)} custom-call(f32[1,24,24]{2,1,0:T(8,128)S(1)} %fusion.13), custom_call_target="InvertDiagBlocksLowerTriangular" | custom-call | tf_op jit(solution)/shard_map/triangular_solve/custom-call.4 | solution.py:431
  169.2 0.2 convolution_bitcast_fusion
  169.4 0.8 fusion.17
  170.3 0.6 copy.28
  170.9 1.3 copy.29
  (48 shorter events, 2.1 us)
Async XLA Ops:
  0.6 124.8 %copy-start = (f32[8,512]{1,0:T(8,128)S(1)}, f32[8,512]{1,0:T(8,128)}, u32[]{:S(2)}) copy-start(f32[8,512]{1,0:T(8,128)} %param.17) | copy-start | bytes 49156
  46.8 8.3 %copy-start.4 = (f32[8,512]{1,0:T(8,128)S(1)}, f32[8,512]{1,0:T(8,128)}, u32[]{:S(2)}) copy-start(f32[8,512]{1,0:T(8,128)} %param.15) | copy-start | bytes 49156
  46.8 8.3 %copy-start.12 = (f32[512]{0:T(512)S(1)}, f32[512]{0:T(512)}, u32[]{:S(2)}) copy-start(f32[512]{0:T(512)} %param.14) | copy-start | bytes 6148
  46.8 8.4 %copy-start.3 = (f32[16,4096]{1,0:T(8,128)S(1)}, f32[16,4096]{1,0:T(8,128)}, u32[]{:S(2)}) copy-start(f32[16,4096]{1,0:T(8,128)} %get-tuple-element.17.rowv_ref) | copy-start | bytes 786436
  46.8 9.7 %copy-start.1 = (f32[16,16384]{1,0:T(8,128)S(1)}, f32[16,16384]{1,0:T(8,128)}, u32[]{:S(2)}) copy-start(f32[16,16384]{1,0:T(8,128)} %get-tuple-element.18.colv_ref) | copy-start | bytes 3145732
  106.5 4.2 %copy-start.6 = (f32[8,16384]{1,0:T(8,128)S(1)}, f32[8,16384]{1,0:T(8,128)}, u32[]{:S(2)}) copy-start(f32[8,16384]{1,0:T(8,128)} %get-tuple-element.24) | copy-start | bytes 1572868
  110.8 1.3 copy-start.11
  112.8 8.0 %copy-start.5 = (f32[8,4096]{1,0:T(8,128)S(1)}, f32[8,4096]{1,0:T(8,128)}, u32[]{:S(2)}) copy-start(f32[8,4096]{1,0:T(8,128)} %get-tuple-element.62.rowv_ref) | copy-start | bytes 393220
  112.8 9.4 %copy-start.2 = (f32[8,16384]{1,0:T(8,128)S(1)}, f32[8,16384]{1,0:T(8,128)}, u32[]{:S(2)}) copy-start(f32[8,16384]{1,0:T(8,128)} %get-tuple-element.61.colv_ref) | copy-start | bytes 1572868
  120.9 4.0 %copy-start.10 = (f32[8,512]{1,0:T(8,128)S(1)}, f32[8,512]{1,0:T(8,128)}, u32[]{:S(2)}) copy-start(f32[8,512]{1,0:T(8,128)} %get-tuple-element.67) | copy-start | bytes 49156
  120.9 4.3 %copy-start.7 = (f32[8,512]{1,0:T(8,128)S(1)}, f32[8,512]{1,0:T(8,128)}, u32[]{:S(2)}) copy-start(f32[8,512]{1,0:T(8,128)} %param.16) | copy-start | bytes 49156
  125.1 1.7 copy-start.9
  125.1 47.1 %copy-start.8 = (f32[8,512]{1,0:T(8,128)}, f32[8,512]{1,0:T(8,128)S(1)}, u32[]{:S(2)}) copy-start(f32[8,512]{1,0:T(8,128)S(1)} %get-tuple-element.68) | copy-start | bytes 49156

commit v16 on v15

--- a/solution.py
+++ b/solution.py
@@ -8,7 +8,7 @@
 from jax.sharding import PartitionSpec as P
 
 highest = lax.Precision.HIGHEST
-group_width = 16
+group_width = 4
 MESH = pl.DeviceIdType.MESH
 
 

time: 175 us -> 180 us (1.029)
  Pallas kernels: 142 us -> 147 us
    pallas_call x2, Pallas kernels: 16.2 us -> 24.8 us  [slot_products(): pl.pallas_call(functools.partial(_slots_kernel, group, rows_k, tile), gri...]
    pallas_call x2, Pallas kernels: 82 us -> 78.6 us  [reduce_tiles(): pl.pallas_call(functools.partial(_reduce_kernel, n_row, n_col, forward),...]
where the time goes in v16:
time: 180 us; the launch traced here: 177 us
  Pallas kernels  147 us (82%)
  other arithmetic  13.3 us (7%)
  matrix products  10.1 us (6%)
  local copies, waits for them, and re-layouts  4.87 us (3%)
    pallas_call x2, Pallas kernels, reduce_tiles(): pl.pallas_call(functools.partial(_reduce_kernel, n_row, n_col, forward),...  78.6 us
    pallas_call x1, Pallas kernels, gather_tiles(): pl.pallas_call(functools.partial(_gather_kernel, n_row, n_col), out_shape...  44.1 us
    pallas_call x2, Pallas kernels, slot_products(): pl.pallas_call(functools.partial(_slots_kernel, group, rows_k, tile), gri...  24.8 us
    dot_general x4, matrix products, tile_dot(): return jnp.dot(left, right.T, precision=highest)  7.66 us
    another operation x4, other arithmetic, lower_solve(): lax.linalg.triangular_solve(factor, rhs, left_side=True, lower=True, tran...  3.76 us

profile of v16, /device:TPU:24, one launch (start us, length us, event | category | flops | bytes accessed | tf_op | source)
XLA Modules:
  0.0 177.4 jit_solution(17985177124325179963)
XLA Ops:
  0.6 1.4 pad_maximum_fusion.1.x_ref
  2.0 44.1 %shard_map.111 = (f32[16,4096]{1,0:T(8,128)}, f32[16,16384]{1,0:T(8,128)}) custom-call(f32[16,512]{1,0:T(8,128)} %pad_maximum_fusion.1.x_ref), custom_call_target="tpu_custom_call" | custom-call | tf_op jit(solution)/shard_map/pallas_call | solution.py:92
  46.8 12.5 %shard_map.112 = (f32[8,4096]{1,0:T(8,128)}, f32[8,16384]{1,0:T(8,128)}) custom-call(s32[64]{0:T(128)} %bitcast.103, s32[64]{0:T(128)} %bitcast.105, s32[1]{0:T(128)} %bitcast.82.count_ref, f32[64,128,128]{2,1,0:T(8,128)} %bitcast.84, f32[16,4096]{1,0:T(8,128)} %get-tuple-element.17.rowv_ref, f32[16,16384]{1,0:T(8,128)} %get-tuple-element.18.colv_ref), custom_call_target="tpu_custom_call" | custom-call | tf_op jit(solution)/shard_map/pallas_call | solution.py:415
  59.5 1.3 convolution_add_fusion.2
  60.8 2.3 %convolution_add_fusion.1 = f32[8,8]{0,1:T(8,128)S(1)} fusion(f32[8,8]{0,1:T(8,128)S(1)} %convolution_add_fusion.2, f32[8,16384]{1,0:T(8,128)} %get-tuple-element.20.csum_ref, f32[16,16384]{1,0:T(8,128)S(1)} %copy-done.1), kind=kOutput, calls=%fused_computation.10 | convolution fusion | flops 12582976 | bytes 1052928 | tf_op jit(solution)/shard_map/dot_general | solution.py:427
  63.5 0.7 fusion.27.small_ref
  64.2 0.6 broadcast_multiply_fusion.1.base_ref
  64.8 43.1 %shard_map.113 = (f32[8,512]{1,0:T(8,128)}, f32[8,128]{1,0:T(8,128)}, f32[8,4096]{1,0:T(8,128)}, f32[8,16384]{1,0:T(8,128)}) custom-call(f32[8,512]{1,0:T(8,128)} %broadcast_multiply_fusion.1.base_ref, f32[8,4096]{1,0:T(8,128)} %get-tuple-element.19.rsum_ref, f32[8,16384]{1,0:T(8,128)} %get-tuple-element.20.csum_ref, f32[8,128]{1,0:T(8,128)} %fusion.27.small_ref), custom_call_target="tpu_custom_call" | custom-call | tf_op jit(solution)/shard_map/pallas_call | solution.py:323
  107.9 0.8 slice.144
  108.7 0.7 cholesky.30
  109.5 0.6 compare_reduce_fusion.1
  110.1 0.6 fusion.24
  110.8 0.6 custom-call.12
  111.4 0.2 fusion.25
  111.8 0.4 fusion.41
  112.2 1.2 fusion.40
  113.4 0.8 fusion.42
  114.2 12.3 %shard_map.114 = (f32[8,4096]{1,0:T(8,128)}, f32[8,16384]{1,0:T(8,128)}) custom-call(s32[64]{0:T(128)} %bitcast.104, s32[64]{0:T(128)} %bitcast.106, s32[1]{0:T(128)} %bitcast.83.count_ref, f32[64,128,128]{2,1,0:T(8,128)} %bitcast.85, f32[8,4096]{1,0:T(8,128)} %get-tuple-element.62.rowv_ref, f32[8,16384]{1,0:T(8,128)} %get-tuple-element.61.colv_ref), custom_call_target="tpu_custom_call" | custom-call | tf_op jit(solution)/shard_map/pallas_call | solution.py:415
  126.5 1.4 fusion.7
  127.9 2.6 %fusion = f32[24,8]{0,1:T(8,128)S(1)} fusion(f32[8,16384]{1,0:T(8,128)} %get-tuple-element.26.csum_ref, f32[8,16384]{1,0:T(8,128)S(1)} %get-tuple-element.30, f32[8,16384]{1,0:T(8,128)S(1)} %copy-done.2, f32[8,16384]{1,0:T(8,128)S(1)} %get-tuple-element.29), kind=kOutput, calls=%fused_computation | convolution fusion | flops 38535168 | bytes 2097920 | tf_op jit(solution)/shard_map/dot_general | solution.py:427
  130.5 0.2 broadcast_multiply_fusion
  131.7 0.7 fusion.19.small_ref
  132.4 35.5 %shard_map.115 = (f32[8,512]{1,0:T(8,128)}, f32[16,128]{1,0:T(8,128)}) custom-call(f32[8,512]{1,0:T(8,128)} %copy-done.9, f32[8,4096]{1,0:T(8,128)} %get-tuple-element.25.rsum_ref, f32[8,16384]{1,0:T(8,128)} %get-tuple-element.26.csum_ref, f32[16,128]{1,0:T(8,128)} %fusion.19.small_ref), custom_call_target="tpu_custom_call" | custom-call | tf_op jit(solution)/shard_map/pallas_call | solution.py:323
  167.9 0.8 fusion.44
  168.8 2.2 %cholesky.64 = f32[24,24]{1,0:T(8,128)S(1)} custom-call(f32[24,24]{1,0:T(8,128)S(1)} %reshape.90), custom_call_target="Cholesky" | custom-call | tf_op jit(solution)/shard_map/cholesky | solution.py:488
  171.1 0.6 compare_reduce_fusion
  171.7 0.6 fusion.13
  172.4 1.8 %custom-call.15 = f32[1,24,24]{1,2,0:T(8,128)S(1)} custom-call(f32[1,24,24]{2,1,0:T(8,128)S(1)} %fusion.13), custom_call_target="InvertDiagBlocksLowerTriangular" | custom-call | tf_op jit(solution)/shard_map/triangular_solve/custom-call.4 | solution.py:431
  174.4 0.2 convolution_bitcast_fusion
  174.6 0.8 fusion.17
  175.4 0.6 copy.28
  176.0 1.3 copy.29
  (48 shorter events, 2.1 us)
Async XLA Ops:
  0.6 130.5 %copy-start = (f32[8,512]{1,0:T(8,128)S(1)}, f32[8,512]{1,0:T(8,128)}, u32[]{:S(2)}) copy-start(f32[8,512]{1,0:T(8,128)} %param.17) | copy-start | bytes 49156
  46.8 12.6 %copy-start.4 = (f32[8,512]{1,0:T(8,128)S(1)}, f32[8,512]{1,0:T(8,128)}, u32[]{:S(2)}) copy-start(f32[8,512]{1,0:T(8,128)} %param.15) | copy-start | bytes 49156
  46.8 12.5 %copy-start.12 = (f32[512]{0:T(512)S(1)}, f32[512]{0:T(512)}, u32[]{:S(2)}) copy-start(f32[512]{0:T(512)} %param.14) | copy-start | bytes 6148
  46.8 12.7 %copy-start.3 = (f32[16,4096]{1,0:T(8,128)S(1)}, f32[16,4096]{1,0:T(8,128)}, u32[]{:S(2)}) copy-start(f32[16,4096]{1,0:T(8,128)} %get-tuple-element.17.rowv_ref) | copy-start | bytes 786436
  46.8 14.0 %copy-start.1 = (f32[16,16384]{1,0:T(8,128)S(1)}, f32[16,16384]{1,0:T(8,128)}, u32[]{:S(2)}) copy-start(f32[16,16384]{1,0:T(8,128)} %get-tuple-element.18.colv_ref) | copy-start | bytes 3145732
  107.9 4.2 %copy-start.6 = (f32[8,16384]{1,0:T(8,128)S(1)}, f32[8,16384]{1,0:T(8,128)}, u32[]{:S(2)}) copy-start(f32[8,16384]{1,0:T(8,128)} %get-tuple-element.24) | copy-start | bytes 1572868
  112.1 1.3 copy-start.11
  114.2 12.3 %copy-start.5 = (f32[8,4096]{1,0:T(8,128)S(1)}, f32[8,4096]{1,0:T(8,128)}, u32[]{:S(2)}) copy-start(f32[8,4096]{1,0:T(8,128)} %get-tuple-element.62.rowv_ref) | copy-start | bytes 393220
  114.2 13.7 %copy-start.2 = (f32[8,16384]{1,0:T(8,128)S(1)}, f32[8,16384]{1,0:T(8,128)}, u32[]{:S(2)}) copy-start(f32[8,16384]{1,0:T(8,128)} %get-tuple-element.61.colv_ref) | copy-start | bytes 1572868
  126.5 4.0 %copy-start.10 = (f32[8,512]{1,0:T(8,128)S(1)}, f32[8,512]{1,0:T(8,128)}, u32[]{:S(2)}) copy-start(f32[8,512]{1,0:T(8,128)} %get-tuple-element.67) | copy-start | bytes 49156
  126.5 4.3 %copy-start.7 = (f32[8,512]{1,0:T(8,128)S(1)}, f32[8,512]{1,0:T(8,128)}, u32[]{:S(2)}) copy-start(f32[8,512]{1,0:T(8,128)} %param.16) | copy-start | bytes 49156
  130.7 1.7 copy-start.9
  130.7 46.6 %copy-start.8 = (f32[8,512]{1,0:T(8,128)}, f32[8,512]{1,0:T(8,128)S(1)}, u32[]{:S(2)}) copy-start(f32[8,512]{1,0:T(8,128)S(1)} %get-tuple-element.68) | copy-start | bytes 49156

commit v17 on v14

--- a/solution.py
+++ b/solution.py
@@ -23,8 +23,8 @@
         pl.semaphore_signal(barrier, 1, device_id=(lax.rem(r + k, n_row), c), device_id_type=MESH)
         return carry
 
+    lax.fori_loop(1, n_row, greet_row, 0)
     lax.fori_loop(1, n_col, greet_col, 0)
-    lax.fori_loop(1, n_row, greet_row, 0)
     pl.semaphore_wait(barrier, n_row + n_col - 2)
 
 
@@ -67,8 +67,8 @@
         col_copy(lax.rem(r + k, n_row), r).start()
         return carry
 
+    lax.fori_loop(1, n_row, start_row, 0)
     lax.fori_loop(1, n_col, start_col, 0)
-    lax.fori_loop(1, n_row, start_row, 0)
 
     def wait_col(k, carry):
         row_copy(lax.rem(c + k, n_col), c).wait_send()

time: 176 us -> 180 us (1.023)
  Pallas kernels: 144 us -> 148 us
    pallas_call x2, Pallas kernels: 15 us -> 25.2 us  [slot_products(): pl.pallas_call(functools.partial(_slots_kernel, group, rows_k, tile), gri...]
    pallas_call x2, Pallas kernels: 85.2 us -> 81.8 us  [reduce_tiles(): pl.pallas_call(functools.partial(_reduce_kernel, n_row, n_col, forward),...]
    pallas_call x1, Pallas kernels: 44.1 us -> 40.9 us  [gather_tiles(): pl.pallas_call(functools.partial(_gather_kernel, n_row, n_col), out_shape...]
where the time goes in v17:
time: 180 us; the launch traced here: 178 us
  Pallas kernels  148 us (82%)
  other arithmetic  13.3 us (7%)
  matrix products  10.1 us (6%)
  local copies, waits for them, and re-layouts  4.88 us (3%)
    pallas_call x2, Pallas kernels, reduce_tiles(): pl.pallas_call(functools.partial(_reduce_kernel, n_row, n_col, forward),...  81.8 us
    pallas_call x1, Pallas kernels, gather_tiles(): pl.pallas_call(functools.partial(_gather_kernel, n_row, n_col), out_shape...  40.9 us
    pallas_call x2, Pallas kernels, slot_products(): pl.pallas_call(functools.partial(_slots_kernel, group, rows_k, tile), gri...  25.2 us
    dot_general x4, matrix products, tile_dot(): return jnp.dot(left, right.T, precision=highest)  7.66 us
    another operation x4, other arithmetic, lower_solve(): lax.linalg.triangular_solve(factor, rhs, left_side=True, lower=True, tran...  3.76 us

profile of v17, /device:TPU:24, one launch (start us, length us, event | category | flops | bytes accessed | tf_op | source)
XLA Modules:
  0.0 177.8 jit_solution(12600347272899921743)
XLA Ops:
  0.6 1.4 pad_maximum_fusion.1.x_ref
  2.0 40.9 %shard_map.111 = (f32[16,4096]{1,0:T(8,128)}, f32[16,16384]{1,0:T(8,128)}) custom-call(f32[16,512]{1,0:T(8,128)} %pad_maximum_fusion.1.x_ref), custom_call_target="tpu_custom_call" | custom-call | tf_op jit(solution)/shard_map/pallas_call | solution.py:92
  43.6 12.8 %shard_map.112 = (f32[8,4096]{1,0:T(8,128)}, f32[8,16384]{1,0:T(8,128)}) custom-call(s32[64]{0:T(128)} %bitcast.103, s32[64]{0:T(128)} %bitcast.105, s32[1]{0:T(128)} %bitcast.82.count_ref, f32[64,128,128]{2,1,0:T(8,128)} %bitcast.84, f32[16,4096]{1,0:T(8,128)} %get-tuple-element.17.rowv_ref, f32[16,16384]{1,0:T(8,128)} %get-tuple-element.18.colv_ref), custom_call_target="tpu_custom_call" | custom-call | tf_op jit(solution)/shard_map/pallas_call | solution.py:415
  56.5 1.3 convolution_add_fusion.2
  57.8 2.3 %convolution_add_fusion.1 = f32[8,8]{0,1:T(8,128)S(1)} fusion(f32[8,8]{0,1:T(8,128)S(1)} %convolution_add_fusion.2, f32[8,16384]{1,0:T(8,128)} %get-tuple-element.20.csum_ref, f32[16,16384]{1,0:T(8,128)S(1)} %copy-done.1), kind=kOutput, calls=%fused_computation.10 | convolution fusion | flops 12582976 | bytes 1052928 | tf_op jit(solution)/shard_map/dot_general | solution.py:427
  60.6 0.7 fusion.27.small_ref
  61.2 0.6 broadcast_multiply_fusion.1.base_ref
  61.9 42.6 %shard_map.113 = (f32[8,512]{1,0:T(8,128)}, f32[8,128]{1,0:T(8,128)}, f32[8,4096]{1,0:T(8,128)}, f32[8,16384]{1,0:T(8,128)}) custom-call(f32[8,512]{1,0:T(8,128)} %broadcast_multiply_fusion.1.base_ref, f32[8,4096]{1,0:T(8,128)} %get-tuple-element.19.rsum_ref, f32[8,16384]{1,0:T(8,128)} %get-tuple-element.20.csum_ref, f32[8,128]{1,0:T(8,128)} %fusion.27.small_ref), custom_call_target="tpu_custom_call" | custom-call | tf_op jit(solution)/shard_map/pallas_call | solution.py:323
  104.5 0.8 slice.144
  105.3 0.7 cholesky.30
  106.1 0.6 compare_reduce_fusion.1
  106.7 0.6 fusion.24
  107.4 0.6 custom-call.12
  108.0 0.2 fusion.25
  108.3 0.4 fusion.41
  108.7 1.2 fusion.40
  110.0 0.8 fusion.42
  110.8 12.5 %shard_map.114 = (f32[8,4096]{1,0:T(8,128)}, f32[8,16384]{1,0:T(8,128)}) custom-call(s32[64]{0:T(128)} %bitcast.104, s32[64]{0:T(128)} %bitcast.106, s32[1]{0:T(128)} %bitcast.83.count_ref, f32[64,128,128]{2,1,0:T(8,128)} %bitcast.85, f32[8,4096]{1,0:T(8,128)} %get-tuple-element.62.rowv_ref, f32[8,16384]{1,0:T(8,128)} %get-tuple-element.61.colv_ref), custom_call_target="tpu_custom_call" | custom-call | tf_op jit(solution)/shard_map/pallas_call | solution.py:415
  123.3 1.4 fusion.7
  124.7 2.6 %fusion = f32[24,8]{0,1:T(8,128)S(1)} fusion(f32[8,16384]{1,0:T(8,128)} %get-tuple-element.26.csum_ref, f32[8,16384]{1,0:T(8,128)S(1)} %get-tuple-element.30, f32[8,16384]{1,0:T(8,128)S(1)} %copy-done.2, f32[8,16384]{1,0:T(8,128)S(1)} %get-tuple-element.29), kind=kOutput, calls=%fused_computation | convolution fusion | flops 38535168 | bytes 2097920 | tf_op jit(solution)/shard_map/dot_general | solution.py:427
  127.3 0.2 broadcast_multiply_fusion
  128.5 0.7 fusion.19.small_ref
  129.2 39.2 %shard_map.115 = (f32[8,512]{1,0:T(8,128)}, f32[16,128]{1,0:T(8,128)}) custom-call(f32[8,512]{1,0:T(8,128)} %copy-done.9, f32[8,4096]{1,0:T(8,128)} %get-tuple-element.25.rsum_ref, f32[8,16384]{1,0:T(8,128)} %get-tuple-element.26.csum_ref, f32[16,128]{1,0:T(8,128)} %fusion.19.small_ref), custom_call_target="tpu_custom_call" | custom-call | tf_op jit(solution)/shard_map/pallas_call | solution.py:323
  168.4 0.8 fusion.44
  169.3 2.2 %cholesky.64 = f32[24,24]{1,0:T(8,128)S(1)} custom-call(f32[24,24]{1,0:T(8,128)S(1)} %reshape.90), custom_call_target="Cholesky" | custom-call | tf_op jit(solution)/shard_map/cholesky | solution.py:488
  171.5 0.6 compare_reduce_fusion
  172.2 0.6 fusion.13
  172.9 1.8 %custom-call.15 = f32[1,24,24]{1,2,0:T(8,128)S(1)} custom-call(f32[1,24,24]{2,1,0:T(8,128)S(1)} %fusion.13), custom_call_target="InvertDiagBlocksLowerTriangular" | custom-call | tf_op jit(solution)/shard_map/triangular_solve/custom-call.4 | solution.py:431
  174.9 0.2 convolution_bitcast_fusion
  175.1 0.8 fusion.17
  175.9 0.6 copy.28
  176.5 1.3 copy.29
  (48 shorter events, 2.1 us)
Async XLA Ops:
  0.6 127.2 %copy-start = (f32[8,512]{1,0:T(8,128)S(1)}, f32[8,512]{1,0:T(8,128)}, u32[]{:S(2)}) copy-start(f32[8,512]{1,0:T(8,128)} %param.17) | copy-start | bytes 49156
  43.6 12.8 %copy-start.4 = (f32[8,512]{1,0:T(8,128)S(1)}, f32[8,512]{1,0:T(8,128)}, u32[]{:S(2)}) copy-start(f32[8,512]{1,0:T(8,128)} %param.15) | copy-start | bytes 49156
  43.6 12.8 %copy-start.12 = (f32[512]{0:T(512)S(1)}, f32[512]{0:T(512)}, u32[]{:S(2)}) copy-start(f32[512]{0:T(512)} %param.14) | copy-start | bytes 6148
  43.6 12.9 %copy-start.3 = (f32[16,4096]{1,0:T(8,128)S(1)}, f32[16,4096]{1,0:T(8,128)}, u32[]{:S(2)}) copy-start(f32[16,4096]{1,0:T(8,128)} %get-tuple-element.17.rowv_ref) | copy-start | bytes 786436
  43.6 14.2 %copy-start.1 = (f32[16,16384]{1,0:T(8,128)S(1)}, f32[16,16384]{1,0:T(8,128)}, u32[]{:S(2)}) copy-start(f32[16,16384]{1,0:T(8,128)} %get-tuple-element.18.colv_ref) | copy-start | bytes 3145732
  104.5 4.2 %copy-start.6 = (f32[8,16384]{1,0:T(8,128)S(1)}, f32[8,16384]{1,0:T(8,128)}, u32[]{:S(2)}) copy-start(f32[8,16384]{1,0:T(8,128)} %get-tuple-element.24) | copy-start | bytes 1572868
  108.7 1.3 copy-start.11
  110.8 12.5 %copy-start.5 = (f32[8,4096]{1,0:T(8,128)S(1)}, f32[8,4096]{1,0:T(8,128)}, u32[]{:S(2)}) copy-start(f32[8,4096]{1,0:T(8,128)} %get-tuple-element.62.rowv_ref) | copy-start | bytes 393220
  110.8 13.9 %copy-start.2 = (f32[8,16384]{1,0:T(8,128)S(1)}, f32[8,16384]{1,0:T(8,128)}, u32[]{:S(2)}) copy-start(f32[8,16384]{1,0:T(8,128)} %get-tuple-element.61.colv_ref) | copy-start | bytes 1572868
  123.3 4.0 %copy-start.10 = (f32[8,512]{1,0:T(8,128)S(1)}, f32[8,512]{1,0:T(8,128)}, u32[]{:S(2)}) copy-start(f32[8,512]{1,0:T(8,128)} %get-tuple-element.67) | copy-start | bytes 49156
  123.3 4.3 %copy-start.7 = (f32[8,512]{1,0:T(8,128)S(1)}, f32[8,512]{1,0:T(8,128)}, u32[]{:S(2)}) copy-start(f32[8,512]{1,0:T(8,128)} %param.16) | copy-start | bytes 49156
  127.5 1.7 copy-start.9
  127.5 50.3 %copy-start.8 = (f32[8,512]{1,0:T(8,128)}, f32[8,512]{1,0:T(8,128)S(1)}, u32[]{:S(2)}) copy-start(f32[8,512]{1,0:T(8,128)S(1)} %get-tuple-element.68) | copy-start | bytes 49156

commit v18 on v14

--- a/solution.py
+++ b/solution.py
@@ -462,8 +462,7 @@
     residual = image - jnp.dot(ritz_matrix.T, current, precision=highest)
 
     def residual_of(img_tiles, cur_tiles):
-        fitted = sum(ritz_matrix[l][:, None] * cur_tiles[l:l + 1, :] for l in range(k))
-        return img_tiles - fitted
+        return img_tiles - jnp.dot(ritz_matrix.T, cur_tiles, precision=highest)
 
     row_res = residual_of(row_img, row_cur)
     col_res = residual_of(col_img, col_cur)

time: 176 us -> 181 us (1.028)
  matrix products: 10.1 us -> 15.2 us
    dot_general x0 -> x2, matrix products: none -> 4.4 us  [residual_of(): return img_tiles - jnp.dot(ritz_matrix.T, cur_tiles, precision=highest)]
    slice x2 -> x0, other arithmetic: 1.98 us -> none  [local(): row_cur, col_cur = (row_cp[:k], col_cp[:k])]
where the time goes in v18:
time: 181 us; the launch traced here: 179 us
  Pallas kernels  145 us (80%)
  matrix products  15.2 us (8%)
  other arithmetic  12.1 us (7%)
  local copies, waits for them, and re-layouts  5.38 us (3%)
    pallas_call x2, Pallas kernels, reduce_tiles(): pl.pallas_call(functools.partial(_reduce_kernel, n_row, n_col, forward),...  85.5 us
    pallas_call x1, Pallas kernels, gather_tiles(): pl.pallas_call(functools.partial(_gather_kernel, n_row, n_col), out_shape...  44.1 us
    pallas_call x2, Pallas kernels, slot_products(): pl.pallas_call(functools.partial(_slots_kernel, group, rows_k, tile), gri...  15.3 us
    dot_general x4, matrix products, tile_dot(): return jnp.dot(left, right.T, precision=highest)  6.76 us
    dot_general x2, matrix products, residual_of(): return img_tiles - jnp.dot(ritz_matrix.T, cur_tiles, precision=highest)  4.4 us
    another operation x4, other arithmetic, lower_solve(): lax.linalg.triangular_solve(factor, rhs, left_side=True, lower=True, tran...  3.76 us

profile of v18, /device:TPU:24, one launch (start us, length us, event | category | flops | bytes accessed | tf_op | source)
XLA Modules:
  0.0 179.2 jit_solution(9175376645716145636)
XLA Ops:
  1.3 0.9 convolution_bitcast_fusion.1
  2.2 0.9 fusion.45
  3.3 1.3 broadcast_multiply_fusion.1.base_ref
  4.6 1.3 pad_maximum_fusion.1.x_ref
  5.9 44.1 %shard_map.111 = (f32[16,4096]{1,0:T(8,128)}, f32[16,16384]{1,0:T(8,128)}) custom-call(f32[16,512]{1,0:T(8,128)} %pad_maximum_fusion.1.x_ref), custom_call_target="tpu_custom_call" | custom-call | tf_op jit(solution)/shard_map/pallas_call | solution.py:92
  50.1 1.0 fusion.43
  51.1 7.8 %shard_map.112 = (f32[8,4096]{1,0:T(8,128)}, f32[8,16384]{1,0:T(8,128)}) custom-call(s32[64]{0:T(128)} %bitcast.57, s32[64]{0:T(128)} %bitcast.59, s32[1]{0:T(128)} %bitcast.52.count_ref, f32[64,128,128]{2,1,0:T(8,128)} %bitcast.54, f32[16,4096]{1,0:T(8,128)} %get-tuple-element.17.rowv_ref, f32[16,16384]{1,0:T(8,128)} %get-tuple-element.18.colv_ref), custom_call_target="tpu_custom_call" | custom-call | tf_op jit(solution)/shard_map/pallas_call | solution.py:415
  58.8 1.3 convolution_add_fusion.2
  60.2 2.3 %convolution_add_fusion.1 = f32[8,8]{0,1:T(8,128)S(1)} fusion(f32[8,8]{0,1:T(8,128)S(1)} %convolution_add_fusion.2, f32[8,16384]{1,0:T(8,128)} %get-tuple-element.20.csum_ref, f32[16,16384]{1,0:T(8,128)S(1)} %copy-done.1), kind=kOutput, calls=%fused_computation.12 | convolution fusion | flops 12582976 | bytes 1052928 | tf_op jit(solution)/shard_map/dot_general | solution.py:427
  62.6 0.7 fusion.27.small_ref
  63.3 45.1 %shard_map.113 = (f32[8,512]{1,0:T(8,128)}, f32[8,128]{1,0:T(8,128)}, f32[8,4096]{1,0:T(8,128)}, f32[8,16384]{1,0:T(8,128)}) custom-call(f32[8,512]{1,0:T(8,128)} %broadcast_multiply_fusion.1.base_ref, f32[8,4096]{1,0:T(8,128)} %get-tuple-element.19.rsum_ref, f32[8,16384]{1,0:T(8,128)} %get-tuple-element.20.csum_ref, f32[8,128]{1,0:T(8,128)} %fusion.27.small_ref), custom_call_target="tpu_custom_call" | custom-call | tf_op jit(solution)/shard_map/pallas_call | solution.py:323
  108.4 0.8 slice.48
  109.2 0.7 cholesky.30
  109.9 0.6 compare_reduce_fusion.1
  110.6 0.6 fusion.24
  111.2 0.6 custom-call.12
  112.2 1.9 %convolution_subtract_fusion.1.rowv_ref = f32[8,4096]{1,0:T(8,128)} fusion(f32[8,4096]{1,0:T(8,128)} %get-tuple-element.23, f32[8,8]{1,0:T(8,128)S(1)} %fusion.29, f32[16,4096]{1,0:T(8,128)S(1)} %copy-done.3), kind=kOutput, calls=%fused_computation.1 | convolution fusion | flops 3178496 | bytes 397312 | tf_op jit(solution)/shard_map/dot_general | solution.py:465
  114.1 2.5 %convolution_subtract_fusion.colv_ref = f32[8,16384]{1,0:T(8,128)} fusion(f32[8,16384]{1,0:T(8,128)} %get-tuple-element.24, f32[8,8]{1,0:T(8,128)S(1)} %fusion.29, f32[16,16384]{1,0:T(8,128)S(1)} %copy-done.1), kind=kOutput, calls=%fused_computation | convolution fusion | flops 12713984 | bytes 1576960 | tf_op jit(solution)/shard_map/dot_general | solution.py:465
  117.5 7.5 %shard_map.114 = (f32[8,4096]{1,0:T(8,128)}, f32[8,16384]{1,0:T(8,128)}) custom-call(s32[64]{0:T(128)} %bitcast.58, s32[64]{0:T(128)} %bitcast.60, s32[1]{0:T(128)} %bitcast.53.count_ref, f32[64,128,128]{2,1,0:T(8,128)} %bitcast.55, f32[8,4096]{1,0:T(8,128)} %convolution_subtract_fusion.1.rowv_ref, f32[8,16384]{1,0:T(8,128)} %convolution_subtract_fusion.colv_ref), custom_call_target="tpu_custom_call" | custom-call | tf_op jit(solution)/shard_map/pallas_call | solution.py:415
  125.1 2.7 %fusion = f32[24,8]{0,1:T(8,128)S(1)} fusion(f32[8,16384]{1,0:T(8,128)} %get-tuple-element.26.csum_ref, f32[8,16384]{1,0:T(8,128)S(1)} %get-tuple-element.30, f32[8,16384]{1,0:T(8,128)S(1)} %copy-done.2, f32[8,16384]{1,0:T(8,128)S(1)} %get-tuple-element.29), kind=kOutput, calls=%fused_computation.2 | convolution fusion | flops 38535168 | bytes 2097920 | tf_op jit(solution)/shard_map/dot_general | solution.py:427
  127.7 0.5 fusion.7
  128.6 0.7 fusion.19.small_ref
  129.3 40.5 %shard_map.115 = (f32[8,512]{1,0:T(8,128)}, f32[16,128]{1,0:T(8,128)}) custom-call(f32[8,512]{1,0:T(8,128)} %copy-done.9, f32[8,4096]{1,0:T(8,128)} %get-tuple-element.25.rsum_ref, f32[8,16384]{1,0:T(8,128)} %get-tuple-element.26.csum_ref, f32[16,128]{1,0:T(8,128)} %fusion.19.small_ref), custom_call_target="tpu_custom_call" | custom-call | tf_op jit(solution)/shard_map/pallas_call | solution.py:323
  169.7 0.8 fusion.44
  170.7 2.2 %cholesky.64 = f32[24,24]{1,0:T(8,128)S(1)} custom-call(f32[24,24]{1,0:T(8,128)S(1)} %reshape.82), custom_call_target="Cholesky" | custom-call | tf_op jit(solution)/shard_map/cholesky | solution.py:487
  172.9 0.6 compare_reduce_fusion
  173.5 0.6 fusion.13
  174.2 1.8 %custom-call.15 = f32[1,24,24]{1,2,0:T(8,128)S(1)} custom-call(f32[1,24,24]{2,1,0:T(8,128)S(1)} %fusion.13), custom_call_target="InvertDiagBlocksLowerTriangular" | custom-call | tf_op jit(solution)/shard_map/triangular_solve/custom-call.4 | solution.py:431
  176.2 0.2 convolution_bitcast_fusion
  176.4 0.8 fusion.17
  177.2 0.6 copy.28
  177.8 1.3 copy.29
  (45 shorter events, 2.2 us)
Async XLA Ops:
  0.6 116.4 %copy-start = (f32[8,512]{1,0:T(8,128)S(1)}, f32[8,512]{1,0:T(8,128)}, u32[]{:S(2)}) copy-start(f32[8,512]{1,0:T(8,128)} %param.17) | copy-start | bytes 49156
  51.1 7.8 %copy-start.3 = (f32[16,4096]{1,0:T(8,128)S(1)}, f32[16,4096]{1,0:T(8,128)}, u32[]{:S(2)}) copy-start(f32[16,4096]{1,0:T(8,128)} %get-tuple-element.17.rowv_ref) | copy-start | bytes 786436
  51.1 9.1 %copy-start.1 = (f32[16,16384]{1,0:T(8,128)S(1)}, f32[16,16384]{1,0:T(8,128)}, u32[]{:S(2)}) copy-start(f32[16,16384]{1,0:T(8,128)} %get-tuple-element.18.colv_ref) | copy-start | bytes 3145732
  114.1 2.6 %copy-start.4 = (f32[8,512]{1,0:T(8,128)S(1)}, f32[8,512]{1,0:T(8,128)}, u32[]{:S(2)}) copy-start(f32[8,512]{1,0:T(8,128)} %param.15) | copy-start | bytes 49156
  114.1 2.6 %copy-start.10 = (f32[8,512]{1,0:T(8,128)S(1)}, f32[8,512]{1,0:T(8,128)}, u32[]{:S(2)}) copy-start(f32[8,512]{1,0:T(8,128)} %get-tuple-element.41) | copy-start | bytes 49156
  114.1 2.6 %copy-start.11 = (f32[512]{0:T(512)S(1)}, f32[512]{0:T(512)}, u32[]{:S(2)}) copy-start(f32[512]{0:T(512)} %param.14) | copy-start | bytes 6148
  114.1 2.8 %copy-start.7 = (f32[8,512]{1,0:T(8,128)S(1)}, f32[8,512]{1,0:T(8,128)}, u32[]{:S(2)}) copy-start(f32[8,512]{1,0:T(8,128)} %param.16) | copy-start | bytes 49156
  116.9 11.3 %copy-start.8 = (f32[8,512]{1,0:T(8,128)}, f32[8,512]{1,0:T(8,128)S(1)}, u32[]{:S(2)}) copy-start(f32[8,512]{1,0:T(8,128)S(1)} %get-tuple-element.42) | copy-start | bytes 49156
  116.9 11.3 %copy-start.9 = (f32[8,512]{1,0:T(8,128)}, f32[8,512]{1,0:T(8,128)S(1)}, u32[]{:S(2)}) copy-start(f32[8,512]{1,0:T(8,128)S(1)} %get-tuple-element.35.base_ref) | copy-start | bytes 49156
  117.5 7.6 %copy-start.2 = (f32[8,16384]{1,0:T(8,128)S(1)}, f32[8,16384]{1,0:T(8,128)}, u32[]{:S(2)}) copy-start(f32[8,16384]{1,0:T(8,128)} %convolution_subtract_fusion.colv_ref) | copy-start | bytes 1572868
  125.1 2.7 %copy-start.5 = (f32[8,4096]{1,0:T(8,128)S(1)}, f32[8,4096]{1,0:T(8,128)}, u32[]{:S(2)}) copy-start(f32[8,4096]{1,0:T(8,128)} %convolution_subtract_fusion.1.rowv_ref) | copy-start | bytes 393220
  125.1 2.7 %copy-start.6 = (f32[8,4096]{1,0:T(8,128)S(1)}, f32[8,4096]{1,0:T(8,128)}, u32[]{:S(2)}) copy-start(f32[8,4096]{1,0:T(8,128)} %get-tuple-element.25.rsum_ref) | copy-start | bytes 393220

commit v19 on v14

--- a/solution.py
+++ b/solution.py
@@ -469,12 +469,12 @@
     col_res = residual_of(col_img, col_cur)
     row_sum, col_sum = slot_products(blocks, rows_here, cols_here, live_count, row_res, col_res, k)
     search_basis = jnp.concatenate([current, residual, previous], 0)
-    row_basis = jnp.concatenate([row_cur, row_res, row_cp[k:]], 0)
-    col_basis = jnp.concatenate([col_cur, col_res, col_cp[k:]], 0)
     scaled = diagonal[None, :] * residual
     correlation = dot_rows(search_basis, search_basis)
     residual_part = (
-        dot_rows(search_basis, scaled) + tile_dot(row_basis, row_sum) + tile_dot(col_basis, col_sum)
+        dot_rows(search_basis, scaled)
+        + jnp.concatenate([tile_dot(part, row_sum) for part in (row_cur, row_res, row_cp[k:])], 0)
+        + jnp.concatenate([tile_dot(part, col_sum) for part in (col_cur, col_res, col_cp[k:])], 0)
     )
     mixed_part = jnp.concatenate(
         [dot_rows(search_basis, image), residual_part, dot_rows(search_basis, previous_image)], 1

time: 176 us -> 187 us (1.062)
  matrix products: 10.1 us -> 18.3 us
  other arithmetic: 13.3 us -> 15.3 us
    dot_general x4 -> x8, matrix products: 7.66 us -> 14.3 us  [tile_dot(): return jnp.dot(left, right.T, precision=highest)]
    sub x0 -> x2, other arithmetic: none -> 3.92 us  [residual_of(): return img_tiles - fitted]
    pallas_call x2, Pallas kernels: 85.2 us -> 87.9 us  [reduce_tiles(): pl.pallas_call(functools.partial(_reduce_kernel, n_row, n_col, forward),...]
    slice x2 -> x0, other arithmetic: 1.98 us -> none  [local(): row_cur, col_cur = (row_cp[:k], col_cp[:k])]
where the time goes in v19:
time: 187 us; the launch traced here: 185 us
  Pallas kernels  145 us (78%)
  matrix products  18.3 us (10%)
  other arithmetic  15.3 us (8%)
  local copies, waits for them, and re-layouts  4.8 us (3%)
    pallas_call x2, Pallas kernels, reduce_tiles(): pl.pallas_call(functools.partial(_reduce_kernel, n_row, n_col, forward),...  87.9 us
    pallas_call x1, Pallas kernels, gather_tiles(): pl.pallas_call(functools.partial(_gather_kernel, n_row, n_col), out_shape...  44.1 us
    dot_general x8, matrix products, tile_dot(): return jnp.dot(left, right.T, precision=highest)  14.3 us
    pallas_call x2, Pallas kernels, slot_products(): pl.pallas_call(functools.partial(_slots_kernel, group, rows_k, tile), gri...  13.4 us
    sub x2, other arithmetic, residual_of(): return img_tiles - fitted  3.92 us
    another operation x4, other arithmetic, lower_solve(): lax.linalg.triangular_solve(factor, rhs, left_side=True, lower=True, tran...  3.76 us

profile of v19, /device:TPU:24, one launch (start us, length us, event | category | flops | bytes accessed | tf_op | source)
XLA Modules:
  0.0 185.4 jit_solution(15433421187310262825)
XLA Ops:
  0.7 1.4 pad_maximum_fusion.1.x_ref
  2.1 44.1 %shard_map.111 = (f32[16,4096]{1,0:T(8,128)}, f32[16,16384]{1,0:T(8,128)}) custom-call(f32[16,512]{1,0:T(8,128)} %pad_maximum_fusion.1.x_ref), custom_call_target="tpu_custom_call" | custom-call | tf_op jit(solution)/shard_map/pallas_call | solution.py:92
  46.9 6.8 %shard_map.112 = (f32[8,4096]{1,0:T(8,128)}, f32[8,16384]{1,0:T(8,128)}) custom-call(s32[64]{0:T(128)} %bitcast.109, s32[64]{0:T(128)} %bitcast.111, s32[1]{0:T(128)} %bitcast.88.count_ref, f32[64,128,128]{2,1,0:T(8,128)} %bitcast.90, f32[16,4096]{1,0:T(8,128)} %get-tuple-element.17.rowv_ref, f32[16,16384]{1,0:T(8,128)} %get-tuple-element.18.colv_ref), custom_call_target="tpu_custom_call" | custom-call | tf_op jit(solution)/shard_map/pallas_call | solution.py:415
  53.9 1.3 convolution_add_fusion.2
  55.2 2.3 %convolution_add_fusion.1 = f32[8,8]{0,1:T(8,128)S(1)} fusion(f32[8,8]{0,1:T(8,128)S(1)} %convolution_add_fusion.2, f32[8,16384]{1,0:T(8,128)} %get-tuple-element.20.csum_ref, f32[16,16384]{1,0:T(8,128)S(1)} %copy-done.1), kind=kOutput, calls=%fused_computation.4 | convolution fusion | flops 12582976 | bytes 1052928 | tf_op jit(solution)/shard_map/dot_general | solution.py:427
  57.9 0.7 fusion.25.small_ref
  59.2 47.3 %shard_map.113 = (f32[8,512]{1,0:T(8,128)}, f32[8,128]{1,0:T(8,128)}, f32[8,4096]{1,0:T(8,128)}, f32[8,16384]{1,0:T(8,128)}) custom-call(f32[8,512]{1,0:T(8,128)} %broadcast_multiply_fusion.1.base_ref, f32[8,4096]{1,0:T(8,128)} %get-tuple-element.19.rsum_ref, f32[8,16384]{1,0:T(8,128)} %get-tuple-element.20.csum_ref, f32[8,128]{1,0:T(8,128)} %fusion.25.small_ref), custom_call_target="tpu_custom_call" | custom-call | tf_op jit(solution)/shard_map/pallas_call | solution.py:323
  106.5 0.8 slice.144
  107.3 0.7 cholesky.30
  108.0 0.6 compare_reduce_fusion.1
  108.7 0.6 fusion.22
  109.3 0.6 custom-call.12
  110.3 0.9 broadcast_multiply_fusion
  111.3 0.9 fusion.20
  112.5 2.2 %add_subtract_fusion.colv_ref = f32[8,16384]{1,0:T(8,128)} fusion(f32[8,16384]{1,0:T(8,128)} %get-tuple-element.24, f32[16384]{0:T(1024)S(1)} %bitcast.93, f32[8]{0:T(128)S(1)} %get-tuple-element.48, f32[16384]{0:T(1024)S(1)} %bitcast.94, f32[8]{0:T(128)S(1)} %get-tuple-element.49, f32[16384]{0:T(1024)S(1)} %bitcast.95, f32[8]{0:T(128)S(1)} %get-tuple-element.50, ...), kind=kLoop, calls=%fused_computation.9 | loop fusion | flops 2097152 | bytes 1573120 | tf_op jit(solution)/shard_map/sub | solution.py:466
  114.8 1.8 add_subtract_fusion.1.rowv_ref
  116.5 6.7 %shard_map.114 = (f32[8,4096]{1,0:T(8,128)}, f32[8,16384]{1,0:T(8,128)}) custom-call(s32[64]{0:T(128)} %bitcast.110, s32[64]{0:T(128)} %bitcast.112, s32[1]{0:T(128)} %bitcast.89.count_ref, f32[64,128,128]{2,1,0:T(8,128)} %bitcast.91, f32[8,4096]{1,0:T(8,128)} %add_subtract_fusion.1.rowv_ref, f32[8,16384]{1,0:T(8,128)} %add_subtract_fusion.colv_ref), custom_call_target="tpu_custom_call" | custom-call | tf_op jit(solution)/shard_map/pallas_call | solution.py:415
  123.2 2.3 %fusion.3 = f32[8,8]{0,1:T(8,128)S(1)} fusion(f32[8,16384]{1,0:T(8,128)} %get-tuple-element.26.csum_ref, f32[16,16384]{1,0:T(8,128)S(1)} %copy-done.1), kind=kOutput, calls=%fused_computation.10 | convolution fusion | flops 12582912 | bytes 1048832 | tf_op jit(solution)/shard_map/dot_general | solution.py:427
  125.5 2.3 %fusion.39 = f32[8,8]{0,1:T(8,128)S(1)} fusion(f32[8,16384]{1,0:T(8,128)S(1)} %copy-done.2, f32[8,16384]{1,0:T(8,128)} %get-tuple-element.26.csum_ref), kind=kOutput, calls=%fused_computation.74 | convolution fusion | flops 12582912 | bytes 1048832 | tf_op jit(solution)/shard_map/dot_general | solution.py:427
  127.8 2.3 %fusion.1 = f32[8,8]{0,1:T(8,128)S(1)} fusion(f32[8,16384]{1,0:T(8,128)} %get-tuple-element.26.csum_ref, f32[16,16384]{1,0:T(8,128)S(1)} %copy-done.1), kind=kOutput, calls=%fused_computation.7 | convolution fusion | flops 12582912 | bytes 1048832 | tf_op jit(solution)/shard_map/dot_general | solution.py:427
  130.0 1.3 fusion.8
  131.3 1.3 fusion.38
  132.6 1.3 fusion.6
  134.7 0.7 fusion.17.small_ref
  135.4 40.6 %shard_map.115 = (f32[8,512]{1,0:T(8,128)}, f32[16,128]{1,0:T(8,128)}) custom-call(f32[8,512]{1,0:T(8,128)} %copy-done.9, f32[8,4096]{1,0:T(8,128)} %get-tuple-element.25.rsum_ref, f32[8,16384]{1,0:T(8,128)} %get-tuple-element.26.csum_ref, f32[16,128]{1,0:T(8,128)} %fusion.17.small_ref), custom_call_target="tpu_custom_call" | custom-call | tf_op jit(solution)/shard_map/pallas_call | solution.py:323
  176.0 0.8 fusion.36
  176.9 2.2 %cholesky.64 = f32[24,24]{1,0:T(8,128)S(1)} custom-call(f32[24,24]{1,0:T(8,128)S(1)} %reshape.90), custom_call_target="Cholesky" | custom-call | tf_op jit(solution)/shard_map/cholesky | solution.py:488
  179.1 0.6 compare_reduce_fusion
  179.8 0.6 fusion.11
  180.4 1.8 custom-call.15
  182.6 0.8 fusion.15
  184.1 1.3 copy.29
  (48 shorter events, 3.9 us)
Async XLA Ops:
  0.6 133.5 %copy-start = (f32[8,512]{1,0:T(8,128)S(1)}, f32[8,512]{1,0:T(8,128)}, u32[]{:S(2)}) copy-start(f32[8,512]{1,0:T(8,128)} %param.17) | copy-start | bytes 49156
  0.6 53.1 %copy-start.4 = (f32[8,512]{1,0:T(8,128)S(1)}, f32[8,512]{1,0:T(8,128)}, u32[]{:S(2)}) copy-start(f32[8,512]{1,0:T(8,128)} %param.15) | copy-start | bytes 49156
  0.7 110.6 %copy-start.6 = (f32[8,512]{1,0:T(8,128)S(1)}, f32[8,512]{1,0:T(8,128)}, u32[]{:S(2)}) copy-start(f32[8,512]{1,0:T(8,128)} %param.16) | copy-start | bytes 49156
  0.7 53.1 %copy-start.10 = (f32[512]{0:T(512)S(1)}, f32[512]{0:T(512)}, u32[]{:S(2)}) copy-start(f32[512]{0:T(512)} %param.14) | copy-start | bytes 6148
  46.2 7.7 %copy-start.3 = (f32[16,4096]{1,0:T(8,128)S(1)}, f32[16,4096]{1,0:T(8,128)}, u32[]{:S(2)}) copy-start(f32[16,4096]{1,0:T(8,128)} %get-tuple-element.17.rowv_ref) | copy-start | bytes 786436
  46.2 9.0 %copy-start.1 = (f32[16,16384]{1,0:T(8,128)S(1)}, f32[16,16384]{1,0:T(8,128)}, u32[]{:S(2)}) copy-start(f32[16,16384]{1,0:T(8,128)} %get-tuple-element.18.colv_ref) | copy-start | bytes 3145732
  111.2 22.7 %copy-start.9 = (f32[8,512]{1,0:T(8,128)}, f32[8,512]{1,0:T(8,128)S(1)}, u32[]{:S(2)}) copy-start(f32[8,512]{1,0:T(8,128)S(1)} %get-tuple-element.55.base_ref) | copy-start | bytes 49156
  111.2 23.2 %copy-start.7 = (f32[8,512]{1,0:T(8,128)}, f32[8,512]{1,0:T(8,128)S(1)}, u32[]{:S(2)}) copy-start(f32[8,512]{1,0:T(8,128)S(1)} %get-tuple-element.62) | copy-start | bytes 49156
  114.7 10.8 %copy-start.2 = (f32[8,16384]{1,0:T(8,128)S(1)}, f32[8,16384]{1,0:T(8,128)}, u32[]{:S(2)}) copy-start(f32[8,16384]{1,0:T(8,128)} %add_subtract_fusion.colv_ref) | copy-start | bytes 1572868
  116.5 14.8 %copy-start.5 = (f32[8,4096]{1,0:T(8,128)S(1)}, f32[8,4096]{1,0:T(8,128)}, u32[]{:S(2)}) copy-start(f32[8,4096]{1,0:T(8,128)} %add_subtract_fusion.1.rowv_ref) | copy-start | bytes 393220
  116.5 67.0 %copy-start.8 = (f32[8,512]{1,0:T(8,128)S(1)}, f32[8,512]{1,0:T(8,128)}, u32[]{:S(2)}) copy-start(f32[8,512]{1,0:T(8,128)} %get-tuple-element.61) | copy-start | bytes 49156

commit v20 on v14

--- a/solution.py
+++ b/solution.py
@@ -28,11 +28,19 @@
     pl.semaphore_wait(barrier, n_row + n_col - 2)
 
 
-def _gather_kernel(n_row, n_col, x_ref, rowv_ref, colv_ref, send_row, recv_row, send_col, recv_col, local_sem):
+def _gather_kernel(n_row, n_col, cur_ref, prev_ref, rowv_ref, colv_ref, send_row, recv_row, send_col, recv_col,
+                   local_sem, x_ref, stage_sem):
     vt = x_ref.shape[1]
+    rows = cur_ref.shape[0]
     r = lax.axis_index("row")
     c = lax.axis_index("col")
+    stage_cur = pltpu.make_async_copy(cur_ref, x_ref.at[pl.ds(0, rows)], stage_sem.at[0])
+    stage_prev = pltpu.make_async_copy(prev_ref, x_ref.at[pl.ds(rows, rows)], stage_sem.at[1])
+    stage_cur.start()
+    stage_prev.start()
     _barrier(n_row, n_col, r, c)
+    stage_cur.wait()
+    stage_prev.wait()
 
     def row_copy(j, src):
         return pltpu.make_async_remote_copy(
@@ -86,26 +94,29 @@
     own_col.wait()
 
 
-def gather_tiles(x_tiles, n_row, n_col, collective_id):
-    k, vt = x_tiles.shape
+def gather_tiles(current, previous, n_row, n_col, collective_id):
+    rows, vt = current.shape
+    k = 2 * rows
     vmem = pl.BlockSpec(memory_space=pltpu.VMEM)
     return pl.pallas_call(
         functools.partial(_gather_kernel, n_row, n_col),
         out_shape=(
-            jax.ShapeDtypeStruct((k, n_col * vt), x_tiles.dtype),
-            jax.ShapeDtypeStruct((k, n_row * vt), x_tiles.dtype),
+            jax.ShapeDtypeStruct((k, n_col * vt), current.dtype),
+            jax.ShapeDtypeStruct((k, n_row * vt), current.dtype),
         ),
-        in_specs=[vmem],
+        in_specs=[vmem, vmem],
         out_specs=(vmem, vmem),
         scratch_shapes=[
             pltpu.SemaphoreType.DMA((n_col,)),
             pltpu.SemaphoreType.DMA((n_col,)),
             pltpu.SemaphoreType.DMA((n_row,)),
             pltpu.SemaphoreType.DMA((n_row,)),
+            pltpu.SemaphoreType.DMA((2,)),
+            pltpu.VMEM((k, vt), current.dtype),
             pltpu.SemaphoreType.DMA((2,)),
         ],
         compiler_params=pltpu.CompilerParams(collective_id=collective_id, has_side_effects=True),
-    )(x_tiles)
+    )(current, previous)
 
 
 def _reduce_kernel(n_row, n_col, forward, base_ref, rsum_ref, csum_ref, small_ref, out_ref, small_out, *rest):
@@ -444,7 +455,7 @@
     cols_here = tile_col.reshape(slot_count)
     live_count = counts.reshape(())
 
-    row_cp, col_cp = gather_tiles(jnp.concatenate([current, previous], 0), n_row, n_col, 0)
+    row_cp, col_cp = gather_tiles(current, previous, n_row, n_col, 0)
     row_sum, col_sum = slot_products(blocks, rows_here, cols_here, live_count, row_cp, col_cp, k)
     row_cur, col_cur = row_cp[:k], col_cp[:k]
     scaled = diagonal[None, :] * current

time: 176 us -> 174 us (0.989); the launches traced: 174 us -> 175 us
  Pallas kernels: 144 us -> 146 us
    pallas_call x2, Pallas kernels: 15 us -> 18.1 us  [slot_products(): pl.pallas_call(functools.partial(_slots_kernel, group, rows_k, tile), gri...]
where the time goes in v20:
time: 174 us; the launch traced here: 175 us
  Pallas kernels  146 us (84%)
  other arithmetic  12 us (7%)
  matrix products  10.1 us (6%)
  local copies, waits for them, and re-layouts  4.87 us (3%)
    pallas_call x2, Pallas kernels, reduce_tiles(): pl.pallas_call(functools.partial(_reduce_kernel, n_row, n_col, forward),...  83.5 us
    pallas_call x1, Pallas kernels, gather_tiles(): pl.pallas_call(functools.partial(_gather_kernel, n_row, n_col), out_shape...  44.5 us
    pallas_call x2, Pallas kernels, slot_products(): pl.pallas_call(functools.partial(_slots_kernel, group, rows_k, tile), gri...  18.1 us
    dot_general x4, matrix products, tile_dot(): return jnp.dot(left, right.T, precision=highest)  7.66 us
    another operation x4, other arithmetic, lower_solve(): lax.linalg.triangular_solve(factor, rhs, left_side=True, lower=True, tran...  3.76 us

profile of v20, /device:TPU:24, one launch (start us, length us, event | category | flops | bytes accessed | tf_op | source)
XLA Modules:
  0.0 174.7 jit_solution(15729149072265851139)
XLA Ops:
  0.6 44.5 %shard_map.111 = (f32[16,4096]{1,0:T(8,128)}, f32[16,16384]{1,0:T(8,128)}) custom-call(f32[8,512]{1,0:T(8,128)} %cur_ref.1, f32[8,512]{1,0:T(8,128)} %prev_ref.1), custom_call_target="tpu_custom_call" | custom-call | tf_op jit(solution)/shard_map/pallas_call | solution.py:101
  45.9 9.2 %shard_map.112 = (f32[8,4096]{1,0:T(8,128)}, f32[8,16384]{1,0:T(8,128)}) custom-call(s32[64]{0:T(128)} %bitcast.103, s32[64]{0:T(128)} %bitcast.105, s32[1]{0:T(128)} %bitcast.82.count_ref, f32[64,128,128]{2,1,0:T(8,128)} %bitcast.84, f32[16,4096]{1,0:T(8,128)} %get-tuple-element.17.rowv_ref, f32[16,16384]{1,0:T(8,128)} %get-tuple-element.18.colv_ref), custom_call_target="tpu_custom_call" | custom-call | tf_op jit(solution)/shard_map/pallas_call | solution.py:426
  55.2 1.3 convolution_add_fusion.2
  56.6 2.3 %convolution_add_fusion.1 = f32[8,8]{0,1:T(8,128)S(1)} fusion(f32[8,8]{0,1:T(8,128)S(1)} %convolution_add_fusion.2, f32[8,16384]{1,0:T(8,128)} %get-tuple-element.20.csum_ref, f32[16,16384]{1,0:T(8,128)S(1)} %copy-done.1), kind=kOutput, calls=%fused_computation.10 | convolution fusion | flops 12582976 | bytes 1052928 | tf_op jit(solution)/shard_map/dot_general | solution.py:438
  59.3 0.7 fusion.27.small_ref
  60.0 0.6 broadcast_multiply_fusion.1.base_ref
  60.6 44.8 %shard_map.113 = (f32[8,512]{1,0:T(8,128)}, f32[8,128]{1,0:T(8,128)}, f32[8,4096]{1,0:T(8,128)}, f32[8,16384]{1,0:T(8,128)}) custom-call(f32[8,512]{1,0:T(8,128)} %broadcast_multiply_fusion.1.base_ref, f32[8,4096]{1,0:T(8,128)} %get-tuple-element.19.rsum_ref, f32[8,16384]{1,0:T(8,128)} %get-tuple-element.20.csum_ref, f32[8,128]{1,0:T(8,128)} %fusion.27.small_ref), custom_call_target="tpu_custom_call" | custom-call | tf_op jit(solution)/shard_map/pallas_call | solution.py:334
  105.4 0.8 slice.144
  106.2 0.7 cholesky.30
  107.0 0.6 compare_reduce_fusion.1
  107.6 0.6 fusion.24
  108.3 0.6 custom-call.12
  108.9 0.2 fusion.25
  109.3 0.4 fusion.41
  109.6 1.2 fusion.40
  110.9 0.8 fusion.42
  111.7 8.9 %shard_map.114 = (f32[8,4096]{1,0:T(8,128)}, f32[8,16384]{1,0:T(8,128)}) custom-call(s32[64]{0:T(128)} %bitcast.104, s32[64]{0:T(128)} %bitcast.106, s32[1]{0:T(128)} %bitcast.83.count_ref, f32[64,128,128]{2,1,0:T(8,128)} %bitcast.85, f32[8,4096]{1,0:T(8,128)} %get-tuple-element.62.rowv_ref, f32[8,16384]{1,0:T(8,128)} %get-tuple-element.61.colv_ref), custom_call_target="tpu_custom_call" | custom-call | tf_op jit(solution)/shard_map/pallas_call | solution.py:426
  120.7 1.4 fusion.7
  122.1 2.6 %fusion = f32[24,8]{0,1:T(8,128)S(1)} fusion(f32[8,16384]{1,0:T(8,128)} %get-tuple-element.26.csum_ref, f32[8,16384]{1,0:T(8,128)S(1)} %get-tuple-element.30, f32[8,16384]{1,0:T(8,128)S(1)} %copy-done.2, f32[8,16384]{1,0:T(8,128)S(1)} %get-tuple-element.29), kind=kOutput, calls=%fused_computation | convolution fusion | flops 38535168 | bytes 2097920 | tf_op jit(solution)/shard_map/dot_general | solution.py:438
  124.7 0.2 broadcast_multiply_fusion
  125.6 0.2 fusion.23
  125.9 0.7 fusion.19.small_ref
  126.6 38.7 %shard_map.115 = (f32[8,512]{1,0:T(8,128)}, f32[16,128]{1,0:T(8,128)}) custom-call(f32[8,512]{1,0:T(8,128)} %copy-done.9, f32[8,4096]{1,0:T(8,128)} %get-tuple-element.25.rsum_ref, f32[8,16384]{1,0:T(8,128)} %get-tuple-element.26.csum_ref, f32[16,128]{1,0:T(8,128)} %fusion.19.small_ref), custom_call_target="tpu_custom_call" | custom-call | tf_op jit(solution)/shard_map/pallas_call | solution.py:334
  165.3 0.8 fusion.44
  166.2 2.2 %cholesky.64 = f32[24,24]{1,0:T(8,128)S(1)} custom-call(f32[24,24]{1,0:T(8,128)S(1)} %reshape.90), custom_call_target="Cholesky" | custom-call | tf_op jit(solution)/shard_map/cholesky | solution.py:499
  168.4 0.6 compare_reduce_fusion
  169.1 0.6 fusion.13
  169.7 1.8 %custom-call.15 = f32[1,24,24]{1,2,0:T(8,128)S(1)} custom-call(f32[1,24,24]{2,1,0:T(8,128)S(1)} %fusion.13), custom_call_target="InvertDiagBlocksLowerTriangular" | custom-call | tf_op jit(solution)/shard_map/triangular_solve/custom-call.4 | solution.py:442
  171.7 0.2 convolution_bitcast_fusion
  171.9 0.8 fusion.17
  172.8 0.6 copy.28
  173.4 1.3 copy.29
  (47 shorter events, 1.9 us)
Async XLA Ops:
  0.6 124.6 %copy-start = (f32[8,512]{1,0:T(8,128)S(1)}, f32[8,512]{1,0:T(8,128)}, u32[]{:S(2)}) copy-start(f32[8,512]{1,0:T(8,128)} %param.17) | copy-start | bytes 49156
  45.8 9.3 %copy-start.4 = (f32[8,512]{1,0:T(8,128)S(1)}, f32[8,512]{1,0:T(8,128)}, u32[]{:S(2)}) copy-start(f32[8,512]{1,0:T(8,128)} %cur_ref.1) | copy-start | bytes 49156
  45.9 9.2 %copy-start.12 = (f32[512]{0:T(512)S(1)}, f32[512]{0:T(512)}, u32[]{:S(2)}) copy-start(f32[512]{0:T(512)} %param.14) | copy-start | bytes 6148
  45.9 9.4 %copy-start.3 = (f32[16,4096]{1,0:T(8,128)S(1)}, f32[16,4096]{1,0:T(8,128)}, u32[]{:S(2)}) copy-start(f32[16,4096]{1,0:T(8,128)} %get-tuple-element.17.rowv_ref) | copy-start | bytes 786436
  45.9 10.7 %copy-start.1 = (f32[16,16384]{1,0:T(8,128)S(1)}, f32[16,16384]{1,0:T(8,128)}, u32[]{:S(2)}) copy-start(f32[16,16384]{1,0:T(8,128)} %get-tuple-element.18.colv_ref) | copy-start | bytes 3145732
  105.4 4.2 %copy-start.6 = (f32[8,16384]{1,0:T(8,128)S(1)}, f32[8,16384]{1,0:T(8,128)}, u32[]{:S(2)}) copy-start(f32[8,16384]{1,0:T(8,128)} %get-tuple-element.24) | copy-start | bytes 1572868
  109.6 1.3 copy-start.11
  111.7 8.9 %copy-start.5 = (f32[8,4096]{1,0:T(8,128)S(1)}, f32[8,4096]{1,0:T(8,128)}, u32[]{:S(2)}) copy-start(f32[8,4096]{1,0:T(8,128)} %get-tuple-element.62.rowv_ref) | copy-start | bytes 393220
  111.7 10.3 %copy-start.2 = (f32[8,16384]{1,0:T(8,128)S(1)}, f32[8,16384]{1,0:T(8,128)}, u32[]{:S(2)}) copy-start(f32[8,16384]{1,0:T(8,128)} %get-tuple-element.61.colv_ref) | copy-start | bytes 1572868
  120.7 4.0 %copy-start.10 = (f32[8,512]{1,0:T(8,128)S(1)}, f32[8,512]{1,0:T(8,128)}, u32[]{:S(2)}) copy-start(f32[8,512]{1,0:T(8,128)} %get-tuple-element.67) | copy-start | bytes 49156
  120.7 4.3 %copy-start.7 = (f32[8,512]{1,0:T(8,128)S(1)}, f32[8,512]{1,0:T(8,128)}, u32[]{:S(2)}) copy-start(f32[8,512]{1,0:T(8,128)} %prev_ref.1) | copy-start | bytes 49156
  124.9 1.7 copy-start.9
  124.9 49.8 %copy-start.8 = (f32[8,512]{1,0:T(8,128)}, f32[8,512]{1,0:T(8,128)S(1)}, u32[]{:S(2)}) copy-start(f32[8,512]{1,0:T(8,128)S(1)} %get-tuple-element.68) | copy-start | bytes 49156
